TPU v7x, 128 devices: a whole 4x4x4 slice. The times are simulated.
128 devices in a mesh: section: 2 (over y_hi), expert: 8 (over z, core), hid: 8 (over x, y_lo).
Axes of the slice: x: 4, y: 4 (y_hi: 2, y_lo: 2; y = y_hi * 2 + y_lo), z: 4, core: 2. Of those that a mesh axis runs over, the one named last changes fastest.
Arguments:
- saved_input: bfloat16 [2, 1024, 4096], P('section', 'expert', 'hid'), may hold values from -6 to 6
- cotangent: bfloat16 [2, 1024, 4096], P('section', 'expert', 'hid'), may hold values from -6 to 6
- next_input: bfloat16 [2, 1024, 4096], P('section', 'expert', 'hid'), may hold values from -6 to 6
- routes_saved: int32 [2, 1024, 2], P('section', 'expert'), may hold values from 0 to 7, all different within a row; in each aligned block of 128 rows (0 to 127, 128 to 255, ..., all dimensions but the last counted through in order) at most 48 rows name the same one
- routes_next: int32 [2, 1024, 2], P('section', 'expert'), may hold values from 0 to 7, all different within a row; in each aligned block of 128 rows (0 to 127, 128 to 255, ..., all dimensions but the last counted through in order) at most 48 rows name the same one
- norm_gain: float32 [2, 4096], P('section', 'hid'), may hold values from 0.1 to 1.9
- router: float32 [2, 4096, 8], P('section', 'hid'), may hold values from -0.18 to 0.18
- expert_gate: bfloat16 [2, 8, 4096, 7168], P('section', 'expert', None, 'hid'), may hold values from -0.09375 to 0.09375
- expert_up: bfloat16 [2, 8, 4096, 7168], P('section', 'expert', None, 'hid'), may hold values from -0.09375 to 0.09375
- expert_down: bfloat16 [2, 8, 7168, 4096], P('section', 'expert', 'hid'), may hold values from -0.0625 to 0.0625
Outputs:
- leaving: bfloat16 [2, 1024, 4096], P('section', 'expert', 'hid')
- arriving: bfloat16 [2, 1024, 4096], P('section', 'expert', 'hid')
Inputs may be any that keep to these rules, and one draw needn't show every extreme that they name: `routes_saved`: A token's two ids differ. In each aligned block of 128 tokens of a section no expert is named by more than 48 tokens, and some block names some expert exactly 48 times. `routes_next`: A token's two ids differ. In each aligned block of 128 tokens of a section no expert is named by more than 48 tokens, and some block names some expert exactly 48 times.
All inputs are finite; a program needn't handle non-finite values.
Results may differ from a plain program's by a relative error of at most 0.0052.
Values may be sent and summed in bfloat16 or wider, within the bound.
No kernel may reach another device: no remote copies, remote signals or barrier semaphores. Data moves between devices by JAX's collectives and lax.ppermute only.
A program may use at most 128 MiB of HBM per device.

v0:
```python
import functools

import jax
import jax.numpy as jnp
from jax import lax
from jax.experimental import pallas as pl
from jax.experimental.pallas import tpu as pltpu
from jax.sharding import PartitionSpec as P

EPSILON = 1e-05
INNER = (((1,), (0,)), ((), ()))
CONTRACT = (((1,), (1,)), ((), ()))
LEADING = (((0,), (0,)), ((), ()))
BOTH = ("expert", "hid")
STEP = 48
GROUPS = 8
TABLE = 32
LIMIT = 56 * 1024 * 1024
VMEM = pl.BlockSpec(memory_space=pltpu.VMEM)
SMEM = pl.BlockSpec(memory_space=pltpu.SMEM)
PLACE = pl.BlockSpec(memory_space=pl.ANY)


def product(left, right, dims):
    return lax.dot_general(left, right, dims, preferred_element_type=jnp.float32)


def partner(block, axis, bit):
    count = lax.axis_size(axis)
    route = []
    for low in range(count):
        high = low | 1 << bit
        if high != low and high < count:
            route += [(low, high), (high, low)]
    return lax.ppermute(block, axis, route)


def swap(block, axes):
    return lax.all_to_all(block, axes, split_axis=0, concat_axis=0, tiled=True)


def shift(block, along, across):
    count = lax.axis_size("hid")
    route = []
    for source in range(count):
        x, y = source // 2, source % 2
        route.append((source, (x + along) % (count // 2) * 2 + (y ^ across)))
    return lax.ppermute(block, "hid", route)


def gather_groups(block):
    other = shift(block, 0, 1)
    right, left = shift(block, 1, 0), shift(block, -1, 0)
    right_other, left_other = shift(other, 1, 0), shift(other, -1, 0)
    far, far_other = shift(right, 1, 0), shift(left_other, -1, 0)
    return [block, other, right, right_other, left, left_other, far, far_other]


def arrival_order():
    own = lax.axis_index("hid")
    half = lax.axis_size("hid") // 2
    x, y = own // 2, own % 2
    places = []
    for along in (0, -1, 1, 2):
        row = (x + along + half) % half * 2
        places += [row + y, row + 1 - y]
    return jnp.stack(places).astype(jnp.int32)


def three_parts(value):
    high = value.astype(jnp.bfloat16)
    rest = value - high.astype(jnp.float32)
    middle = rest.astype(jnp.bfloat16)
    low = (rest - middle.astype(jnp.float32)).astype(jnp.bfloat16)
    return high, middle, low


def pack_kernel(
    capacity, routes_s, routes_n, saved, cot, upcoming, gain, router, packed, tokens_out, sel_s, sel_n
):
    tokens, part = saved.shape
    experts = router.shape[0]
    tokens_out[0:tokens, :] = upcoming[...]
    gains = gain[...]
    scaled = router[...] * gains
    rows = [p.astype(jnp.float32) for p in three_parts(scaled)]
    rows += [p.astype(jnp.float32) for p in three_parts(gains)]
    rows.append(jnp.zeros((TABLE - 3 * experts - 3, part), jnp.float32))
    tokens_out[tokens : tokens + TABLE, :] = jnp.concatenate(rows, axis=0).astype(jnp.bfloat16)

    row = lax.broadcasted_iota(jnp.int32, (tokens, tokens), 0)
    lane = lax.broadcasted_iota(jnp.int32, (tokens, tokens), 1)
    earlier = jnp.where(lane < row, 1.0, 0.0).astype(jnp.bfloat16)
    wide = lax.broadcasted_iota(jnp.int32, (tokens, 128), 1)
    slots = lax.broadcasted_iota(jnp.int32, (tokens, experts * capacity), 1)

    def select(routes):
        ids = routes[...]
        one, two = ids[:, 0:1], ids[:, 1:2]
        hit_one = jnp.where(wide == one, 1.0, 0.0)
        hit_two = jnp.where(wide == two, 1.0, 0.0)
        counts = product(earlier, (hit_one + hit_two).astype(jnp.bfloat16), INNER)
        rank_one = jnp.sum(counts * hit_one, axis=1, keepdims=True).astype(jnp.int32)
        rank_two = jnp.sum(counts * hit_two, axis=1, keepdims=True).astype(jnp.int32)
        first = jnp.where(slots == one * capacity + rank_one, 1.0, 0.0)
        second = jnp.where(slots == two * capacity + rank_two, 1.0, 0.0)
        inside = wide < 3 * experts
        wide_one = jnp.where(inside & (lax.rem(wide, experts) == one), 1.0, 0.0).astype(jnp.bfloat16)
        wide_two = jnp.where(inside & (lax.rem(wide, experts) == two), 1.0, 0.0).astype(jnp.bfloat16)
        other = product(first.astype(jnp.bfloat16), wide_two, LEADING)
        other = other + product(second.astype(jnp.bfloat16), wide_one, LEADING)
        return (first + second).astype(jnp.bfloat16), other.astype(jnp.bfloat16)

    def put(start, lanes, width, value):
        packed[:, start : start + capacity, lanes : lanes + width] = value.reshape(
            experts, capacity, width
        )

    both, other = select(routes_s)
    sel_s[...] = both
    put(0, 0, part, product(both, saved[...], LEADING).astype(jnp.bfloat16))
    put(capacity, 0, part, product(both, cot[...], LEADING).astype(jnp.bfloat16))
    put(0, part, 128, other)
    both, other = select(routes_n)
    sel_n[...] = both
    put(capacity, part, 128, other)


def pack(routes_s, routes_n, saved, cot, upcoming, gain, router, capacity):
    tokens, part = saved.shape
    experts = router.shape[0]
    total = experts * capacity
    shapes = [
        (experts, 2 * capacity, part + 128),
        (tokens + TABLE, part),
        (tokens, total),
        (tokens, total),
    ]
    return pl.pallas_call(
        functools.partial(pack_kernel, capacity),
        out_shape=[jax.ShapeDtypeStruct(s, jnp.bfloat16) for s in shapes],
        in_specs=[VMEM] * 7,
        out_specs=[VMEM] * 4,
        compiler_params=pltpu.CompilerParams(vmem_limit_bytes=LIMIT // 2),
    )(routes_s, routes_n, saved, cot, upcoming, gain, router)


def spread_kernel(sel, *refs):
    pieces, (moved, table) = refs[:GROUPS], refs[GROUPS:]
    tokens = sel.shape[0]
    blocks, _, capacity, part = moved.shape
    for group, piece in enumerate(pieces):
        rows = product(sel[...], piece[0:tokens, :], LEADING).astype(jnp.bfloat16)
        moved[:, group] = rows.reshape(blocks, capacity, part)
        table[group] = piece[tokens : tokens + TABLE, :]


def spread(sel, pieces, blocks):
    part = pieces[0].shape[1]
    capacity = sel.shape[1] // blocks
    return pl.pallas_call(
        spread_kernel,
        out_shape=(
            jax.ShapeDtypeStruct((blocks, GROUPS, capacity, part), jnp.bfloat16),
            jax.ShapeDtypeStruct((GROUPS, TABLE, part), jnp.bfloat16),
        ),
        in_specs=[VMEM] * (1 + GROUPS),
        out_specs=(VMEM, VMEM),
        compiler_params=pltpu.CompilerParams(vmem_limit_bytes=LIMIT // 2),
    )(sel, *pieces)


def widen(value, width):
    return jnp.concatenate([value] * (width // 128), axis=1)


def lanes(value):
    total = value[:, 0:128]
    for start in range(128, value.shape[1], 128):
        total = total + value[:, start : start + 128]
    return total


def even(value):
    return jnp.broadcast_to(jnp.sum(value, axis=1, keepdims=True), (value.shape[0], 128))


def gains_of(table, group):
    rows = table[group, 24:32, :].astype(jnp.float32)
    return rows[0:1] + (rows[1:2] + rows[2:3])


def fetch_rows(order, source, target, sems, part):
    copies = []
    for group in range(GROUPS):
        start = pl.multiple_of(order[group] * part, part)
        copies.append(
            pltpu.make_async_copy(
                source.at[pl.ds(start, part), :],
                target.at[pl.ds(group * part, part), :],
                sems.at[group],
            )
        )
    return copies


def fetch_columns(order, source, target, sems, part):
    copies = []
    for group in range(GROUPS):
        start = group * part
        if order is not None:
            start = pl.multiple_of(order[group] * part, part)
        copies.append(
            pltpu.make_async_copy(
                source.at[:, pl.ds(start, part)],
                target.at[:, pl.ds(group * part, part)],
                sems.at[group],
            )
        )
    return copies


def prepare(own, other_start, take, other, table, normed, scales, diffs, logits, width):
    blocks = other.shape[0]
    part = width // GROUPS
    for group in range(GROUPS):
        rows = jnp.concatenate([take(group, block) for block in range(blocks)], axis=0)
        found = product(rows, table[group], CONTRACT)
        if group == 0:
            logits[...] = found
        else:
            logits[...] += found

    @pl.loop(0, blocks)
    def _(block):
        at = pl.ds(pl.multiple_of(block * STEP, STEP), STEP)
        total = jnp.zeros((STEP, 128), jnp.float32)
        for group in range(GROUPS):
            values = take(group, block).astype(jnp.float32)
            total = total + lanes(values * values)
        scale = lax.rsqrt(even(total) / width + EPSILON)
        scales[at, :] = scale
        place = lax.broadcasted_iota(jnp.int32, (STEP, TABLE), 1)
        ours = jnp.where((place < 24) & (lax.rem(place, 8) == own), 1.0, 0.0)
        theirs = other[block, other_start : other_start + STEP, 0:TABLE].astype(jnp.float32)
        diffs[at, :] = even(logits[at, :] * (ours - theirs)) * scale
        for group in range(GROUPS):
            values = take(group, block).astype(jnp.float32)
            normed[at, group * part : (group + 1) * part] = (
                values * widen(scale, part) * gains_of(table, group)
            ).astype(jnp.bfloat16)


def forward_kernel(
    order, own, moved, other, table, gate_w, up_w, down_w, out,
    gate_b, up_b, down_b, normed, gate, up, hidden, scales, diffs, logits, sem_g, sem_u, sem_d
):
    blocks, _, capacity, part = moved.shape
    copies = fetch_rows(order, gate_w, gate_b, sem_g, part)
    copies_up = fetch_rows(order, up_w, up_b, sem_u, part)
    copies_down = fetch_columns(None, down_w, down_b, sem_d, part)
    for copy in copies + copies_up + copies_down:
        copy.start()

    def take(group, block):
        return moved[block, group]

    prepare(own[0], capacity, take, other, table, normed, scales, diffs, logits, GROUPS * part)
    for copy in copies:
        copy.wait()
    gate[...] = product(normed[...], gate_b[...], INNER)
    for copy in copies_up:
        copy.wait()
    up[...] = product(normed[...], up_b[...], INNER)

    @pl.loop(0, blocks)
    def _(block):
        at = pl.ds(pl.multiple_of(block * STEP, STEP), STEP)
        value = gate[at, :]
        hidden[at, :] = (value * jax.nn.sigmoid(value) * up[at, :]).astype(jnp.bfloat16)

    share = widen(jax.nn.sigmoid(diffs[...]), part)
    for group in range(GROUPS):
        copies_down[group].wait()
        rows = product(hidden[...], down_b[:, group * part : (group + 1) * part], INNER)
        out[:, group] = (rows * share).astype(jnp.bfloat16).reshape(blocks, capacity, part)


def weight_scratch(width, units):
    return [
        pltpu.VMEM((width, units), jnp.bfloat16),
        pltpu.VMEM((width, units), jnp.bfloat16),
        pltpu.VMEM((units, width), jnp.bfloat16),
    ]


def forward(order, own, moved, other, table, gate_w, up_w, down_w):
    blocks, _, capacity, part = moved.shape
    width, units = gate_w.shape
    total = blocks * capacity
    return pl.pallas_call(
        forward_kernel,
        out_shape=jax.ShapeDtypeStruct(moved.shape, jnp.bfloat16),
        in_specs=[SMEM, SMEM, VMEM, VMEM, VMEM, PLACE, PLACE, PLACE],
        out_specs=VMEM,
        scratch_shapes=weight_scratch(width, units)
        + [
            pltpu.VMEM((total, width), jnp.bfloat16),
            pltpu.VMEM((total, units), jnp.float32),
            pltpu.VMEM((total, units), jnp.float32),
            pltpu.VMEM((total, units), jnp.bfloat16),
            pltpu.VMEM((total, 128), jnp.float32),
            pltpu.VMEM((total, 128), jnp.float32),
            pltpu.VMEM((total, TABLE), jnp.float32),
        ]
        + [pltpu.SemaphoreType.DMA((GROUPS,))] * 3,
        compiler_params=pltpu.CompilerParams(vmem_limit_bytes=LIMIT),
        cost_estimate=pl.CostEstimate(
            flops=6 * total * width * units,
            bytes_accessed=6 * width * units + 4 * total * width,
            transcendentals=total * units,
        ),
    )(order, own, moved, other, table, gate_w, up_w, down_w)


def backward_kernel(*refs):
    order, own, other, table, gate_w, up_w, down_w = refs[:7]
    pieces = refs[7 : 7 + GROUPS]
    (
        out, gate_b, up_b, down_b, normed, cots, gate, up, grad, grad_gate, grad_up,
        scales, diffs, ones, twos, logits, sem_g, sem_u, sem_d,
    ) = refs[7 + GROUPS :]
    blocks, _, capacity, part = out.shape
    width = GROUPS * part
    copies = fetch_rows(order, gate_w, gate_b, sem_g, part)
    copies_up = fetch_rows(order, up_w, up_b, sem_u, part)
    copies_down = fetch_columns(order, down_w, down_b, sem_d, part)
    for copy in copies + copies_up + copies_down:
        copy.start()

    def take(group, block):
        return pieces[group][block, 0:STEP, :]

    prepare(own[0], 0, take, other, table, normed, scales, diffs, logits, width)

    @pl.loop(0, blocks)
    def _(block):
        at = pl.ds(pl.multiple_of(block * STEP, STEP), STEP)
        for group in range(GROUPS):
            cots[at, group * part : (group + 1) * part] = pieces[group][block, STEP : 2 * STEP, :]

    for copy in copies:
        copy.wait()
    gate[...] = product(normed[...], gate_b[...], INNER)
    for copy in copies_up:
        copy.wait()
    up[...] = product(normed[...], up_b[...], INNER)
    for copy in copies_down:
        copy.wait()
    grad[...] = product(cots[...], down_b[...], CONTRACT)

    @pl.loop(0, blocks)
    def _(block):
        at = pl.ds(pl.multiple_of(block * STEP, STEP), STEP)
        slope, value, lift = grad[at, :], gate[at, :], up[at, :]
        sig = jax.nn.sigmoid(value)
        silu = value * sig
        hidden = (silu * lift).astype(jnp.bfloat16).astype(jnp.float32)
        to_gate = (slope * lift * (sig * (1.0 + value * (1.0 - sig)))).astype(jnp.bfloat16)
        to_up = (slope * silu).astype(jnp.bfloat16)
        grad_gate[at, :] = to_gate
        grad_up[at, :] = to_up
        row_dot = even(lanes(slope * hidden))
        norm_dot = even(
            lanes(to_gate.astype(jnp.float32) * value + to_up.astype(jnp.float32) * lift)
        )
        scale, diff = scales[at, :], diffs[at, :]
        ours, theirs = jax.nn.sigmoid(diff), jax.nn.sigmoid(-diff)
        through = ours * theirs * row_dot
        ones[at, :] = scale * through
        twos[at, :] = scale * scale * ((ours * norm_dot + through * diff) / width)
        diffs[at, :] = scale * ours

    place = lax.broadcasted_iota(jnp.int32, (blocks * STEP, TABLE), 1)
    away = jnp.where((place < 24) & (lax.rem(place, 8) == own[0]), 1.0, 0.0)
    away = away - jnp.concatenate(
        [other[block, 0:STEP, 0:TABLE].astype(jnp.float32) for block in range(blocks)], axis=0
    )
    away = away.astype(jnp.bfloat16)
    for group in range(GROUPS):
        at = slice(group * part, (group + 1) * part)
        rows = product(grad_gate[...], gate_b[at, :], CONTRACT)
        rows = rows + product(grad_up[...], up_b[at, :], CONTRACT)
        turn = product(away, table[group], INNER)
        values = jnp.concatenate([take(group, block) for block in range(blocks)], axis=0)
        rows = (
            rows * (widen(diffs[...], part) * gains_of(table, group))
            + turn * widen(ones[...], part)
            - values.astype(jnp.float32) * widen(twos[...], part)
        )
        out[:, pl.ds(order[group], 1)] = rows.astype(jnp.bfloat16).reshape(blocks, 1, capacity, part)


def backward(order, own, other, table, gate_w, up_w, down_w, pieces):
    blocks, double, part = pieces[0].shape
    capacity = double // 2
    width, units = gate_w.shape
    total = blocks * capacity
    small = pltpu.VMEM((total, 128), jnp.float32)
    return pl.pallas_call(
        backward_kernel,
        out_shape=jax.ShapeDtypeStruct((blocks, GROUPS, capacity, part), jnp.bfloat16),
        in_specs=[SMEM, SMEM, VMEM, VMEM, PLACE, PLACE, PLACE] + [VMEM] * GROUPS,
        out_specs=VMEM,
        scratch_shapes=weight_scratch(width, units)
        + [
            pltpu.VMEM((total, width), jnp.bfloat16),
            pltpu.VMEM((total, width), jnp.bfloat16),
            pltpu.VMEM((total, units), jnp.float32),
            pltpu.VMEM((total, units), jnp.float32),
            pltpu.VMEM((total, units), jnp.float32),
            pltpu.VMEM((total, units), jnp.bfloat16),
            pltpu.VMEM((total, units), jnp.bfloat16),
            small,
            small,
            small,
            small,
            pltpu.VMEM((total, TABLE), jnp.float32),
        ]
        + [pltpu.SemaphoreType.DMA((GROUPS,))] * 3,
        compiler_params=pltpu.CompilerParams(vmem_limit_bytes=LIMIT),
        cost_estimate=pl.CostEstimate(
            flops=10 * total * width * units,
            bytes_accessed=6 * width * units + 6 * total * width,
            transcendentals=total * units,
        ),
    )(order, own, other, table, gate_w, up_w, down_w, *pieces)


def finish_kernel(sel, home, base, out):
    blocks, groups, capacity, part = home.shape
    total = base[...].astype(jnp.float32)
    for group in range(groups):
        total = total + product(sel[...], home[:, group].reshape(blocks * capacity, part), INNER)
    out[...] = total.astype(jnp.bfloat16)


def finish(sel, home, base):
    return pl.pallas_call(
        finish_kernel,
        out_shape=jax.ShapeDtypeStruct(base.shape, jnp.bfloat16),
        in_specs=[VMEM] * 3,
        out_specs=VMEM,
        compiler_params=pltpu.CompilerParams(vmem_limit_bytes=LIMIT // 2),
    )(sel, home, base)


def send_home(pieces):
    experts, hids, capacity, part = pieces.shape
    home = swap(pieces.reshape(experts * hids, capacity, part), BOTH)
    return home.reshape(experts, hids, capacity, part)


def per_device(
    saved_input,
    cotangent,
    next_input,
    routes_saved,
    routes_next,
    norm_gain,
    router,
    expert_gate,
    expert_up,
    expert_down,
):
    gate_w, up_w, down_w = expert_gate[0, 0], expert_up[0, 0], expert_down[0, 0]
    tokens, part = saved_input.shape[1:]
    experts = lax.axis_size("expert")
    capacity = 3 * tokens // experts
    own = lax.axis_index("expert").astype(jnp.int32).reshape(1)
    order = arrival_order()

    packed, tokens_next, sel_saved, sel_next = pack(
        routes_saved[0],
        routes_next[0],
        saved_input[0],
        cotangent[0],
        next_input[0],
        norm_gain,
        router[0].T,
        capacity,
    )
    packed = swap(packed, "expert")
    moved_next, table = spread(sel_next, gather_groups(tokens_next), experts)
    moved_next = swap(moved_next, "expert")
    other = packed[:, :, part:]
    pieces = gather_groups(packed[:, :, :part])

    out_next = forward(order, own, moved_next, other, table, gate_w, up_w, down_w)
    out_home = send_home(out_next)
    pieces, out_next = lax.optimization_barrier((pieces, out_next))
    back_part = backward(order, own, other, table, gate_w, up_w, down_w, pieces)
    back_home = send_home(back_part)

    forward_out = finish(sel_next, out_home, next_input[0])
    grad_input = finish(sel_saved, back_home, cotangent[0])

    first_section = lax.axis_index("section") == 0
    outgoing = jnp.where(first_section, forward_out, grad_input)
    leaving = jnp.where(first_section, grad_input, forward_out)
    arriving = partner(outgoing, "section", 0)
    return (leaving[None], arriving[None])


def solution(mesh):
    placed = (
        P("section", "expert", "hid"),
        P("section", "expert", "hid"),
        P("section", "expert", "hid"),
        P("section", "expert", None),
        P("section", "expert", None),
        P("section", "hid"),
        P("section", "hid", None),
        P("section", "expert", None, "hid"),
        P("section", "expert", None, "hid"),
        P("section", "expert", "hid", None),
    )
    return jax.shard_map(
        per_device,
        mesh=mesh,
        in_specs=placed,
        out_specs=(P("section", "expert", "hid"), P("section", "expert", "hid")),
        check_vma=False,
    )
```

profile of v0, /device:TPU:1, one launch (start us, length us, event | category | flops | bytes accessed | tf_op | source)
XLA Modules:
  0.0 293.2 jit_solution(28365192917792291)
XLA Ops:
  6.3 2.2 shard_map.113
  9.2 6.8 %all-to-all-start = ((bf16[8,96,640]{2,1,0:T(8,128)(2,1)}), bf16[8,96,640]{2,1,0:T(8,128)(2,1)S(1)}, u32[]{:S(2)}, u32[]{:S(2)}) async-start(bf16[8,96,640]{2,1,0:T(8,128)(2,1)} %get-tuple-element.17), calls=%async_computation | async-start | bytes 1966080 | tf_op jit(solution)/shard_map/all_to_all | solution.py:39
  18.5 3.3 %collective-permute-done.refs_1_ = bf16[160,512]{1,0:T(8,128)(2,1)S(1)} collective-permute-done((bf16[160,512]{1,0:T(8,128)(2,1)S(1)}, bf16[160,512]{1,0:T(8,128)(2,1)S(1)}, u32[]{:S(2)}, u32[]{:S(2)}) %collective-permute-start) | collective-permute-done | bytes 163872 | tf_op jit(solution)/shard_map/ppermute | solution.py:48
  21.8 2.5 collective-permute-start.4
  27.1 3.4 %collective-permute-start.6 = (bf16[160,512]{1,0:T(8,128)(2,1)S(1)}, bf16[160,512]{1,0:T(8,128)(2,1)S(1)}, u32[]{:S(2)}, u32[]{:S(2)}) collective-permute-start(bf16[160,512]{1,0:T(8,128)(2,1)S(1)} %collective-permute-done.4.refs_5_), channel_id=1, source_target_pairs={{0,6},{1,7},{2,0},{3,1},{4,2},{5,3},{6,4},{7,5},{8,14},{9,15},{10,... | collective-permute-start | bytes 491528 | tf_op jit(solution)/shard_map/ppermute | solution.py:48
  30.6 3.4 %collective-permute-done.5.refs_6_ = bf16[160,512]{1,0:T(8,128)(2,1)S(1)} collective-permute-done((bf16[160,512]{1,0:T(8,128)(2,1)S(1)}, bf16[160,512]{1,0:T(8,128)(2,1)S(1)}, u32[]{:S(2)}, u32[]{:S(2)}) %collective-permute-start.5) | collective-permute-done | bytes 163872 | tf_op jit(solution)/shard_map/ppermute | solution.py:48
  33.9 2.6 shard_map.114
  37.3 7.1 %all-to-all-start.1 = ((bf16[8,8,48,512]{3,2,1,0:T(8,128)(2,1)}), bf16[8,8,48,512]{3,2,1,0:T(8,128)(2,1)}, u32[]{:S(2)}, u32[]{:S(2)}) async-start(bf16[8,8,48,512]{3,2,1,0:T(8,128)(2,1)} %get-tuple-element.21), calls=%async_computation.1 | async-start | bytes 6291456 | tf_op jit(solution)/shard_map/all_to_all | solution.py:39
  48.0 34.1 %all-to-all-done.1.moved = bf16[8,8,48,512]{3,2,1,0:T(8,128)(2,1)} async-done(((bf16[8,8,48,512]{3,2,1,0:T(8,128)(2,1)}), bf16[8,8,48,512]{3,2,1,0:T(8,128)(2,1)}, u32[]{:S(2)}, u32[]{:S(2)}) %all-to-all-start.1) | async-done | bytes 3145760 | tf_op jit(solution)/shard_map/all_to_all | solution.py:39
  82.1 22.7 %shard_map.115 = bf16[8,8,48,512]{3,2,1,0:T(8,128)(2,1)} custom-call(s32[8]{0:T(128)} %stack.35.order.refs_0_, s32[1]{0:T(128)} %bitcast.15.own.refs_1_, bf16[8,8,48,512]{3,2,1,0:T(8,128)(2,1)} %all-to-all-done.1.moved, bf16[8,96,128]{2,1,0:T(8,128)(2,1)} %slice.8.other.refs_2_, bf16[8,32,512]{2,1,0:T(8,128)(2,1)} %copy-done.11, bf16[4096,896]{1,0:T(8,128)(2,1)} %bitcast.39, ...), custom_call_target="tpu_custom_call" | custom-call | flops 8455716864 | bytes 28311552 | tf_op jit(solution)/shard_map/pallas_call | solution.py:301
  104.8 8.0 %all-to-all-start.3 = ((bf16[64,48,512]{2,1,0:T(8,128)(2,1)}), bf16[64,48,512]{2,1,0:T(8,128)(2,1)S(1)}, u32[]{:S(2)}, u32[]{:S(2)}) async-start(bf16[64,48,512]{2,1,0:T(8,128)(2,1)} %bitcast.36), calls=%async_computation.3 | async-start | bytes 6291456 | tf_op jit(solution)/shard_map/all_to_all | solution.py:39
  112.8 1.5 collective-permute-start.8
  115.6 1.4 collective-permute-start.10
  117.0 49.7 %collective-permute-done.8.refs_9_ = bf16[8,96,512]{2,1,0:T(8,128)(2,1)S(1)} collective-permute-done((bf16[8,96,512]{2,1,0:T(8,128)(2,1)}, bf16[8,96,512]{2,1,0:T(8,128)(2,1)S(1)}, u32[]{:S(2)}, u32[]{:S(2)}) %collective-permute-start.8) | collective-permute-done | bytes 786464 | tf_op jit(solution)/shard_map/ppermute | solution.py:48
  166.7 2.7 collective-permute-start.13
  169.4 12.8 %collective-permute-done.10.refs_11_ = bf16[8,96,512]{2,1,0:T(8,128)(2,1)S(1)} collective-permute-done((bf16[8,96,512]{2,1,0:T(8,128)(2,1)}, bf16[8,96,512]{2,1,0:T(8,128)(2,1)S(1)}, u32[]{:S(2)}, u32[]{:S(2)}) %collective-permute-start.10) | collective-permute-done | bytes 786464 | tf_op jit(solution)/shard_map/ppermute | solution.py:48
  182.2 1.4 collective-permute-done.9.refs_10_
  183.6 16.9 %collective-permute-done.12.refs_13_ = bf16[8,96,512]{2,1,0:T(8,128)(2,1)S(1)} collective-permute-done((bf16[8,96,512]{2,1,0:T(8,128)(2,1)S(1)}, bf16[8,96,512]{2,1,0:T(8,128)(2,1)S(1)}, u32[]{:S(2)}, u32[]{:S(2)}) %collective-permute-start.12) | collective-permute-done | bytes 786464 | tf_op jit(solution)/shard_map/ppermute | solution.py:48
  202.2 32.1 %shard_map.116 = bf16[8,8,48,512]{3,2,1,0:T(8,128)(2,1)} custom-call(s32[8]{0:T(128)} %stack.35.order.refs_0_, s32[1]{0:T(128)} %bitcast.15.own.refs_1_, bf16[8,96,128]{2,1,0:T(8,128)(2,1)} %slice.8.other.refs_2_, bf16[8,32,512]{2,1,0:T(8,128)(2,1)} %copy-done.11, bf16[4096,896]{1,0:T(8,128)(2,1)} %bitcast.40, bf16[4096,896]{1,0:T(8,128)(2,1)} %bitcast.42, ...), custom_call_target="tpu_custom_call" | custom-call | flops 14092861440 | bytes 31457280 | tf_op jit(solution)/shard_map/pallas_call | solution.py:410
  234.4 7.2 %all-to-all-start.2 = ((bf16[64,48,512]{2,1,0:T(8,128)(2,1)}), bf16[64,48,512]{2,1,0:T(8,128)(2,1)}, u32[]{:S(2)}, u32[]{:S(2)}) async-start(bf16[64,48,512]{2,1,0:T(8,128)(2,1)} %bitcast.37), calls=%async_computation.2 | async-start | bytes 6291456 | tf_op jit(solution)/shard_map/all_to_all | solution.py:39
  243.3 38.4 %all-to-all-done.2 = bf16[64,48,512]{2,1,0:T(8,128)(2,1)} async-done(((bf16[64,48,512]{2,1,0:T(8,128)(2,1)}), bf16[64,48,512]{2,1,0:T(8,128)(2,1)}, u32[]{:S(2)}, u32[]{:S(2)}) %all-to-all-start.2) | async-done | bytes 3145760 | tf_op jit(solution)/shard_map/all_to_all | solution.py:39
  282.6 2.6 shard_map.117
  285.9 2.6 collective-permute-start.14
  288.5 4.1 %collective-permute-done.14 = bf16[128,512]{1,0:T(8,128)(2,1)S(1)} collective-permute-done((bf16[128,512]{1,0:T(8,128)(2,1)S(1)}, bf16[128,512]{1,0:T(8,128)(2,1)S(1)}, u32[]{:S(2)}, u32[]{:S(2)}) %collective-permute-start.14) | collective-permute-done | bytes 131104 | tf_op jit(solution)/shard_map/ppermute | solution.py:35
  (63 shorter events, 23.0 us)
Async XLA Ops:
  9.2 28.1 %copy-start.4 = (bf16[128,384]{1,0:T(8,128)(2,1)}, bf16[128,384]{1,0:T(8,128)(2,1)S(1)}, u32[]{:S(2)}) copy-start(bf16[128,384]{1,0:T(8,128)(2,1)S(1)} %get-tuple-element.18.sel) | copy-start | bytes 294916
  9.2 28.1 %all-to-all-start = ((bf16[8,96,640]{2,1,0:T(8,128)(2,1)}), bf16[8,96,640]{2,1,0:T(8,128)(2,1)S(1)}, u32[]{:S(2)}, u32[]{:S(2)}) async-start(bf16[8,96,640]{2,1,0:T(8,128)(2,1)} %get-tuple-element.17), calls=%async_computation | async-start | bytes 1966080 | tf_op jit(solution)/shard_map/all_to_all | solution.py:39
  16.0 5.8 %collective-permute-start = (bf16[160,512]{1,0:T(8,128)(2,1)S(1)}, bf16[160,512]{1,0:T(8,128)(2,1)S(1)}, u32[]{:S(2)}, u32[]{:S(2)}) collective-permute-start(bf16[160,512]{1,0:T(8,128)(2,1)S(1)} %get-tuple-element.19.refs_0_), channel_id=1, source_target_pairs={{0,1},{1,0},{2,3},{3,2},{4,5},{5,4},{6,7},{7,6},{8,9},{9,8},{10,11... | collective-permute-start | bytes 491528 | tf_op jit(solution)/shard_map/ppermute | solution.py:48
  17.3 8.5 %collective-permute-start.1 = (bf16[160,512]{1,0:T(8,128)(2,1)S(1)}, bf16[160,512]{1,0:T(8,128)(2,1)S(1)}, u32[]{:S(2)}, u32[]{:S(2)}) collective-permute-start(bf16[160,512]{1,0:T(8,128)(2,1)S(1)} %get-tuple-element.19.refs_0_), channel_id=1, source_target_pairs={{0,2},{1,3},{2,4},{3,5},{4,6},{5,7},{6,0},{7,1},{8,10},{9,11},{10,... | collective-permute-start | bytes 491528 | tf_op jit(solution)/shard_map/ppermute | solution.py:48
  21.8 5.2 %collective-permute-start.4 = (bf16[160,512]{1,0:T(8,128)(2,1)S(1)}, bf16[160,512]{1,0:T(8,128)(2,1)S(1)}, u32[]{:S(2)}, u32[]{:S(2)}) collective-permute-start(bf16[160,512]{1,0:T(8,128)(2,1)S(1)} %collective-permute-done.refs_1_), channel_id=1, source_target_pairs={{0,6},{1,7},{2,0},{3,1},{4,2},{5,3},{6,4},{7,5},{8,14},{9,15},{10,... | collective-permute-start | bytes 491528 | tf_op jit(solution)/shard_map/ppermute | solution.py:48
  24.3 6.3 %collective-permute-start.3 = (bf16[160,512]{1,0:T(8,128)(2,1)S(1)}, bf16[160,512]{1,0:T(8,128)(2,1)S(1)}, u32[]{:S(2)}, u32[]{:S(2)}) collective-permute-start(bf16[160,512]{1,0:T(8,128)(2,1)S(1)} %get-tuple-element.19.refs_0_), channel_id=1, source_target_pairs={{0,6},{1,7},{2,0},{3,1},{4,2},{5,3},{6,4},{7,5},{8,14},{9,15},{10,... | collective-permute-start | bytes 491528 | tf_op jit(solution)/shard_map/ppermute | solution.py:48
  24.9 5.7 %collective-permute-start.2 = (bf16[160,512]{1,0:T(8,128)(2,1)S(1)}, bf16[160,512]{1,0:T(8,128)(2,1)S(1)}, u32[]{:S(2)}, u32[]{:S(2)}) collective-permute-start(bf16[160,512]{1,0:T(8,128)(2,1)S(1)} %collective-permute-done.refs_1_), channel_id=1, source_target_pairs={{0,2},{1,3},{2,4},{3,5},{4,6},{5,7},{6,0},{7,1},{8,10},{9,11},{10,... | collective-permute-start | bytes 491528 | tf_op jit(solution)/shard_map/ppermute | solution.py:48
  25.8 8.1 %collective-permute-start.5 = (bf16[160,512]{1,0:T(8,128)(2,1)S(1)}, bf16[160,512]{1,0:T(8,128)(2,1)S(1)}, u32[]{:S(2)}, u32[]{:S(2)}) collective-permute-start(bf16[160,512]{1,0:T(8,128)(2,1)S(1)} %collective-permute-done.1.refs_2_), channel_id=1, source_target_pairs={{0,2},{1,3},{2,4},{3,5},{4,6},{5,7},{6,0},{7,1},{8,10},{9,11},{10,... | collective-permute-start | bytes 491528 | tf_op jit(solution)/shard_map/ppermute | solution.py:48
  27.1 6.9 %collective-permute-start.6 = (bf16[160,512]{1,0:T(8,128)(2,1)S(1)}, bf16[160,512]{1,0:T(8,128)(2,1)S(1)}, u32[]{:S(2)}, u32[]{:S(2)}) collective-permute-start(bf16[160,512]{1,0:T(8,128)(2,1)S(1)} %collective-permute-done.4.refs_5_), channel_id=1, source_target_pairs={{0,6},{1,7},{2,0},{3,1},{4,2},{5,3},{6,4},{7,5},{8,14},{9,15},{10,... | collective-permute-start | bytes 491528 | tf_op jit(solution)/shard_map/ppermute | solution.py:48
  37.3 44.7 %all-to-all-start.1 = ((bf16[8,8,48,512]{3,2,1,0:T(8,128)(2,1)}), bf16[8,8,48,512]{3,2,1,0:T(8,128)(2,1)}, u32[]{:S(2)}, u32[]{:S(2)}) async-start(bf16[8,8,48,512]{3,2,1,0:T(8,128)(2,1)} %get-tuple-element.21), calls=%async_computation.1 | async-start | bytes 6291456 | tf_op jit(solution)/shard_map/all_to_all | solution.py:39
  46.0 68.3 %collective-permute-start.7 = (bf16[8,96,512]{2,1,0:T(8,128)(2,1)}, bf16[8,96,512]{2,1,0:T(8,128)(2,1)}, u32[]{:S(2)}, u32[]{:S(2)}) collective-permute-start(bf16[8,96,512]{2,1,0:T(8,128)(2,1)} %slice.9.refs_7_), channel_id=1, source_target_pairs={{0,1},{1,0},{2,3},{3,2},{4,5},{5,4},{6,7},{7,6},{8,9},{9,8},{10,11... | collective-permute-start | bytes 2359304 | tf_op jit(solution)/shard_map/ppermute | solution.py:48
  104.8 129.6 %all-to-all-start.3 = ((bf16[64,48,512]{2,1,0:T(8,128)(2,1)}), bf16[64,48,512]{2,1,0:T(8,128)(2,1)S(1)}, u32[]{:S(2)}, u32[]{:S(2)}) async-start(bf16[64,48,512]{2,1,0:T(8,128)(2,1)} %bitcast.36), calls=%async_computation.3 | async-start | bytes 6291456 | tf_op jit(solution)/shard_map/all_to_all | solution.py:39
  112.8 53.9 %collective-permute-start.8 = (bf16[8,96,512]{2,1,0:T(8,128)(2,1)}, bf16[8,96,512]{2,1,0:T(8,128)(2,1)S(1)}, u32[]{:S(2)}, u32[]{:S(2)}) collective-permute-start(bf16[8,96,512]{2,1,0:T(8,128)(2,1)} %slice.9.refs_7_), channel_id=1, source_target_pairs={{0,2},{1,3},{2,4},{3,5},{4,6},{5,7},{6,0},{7,1},{8,10},{9,11},{10,... | collective-permute-start | bytes 2359304 | tf_op jit(solution)/shard_map/ppermute | solution.py:48
  114.3 52.5 %collective-permute-start.11 = (bf16[8,96,512]{2,1,0:T(8,128)(2,1)}, bf16[8,96,512]{2,1,0:T(8,128)(2,1)S(1)}, u32[]{:S(2)}, u32[]{:S(2)}) collective-permute-start(bf16[8,96,512]{2,1,0:T(8,128)(2,1)} %collective-permute-done.7.refs_8_), channel_id=1, source_target_pairs={{0,6},{1,7},{2,0},{3,1},{4,2},{5,3},{6,4},{7,5},{8,14},{9,15},{10,... | collective-permute-start | bytes 2359304 | tf_op jit(solution)/shard_map/ppermute | solution.py:48
  115.6 66.6 %collective-permute-start.10 = (bf16[8,96,512]{2,1,0:T(8,128)(2,1)}, bf16[8,96,512]{2,1,0:T(8,128)(2,1)S(1)}, u32[]{:S(2)}, u32[]{:S(2)}) collective-permute-start(bf16[8,96,512]{2,1,0:T(8,128)(2,1)} %slice.9.refs_7_), channel_id=1, source_target_pairs={{0,6},{1,7},{2,0},{3,1},{4,2},{5,3},{6,4},{7,5},{8,14},{9,15},{10,... | collective-permute-start | bytes 2359304 | tf_op jit(solution)/shard_map/ppermute | solution.py:48
  116.9 66.6 %collective-permute-start.9 = (bf16[8,96,512]{2,1,0:T(8,128)(2,1)}, bf16[8,96,512]{2,1,0:T(8,128)(2,1)S(1)}, u32[]{:S(2)}, u32[]{:S(2)}) collective-permute-start(bf16[8,96,512]{2,1,0:T(8,128)(2,1)} %collective-permute-done.7.refs_8_), channel_id=1, source_target_pairs={{0,2},{1,3},{2,4},{3,5},{4,6},{5,7},{6,0},{7,1},{8,10},{9,11},{10,... | collective-permute-start | bytes 2359304 | tf_op jit(solution)/shard_map/ppermute | solution.py:48
  166.7 33.7 %copy-start.12 = (bf16[8,96,512]{2,1,0:T(8,128)(2,1)}, bf16[8,96,512]{2,1,0:T(8,128)(2,1)S(1)}, u32[]{:S(2)}) copy-start(bf16[8,96,512]{2,1,0:T(8,128)(2,1)S(1)} %collective-permute-done.8.refs_9_) | copy-start | bytes 2359300
  166.7 33.7 %collective-permute-start.12 = (bf16[8,96,512]{2,1,0:T(8,128)(2,1)S(1)}, bf16[8,96,512]{2,1,0:T(8,128)(2,1)S(1)}, u32[]{:S(2)}, u32[]{:S(2)}) collective-permute-start(bf16[8,96,512]{2,1,0:T(8,128)(2,1)S(1)} %collective-permute-done.8.refs_9_), channel_id=1, source_target_pairs={{0,2},{1,3},{2,4},{3,5},{4,6},{5,7},{6,0},{7,1},{8,10},{9,11},{10,... | collective-permute-start | bytes 2359304 | tf_op jit(solution)/shard_map/ppermute | solution.py:48
  166.7 33.7 %copy-start.13 = (bf16[8,96,512]{2,1,0:T(8,128)(2,1)}, bf16[8,96,512]{2,1,0:T(8,128)(2,1)S(1)}, u32[]{:S(2)}) copy-start(bf16[8,96,512]{2,1,0:T(8,128)(2,1)S(1)} %collective-permute-done.11.refs_12_) | copy-start | bytes 2359300
  166.7 33.7 %collective-permute-start.13 = (bf16[8,96,512]{2,1,0:T(8,128)(2,1)S(1)}, bf16[8,96,512]{2,1,0:T(8,128)(2,1)S(1)}, u32[]{:S(2)}, u32[]{:S(2)}) collective-permute-start(bf16[8,96,512]{2,1,0:T(8,128)(2,1)S(1)} %collective-permute-done.11.refs_12_), channel_id=1, source_target_pairs={{0,6},{1,7},{2,0},{3,1},{4,2},{5,3},{6,4},{7,5},{8,14},{9,15},{10,... | collective-permute-start | bytes 2359304 | tf_op jit(solution)/shard_map/ppermute | solution.py:48
  182.2 18.2 %copy-start.14 = (bf16[8,96,512]{2,1,0:T(8,128)(2,1)}, bf16[8,96,512]{2,1,0:T(8,128)(2,1)S(1)}, u32[]{:S(2)}) copy-start(bf16[8,96,512]{2,1,0:T(8,128)(2,1)S(1)} %collective-permute-done.10.refs_11_) | copy-start | bytes 2359300
  234.4 47.3 %all-to-all-start.2 = ((bf16[64,48,512]{2,1,0:T(8,128)(2,1)}), bf16[64,48,512]{2,1,0:T(8,128)(2,1)}, u32[]{:S(2)}, u32[]{:S(2)}) async-start(bf16[64,48,512]{2,1,0:T(8,128)(2,1)} %bitcast.37), calls=%async_computation.2 | async-start | bytes 6291456 | tf_op jit(solution)/shard_map/all_to_all | solution.py:39
  241.6 40.1 %copy-start.3 = (bf16[1,128,512]{2,1,0:T(8,128)(2,1)S(1)}, bf16[1,128,512]{2,1,0:T(8,128)(2,1)}, u32[]{:S(2)}) copy-start(bf16[1,128,512]{2,1,0:T(8,128)(2,1)} %param.11) | copy-start | bytes 393220
  285.9 6.7 %collective-permute-start.14 = (bf16[128,512]{1,0:T(8,128)(2,1)S(1)}, bf16[128,512]{1,0:T(8,128)(2,1)S(1)}, u32[]{:S(2)}, u32[]{:S(2)}) collective-permute-start(bf16[128,512]{1,0:T(8,128)(2,1)S(1)} %get-tuple-element.30), channel_id=1, source_target_pairs={{0,64},{64,0},{1,65},{65,1},{2,66},{66,2},{3,67},{67,3},{4,68},{68... | collective-permute-start | bytes 393224 | tf_op jit(solution)/shard_map/ppermute | solution.py:35
  (13 other events, 33.2 us)
where the time goes:
time: 294 us; the launch traced here: 293 us
  waiting for transfers between devices  165 us (56%)
  Pallas kernels  63 us (21%)
  starting transfers between devices  49.8 us (17%)
  local copies, waits for them, and re-layouts  13.6 us (5%)
    ppermute x14, waiting for transfers between devices, shift(): return lax.ppermute(block, 'hid', route)  88.7 us
    all_to_all x4, waiting for transfers between devices, swap(): return lax.all_to_all(block, axes, split_axis=0, concat_axis=0, tiled=True)  72.5 us
    pallas_call x1, Pallas kernels, backward(): pl.pallas_call(backward_kernel, out_shape=jax.ShapeDtypeStruct((blocks, G...  32.1 us
    all_to_all x4, starting transfers between devices, swap(): return lax.all_to_all(block, axes, split_axis=0, concat_axis=0, tiled=True)  29.1 us
    pallas_call x1, Pallas kernels, forward(): pl.pallas_call(forward_kernel, out_shape=jax.ShapeDtypeStruct(moved.shape...  22.7 us
    ppermute x14, starting transfers between devices, shift(): return lax.ppermute(block, 'hid', route)  18.1 us
    unnamed x39, local copies, waits for them, and re-layouts  11.3 us
  transfers between devices with their start and end apart: 19, of which 11 were waited for; matrix products, arithmetic and copies ran while one was open for 1% of the time, Pallas kernels for 20%

commit v1 on v0

--- a/solution.py
+++ b/solution.py
@@ -51,6 +51,7 @@
 def gather_groups(block):
     other = shift(block, 0, 1)
     right, left = shift(block, 1, 0), shift(block, -1, 0)
+    other, right, left = lax.optimization_barrier((other, right, left))
     right_other, left_other = shift(other, 1, 0), shift(other, -1, 0)
     far, far_other = shift(right, 1, 0), shift(left_other, -1, 0)
     return [block, other, right, right_other, left, left_other, far, far_other]
@@ -496,6 +497,7 @@
     other = packed[:, :, part:]
     pieces = gather_groups(packed[:, :, :part])
 
+    pieces, moved_next = lax.optimization_barrier((pieces, moved_next))
     out_next = forward(order, own, moved_next, other, table, gate_w, up_w, down_w)
     out_home = send_home(out_next)
     pieces, out_next = lax.optimization_barrier((pieces, out_next))

time: 294 us -> 237 us (0.81)
  waiting for transfers between devices: 165 us -> 108 us
    ppermute x14, waiting for transfers between devices: 88.7 us -> 57.9 us  [shift(): return lax.ppermute(block, 'hid', route)]
    all_to_all x4, waiting for transfers between devices: 72.5 us -> 46.4 us  [swap(): return lax.all_to_all(block, axes, split_axis=0, concat_axis=0, tiled=True)]
    unnamed x39 -> x35, local copies, waits for them, and re-layouts: 11.3 us -> 10.2 us
  transfers between devices with their start and end apart: 19 -> 19, of which waited for: 11 -> 11; matrix products, arithmetic and copies ran while one was open for 1% -> 1% of each run, Pallas kernels for 20% -> 15%
where the time goes in v1:
time: 237 us
  waiting for transfers between devices  108 us (46%)
  Pallas kernels  63 us (27%)
  starting transfers between devices  52.3 us (22%)
  local copies, waits for them, and re-layouts  11.6 us (5%)
    ppermute x14, waiting for transfers between devices, shift(): return lax.ppermute(block, 'hid', route)  57.9 us
    all_to_all x4, waiting for transfers between devices, swap(): return lax.all_to_all(block, axes, split_axis=0, concat_axis=0, tiled=True)  46.4 us
    pallas_call x1, Pallas kernels, backward(): pl.pallas_call(backward_kernel, out_shape=jax.ShapeDtypeStruct((blocks, G...  32.1 us
    all_to_all x4, starting transfers between devices, swap(): return lax.all_to_all(block, axes, split_axis=0, concat_axis=0, tiled=True)  29.6 us
    pallas_call x1, Pallas kernels, forward(): pl.pallas_call(forward_kernel, out_shape=jax.ShapeDtypeStruct(moved.shape...  22.7 us
    ppermute x14, starting transfers between devices, shift(): return lax.ppermute(block, 'hid', route)  20.1 us
    unnamed x35, local copies, waits for them, and re-layouts  10.2 us
  transfers between devices with their start and end apart: 19, of which 11 were waited for; matrix products, arithmetic and copies ran while one was open for 1% of the time, Pallas kernels for 15%

profile of v1, /device:TPU:1, one launch (start us, length us, event | category | flops | bytes accessed | tf_op | source)
XLA Modules:
  0.0 236.7 jit_solution(16302679525973548000)
XLA Ops:
  6.3 2.2 shard_map.113
  9.2 6.8 %all-to-all-start = ((bf16[8,96,640]{2,1,0:T(8,128)(2,1)}), bf16[8,96,640]{2,1,0:T(8,128)(2,1)S(1)}, u32[]{:S(2)}, u32[]{:S(2)}) async-start(bf16[8,96,640]{2,1,0:T(8,128)(2,1)} %get-tuple-element.32), calls=%async_computation | async-start | bytes 1966080 | tf_op jit(solution)/shard_map/all_to_all | solution.py:39
  21.8 2.2 collective-permute-done.1.refs_2_
  24.0 2.4 collective-permute-start.4
  26.4 2.3 collective-permute-done.4.refs_5_
  28.6 3.4 %collective-permute-start.6 = (bf16[160,512]{1,0:T(8,128)(2,1)S(1)}, bf16[160,512]{1,0:T(8,128)(2,1)S(1)}, u32[]{:S(2)}, u32[]{:S(2)}) collective-permute-start(bf16[160,512]{1,0:T(8,128)(2,1)S(1)} %collective-permute-done.4.refs_5_), channel_id=1, source_target_pairs={{0,6},{1,7},{2,0},{3,1},{4,2},{5,3},{6,4},{7,5},{8,14},{9,15},{10,... | collective-permute-start | bytes 491528 | tf_op jit(solution)/shard_map/ppermute | solution.py:48
  32.1 3.0 %collective-permute-done.5.refs_6_ = bf16[160,512]{1,0:T(8,128)(2,1)S(1)} collective-permute-done((bf16[160,512]{1,0:T(8,128)(2,1)S(1)}, bf16[160,512]{1,0:T(8,128)(2,1)S(1)}, u32[]{:S(2)}, u32[]{:S(2)}) %collective-permute-start.5) | collective-permute-done | bytes 163872 | tf_op jit(solution)/shard_map/ppermute | solution.py:48
  35.1 2.6 %shard_map.114 = (bf16[8,8,48,512]{3,2,1,0:T(8,128)(2,1)}, bf16[8,32,512]{2,1,0:T(8,128)(2,1)S(1)}) custom-call(bf16[128,384]{1,0:T(8,128)(2,1)S(1)} %get-tuple-element.33.sel, bf16[160,512]{1,0:T(8,128)(2,1)S(1)} %get-tuple-element.34.refs_0_, bf16[160,512]{1,0:T(8,128)(2,1)S(1)} %collective-permute-done.refs_1_, ...), custom_call_target="tpu_custom_call" | custom-call | tf_op jit(solution)/shard_map/pallas_call | solution.py:162
  38.5 7.0 %all-to-all-start.1 = ((bf16[8,8,48,512]{3,2,1,0:T(8,128)(2,1)}), bf16[8,8,48,512]{3,2,1,0:T(8,128)(2,1)}, u32[]{:S(2)}, u32[]{:S(2)}) async-start(bf16[8,8,48,512]{3,2,1,0:T(8,128)(2,1)} %get-tuple-element.42), calls=%async_computation.1 | async-start | bytes 6291456 | tf_op jit(solution)/shard_map/all_to_all | solution.py:39
  46.4 3.2 %collective-permute-start.9 = (bf16[8,96,512]{2,1,0:T(8,128)(2,1)S(1)}, bf16[8,96,512]{2,1,0:T(8,128)(2,1)S(1)}, u32[]{:S(2)}, u32[]{:S(2)}) collective-permute-start(bf16[8,96,512]{2,1,0:T(8,128)(2,1)S(1)} %slice.9.refs_7_), channel_id=1, source_target_pairs={{0,6},{1,7},{2,0},{3,1},{4,2},{5,3},{6,4},{7,5},{8,14},{9,15},{10,... | collective-permute-start | bytes 2359304 | tf_op jit(solution)/shard_map/ppermute | solution.py:48
  49.6 15.1 %collective-permute-done.7.refs_8_ = bf16[8,96,512]{2,1,0:T(8,128)(2,1)S(1)} collective-permute-done((bf16[8,96,512]{2,1,0:T(8,128)(2,1)S(1)}, bf16[8,96,512]{2,1,0:T(8,128)(2,1)S(1)}, u32[]{:S(2)}, u32[]{:S(2)}) %collective-permute-start.7) | collective-permute-done | bytes 786464 | tf_op jit(solution)/shard_map/ppermute | solution.py:48
  66.8 3.3 %collective-permute-start.11 = (bf16[8,96,512]{2,1,0:T(8,128)(2,1)S(1)}, bf16[8,96,512]{2,1,0:T(8,128)(2,1)}, u32[]{:S(2)}, u32[]{:S(2)}) collective-permute-start(bf16[8,96,512]{2,1,0:T(8,128)(2,1)S(1)} %collective-permute-done.7.refs_8_), channel_id=1, source_target_pairs={{0,6},{1,7},{2,0},{3,1},{4,2},{5,3},{6,4},{7,5},{8,14},{9,15},{10,... | collective-permute-start | bytes 2359304 | tf_op jit(solution)/shard_map/ppermute | solution.py:48
  70.1 16.2 %collective-permute-done.11.refs_12_ = bf16[8,96,512]{2,1,0:T(8,128)(2,1)} collective-permute-done((bf16[8,96,512]{2,1,0:T(8,128)(2,1)S(1)}, bf16[8,96,512]{2,1,0:T(8,128)(2,1)}, u32[]{:S(2)}, u32[]{:S(2)}) %collective-permute-start.11) | collective-permute-done | bytes 786464 | tf_op jit(solution)/shard_map/ppermute | solution.py:48
  86.3 3.5 %collective-permute-start.13 = (bf16[8,96,512]{2,1,0:T(8,128)(2,1)}, bf16[8,96,512]{2,1,0:T(8,128)(2,1)}, u32[]{:S(2)}, u32[]{:S(2)}) collective-permute-start(bf16[8,96,512]{2,1,0:T(8,128)(2,1)} %collective-permute-done.11.refs_12_), channel_id=1, source_target_pairs={{0,6},{1,7},{2,0},{3,1},{4,2},{5,3},{6,4},{7,5},{8,14},{9,15},{10,... | collective-permute-start | bytes 2359304 | tf_op jit(solution)/shard_map/ppermute | solution.py:48
  91.2 15.2 %collective-permute-done.12.refs_13_ = bf16[8,96,512]{2,1,0:T(8,128)(2,1)} collective-permute-done((bf16[8,96,512]{2,1,0:T(8,128)(2,1)S(1)}, bf16[8,96,512]{2,1,0:T(8,128)(2,1)}, u32[]{:S(2)}, u32[]{:S(2)}) %collective-permute-start.12) | collective-permute-done | bytes 786464 | tf_op jit(solution)/shard_map/ppermute | solution.py:48
  106.3 22.7 %shard_map.115 = bf16[8,8,48,512]{3,2,1,0:T(8,128)(2,1)} custom-call(s32[8]{0:T(128)} %stack.35.order.refs_0_, s32[1]{0:T(128)} %bitcast.15.own.refs_1_, bf16[8,8,48,512]{3,2,1,0:T(8,128)(2,1)} %all-to-all-done.1.moved, bf16[8,96,128]{2,1,0:T(8,128)(2,1)} %slice.8.other.refs_2_, bf16[8,32,512]{2,1,0:T(8,128)(2,1)} %copy-done.11, bf16[4096,896]{1,0:T(8,128)(2,1)} %bitcast.39, ...), custom_call_target="tpu_custom_call" | custom-call | flops 8455716864 | bytes 28311552 | tf_op jit(solution)/shard_map/pallas_call | solution.py:302
  129.1 8.7 %all-to-all-start.3 = ((bf16[64,48,512]{2,1,0:T(8,128)(2,1)}), bf16[64,48,512]{2,1,0:T(8,128)(2,1)S(1)}, u32[]{:S(2)}, u32[]{:S(2)}) async-start(bf16[64,48,512]{2,1,0:T(8,128)(2,1)} %bitcast.37), calls=%async_computation.3 | async-start | bytes 6291456 | tf_op jit(solution)/shard_map/all_to_all | solution.py:39
  137.7 32.1 %shard_map.116 = bf16[8,8,48,512]{3,2,1,0:T(8,128)(2,1)} custom-call(s32[8]{0:T(128)} %stack.35.order.refs_0_, s32[1]{0:T(128)} %bitcast.15.own.refs_1_, bf16[8,96,128]{2,1,0:T(8,128)(2,1)} %slice.8.other.refs_2_, bf16[8,32,512]{2,1,0:T(8,128)(2,1)} %copy-done.11, bf16[4096,896]{1,0:T(8,128)(2,1)} %bitcast.40, bf16[4096,896]{1,0:T(8,128)(2,1)} %bitcast.42, ...), custom_call_target="tpu_custom_call" | custom-call | flops 14092861440 | bytes 31457280 | tf_op jit(solution)/shard_map/pallas_call | solution.py:411
  169.9 8.0 %all-to-all-done.3 = bf16[64,48,512]{2,1,0:T(8,128)(2,1)S(1)} async-done(((bf16[64,48,512]{2,1,0:T(8,128)(2,1)}), bf16[64,48,512]{2,1,0:T(8,128)(2,1)S(1)}, u32[]{:S(2)}, u32[]{:S(2)}) %all-to-all-start.3) | async-done | bytes 3145760 | tf_op jit(solution)/shard_map/all_to_all | solution.py:39
  177.9 7.2 %all-to-all-start.2 = ((bf16[64,48,512]{2,1,0:T(8,128)(2,1)}), bf16[64,48,512]{2,1,0:T(8,128)(2,1)}, u32[]{:S(2)}, u32[]{:S(2)}) async-start(bf16[64,48,512]{2,1,0:T(8,128)(2,1)} %bitcast.36), calls=%async_computation.2 | async-start | bytes 6291456 | tf_op jit(solution)/shard_map/all_to_all | solution.py:39
  186.8 38.4 %all-to-all-done.2 = bf16[64,48,512]{2,1,0:T(8,128)(2,1)} async-done(((bf16[64,48,512]{2,1,0:T(8,128)(2,1)}), bf16[64,48,512]{2,1,0:T(8,128)(2,1)}, u32[]{:S(2)}, u32[]{:S(2)}) %all-to-all-start.2) | async-done | bytes 3145760 | tf_op jit(solution)/shard_map/all_to_all | solution.py:39
  226.1 2.6 %shard_map.117 = bf16[128,512]{1,0:T(8,128)(2,1)S(1)} custom-call(bf16[128,384]{1,0:T(8,128)(2,1)S(1)} %copy-done.8, bf16[8,8,48,512]{3,2,1,0:T(8,128)(2,1)} %bitcast.20.home, bf16[128,512]{1,0:T(8,128)(2,1)S(1)} %bitcast.31), custom_call_target="tpu_custom_call" | custom-call | tf_op jit(solution)/shard_map/pallas_call | solution.py:450
  229.3 2.6 %collective-permute-start.14 = (bf16[128,512]{1,0:T(8,128)(2,1)S(1)}, bf16[128,512]{1,0:T(8,128)(2,1)S(1)}, u32[]{:S(2)}, u32[]{:S(2)}) collective-permute-start(bf16[128,512]{1,0:T(8,128)(2,1)S(1)} %get-tuple-element.60), channel_id=1, source_target_pairs={{0,64},{64,0},{1,65},{65,1},{2,66},{66,2},{3,67},{67,3},{4,68},{68... | collective-permute-start | bytes 393224 | tf_op jit(solution)/shard_map/ppermute | solution.py:35
  232.0 4.1 %collective-permute-done.14 = bf16[128,512]{1,0:T(8,128)(2,1)S(1)} collective-permute-done((bf16[128,512]{1,0:T(8,128)(2,1)S(1)}, bf16[128,512]{1,0:T(8,128)(2,1)S(1)}, u32[]{:S(2)}, u32[]{:S(2)}) %collective-permute-start.14) | collective-permute-done | bytes 131104 | tf_op jit(solution)/shard_map/ppermute | solution.py:35
  (59 shorter events, 21.2 us)
Async XLA Ops:
  9.2 29.3 %copy-start.4 = (bf16[128,384]{1,0:T(8,128)(2,1)}, bf16[128,384]{1,0:T(8,128)(2,1)S(1)}, u32[]{:S(2)}) copy-start(bf16[128,384]{1,0:T(8,128)(2,1)S(1)} %get-tuple-element.33.sel) | copy-start | bytes 294916
  9.2 29.3 %all-to-all-start = ((bf16[8,96,640]{2,1,0:T(8,128)(2,1)}), bf16[8,96,640]{2,1,0:T(8,128)(2,1)S(1)}, u32[]{:S(2)}, u32[]{:S(2)}) async-start(bf16[8,96,640]{2,1,0:T(8,128)(2,1)} %get-tuple-element.32), calls=%async_computation | async-start | bytes 1966080 | tf_op jit(solution)/shard_map/all_to_all | solution.py:39
  16.0 5.8 %collective-permute-start = (bf16[160,512]{1,0:T(8,128)(2,1)S(1)}, bf16[160,512]{1,0:T(8,128)(2,1)S(1)}, u32[]{:S(2)}, u32[]{:S(2)}) collective-permute-start(bf16[160,512]{1,0:T(8,128)(2,1)S(1)} %get-tuple-element.34.refs_0_), channel_id=1, source_target_pairs={{0,1},{1,0},{2,3},{3,2},{4,5},{5,4},{6,7},{7,6},{8,9},{9,8},{10,11... | collective-permute-start | bytes 491528 | tf_op jit(solution)/shard_map/ppermute | solution.py:48
  17.3 6.7 %collective-permute-start.1 = (bf16[160,512]{1,0:T(8,128)(2,1)S(1)}, bf16[160,512]{1,0:T(8,128)(2,1)S(1)}, u32[]{:S(2)}, u32[]{:S(2)}) collective-permute-start(bf16[160,512]{1,0:T(8,128)(2,1)S(1)} %get-tuple-element.34.refs_0_), channel_id=1, source_target_pairs={{0,2},{1,3},{2,4},{3,5},{4,6},{5,7},{6,0},{7,1},{8,10},{9,11},{10,... | collective-permute-start | bytes 491528 | tf_op jit(solution)/shard_map/ppermute | solution.py:48
  18.5 5.5 %collective-permute-start.2 = (bf16[160,512]{1,0:T(8,128)(2,1)S(1)}, bf16[160,512]{1,0:T(8,128)(2,1)S(1)}, u32[]{:S(2)}, u32[]{:S(2)}) collective-permute-start(bf16[160,512]{1,0:T(8,128)(2,1)S(1)} %get-tuple-element.34.refs_0_), channel_id=1, source_target_pairs={{0,6},{1,7},{2,0},{3,1},{4,2},{5,3},{6,4},{7,5},{8,14},{9,15},{10,... | collective-permute-start | bytes 491528 | tf_op jit(solution)/shard_map/ppermute | solution.py:48
  24.0 4.6 %collective-permute-start.4 = (bf16[160,512]{1,0:T(8,128)(2,1)S(1)}, bf16[160,512]{1,0:T(8,128)(2,1)S(1)}, u32[]{:S(2)}, u32[]{:S(2)}) collective-permute-start(bf16[160,512]{1,0:T(8,128)(2,1)S(1)} %collective-permute-done.refs_1_), channel_id=1, source_target_pairs={{0,6},{1,7},{2,0},{3,1},{4,2},{5,3},{6,4},{7,5},{8,14},{9,15},{10,... | collective-permute-start | bytes 491528 | tf_op jit(solution)/shard_map/ppermute | solution.py:48
  26.4 5.7 %collective-permute-start.3 = (bf16[160,512]{1,0:T(8,128)(2,1)S(1)}, bf16[160,512]{1,0:T(8,128)(2,1)S(1)}, u32[]{:S(2)}, u32[]{:S(2)}) collective-permute-start(bf16[160,512]{1,0:T(8,128)(2,1)S(1)} %collective-permute-done.refs_1_), channel_id=1, source_target_pairs={{0,2},{1,3},{2,4},{3,5},{4,6},{5,7},{6,0},{7,1},{8,10},{9,11},{10,... | collective-permute-start | bytes 491528 | tf_op jit(solution)/shard_map/ppermute | solution.py:48
  26.4 8.7 %collective-permute-start.5 = (bf16[160,512]{1,0:T(8,128)(2,1)S(1)}, bf16[160,512]{1,0:T(8,128)(2,1)S(1)}, u32[]{:S(2)}, u32[]{:S(2)}) collective-permute-start(bf16[160,512]{1,0:T(8,128)(2,1)S(1)} %collective-permute-done.1.refs_2_), channel_id=1, source_target_pairs={{0,2},{1,3},{2,4},{3,5},{4,6},{5,7},{6,0},{7,1},{8,10},{9,11},{10,... | collective-permute-start | bytes 491528 | tf_op jit(solution)/shard_map/ppermute | solution.py:48
  28.6 6.5 %collective-permute-start.6 = (bf16[160,512]{1,0:T(8,128)(2,1)S(1)}, bf16[160,512]{1,0:T(8,128)(2,1)S(1)}, u32[]{:S(2)}, u32[]{:S(2)}) collective-permute-start(bf16[160,512]{1,0:T(8,128)(2,1)S(1)} %collective-permute-done.4.refs_5_), channel_id=1, source_target_pairs={{0,6},{1,7},{2,0},{3,1},{4,2},{5,3},{6,4},{7,5},{8,14},{9,15},{10,... | collective-permute-start | bytes 491528 | tf_op jit(solution)/shard_map/ppermute | solution.py:48
  38.5 67.9 %all-to-all-start.1 = ((bf16[8,8,48,512]{3,2,1,0:T(8,128)(2,1)}), bf16[8,8,48,512]{3,2,1,0:T(8,128)(2,1)}, u32[]{:S(2)}, u32[]{:S(2)}) async-start(bf16[8,8,48,512]{3,2,1,0:T(8,128)(2,1)} %get-tuple-element.42), calls=%async_computation.1 | async-start | bytes 6291456 | tf_op jit(solution)/shard_map/all_to_all | solution.py:39
  45.5 19.2 %collective-permute-start.7 = (bf16[8,96,512]{2,1,0:T(8,128)(2,1)S(1)}, bf16[8,96,512]{2,1,0:T(8,128)(2,1)S(1)}, u32[]{:S(2)}, u32[]{:S(2)}) collective-permute-start(bf16[8,96,512]{2,1,0:T(8,128)(2,1)S(1)} %slice.9.refs_7_), channel_id=1, source_target_pairs={{0,1},{1,0},{2,3},{3,2},{4,5},{5,4},{6,7},{7,6},{8,9},{9,8},{10,11... | collective-permute-start | bytes 2359304 | tf_op jit(solution)/shard_map/ppermute | solution.py:48
  45.8 21.0 %collective-permute-start.8 = (bf16[8,96,512]{2,1,0:T(8,128)(2,1)S(1)}, bf16[8,96,512]{2,1,0:T(8,128)(2,1)S(1)}, u32[]{:S(2)}, u32[]{:S(2)}) collective-permute-start(bf16[8,96,512]{2,1,0:T(8,128)(2,1)S(1)} %slice.9.refs_7_), channel_id=1, source_target_pairs={{0,2},{1,3},{2,4},{3,5},{4,6},{5,7},{6,0},{7,1},{8,10},{9,11},{10,... | collective-permute-start | bytes 2359304 | tf_op jit(solution)/shard_map/ppermute | solution.py:48
  46.4 20.4 %collective-permute-start.9 = (bf16[8,96,512]{2,1,0:T(8,128)(2,1)S(1)}, bf16[8,96,512]{2,1,0:T(8,128)(2,1)S(1)}, u32[]{:S(2)}, u32[]{:S(2)}) collective-permute-start(bf16[8,96,512]{2,1,0:T(8,128)(2,1)S(1)} %slice.9.refs_7_), channel_id=1, source_target_pairs={{0,6},{1,7},{2,0},{3,1},{4,2},{5,3},{6,4},{7,5},{8,14},{9,15},{10,... | collective-permute-start | bytes 2359304 | tf_op jit(solution)/shard_map/ppermute | solution.py:48
  64.7 64.4 %copy-start.13 = (bf16[8,96,512]{2,1,0:T(8,128)(2,1)}, bf16[8,96,512]{2,1,0:T(8,128)(2,1)S(1)}, u32[]{:S(2)}) copy-start(bf16[8,96,512]{2,1,0:T(8,128)(2,1)S(1)} %collective-permute-done.7.refs_8_) | copy-start | bytes 2359300
  66.8 62.3 %copy-start.14 = (bf16[8,96,512]{2,1,0:T(8,128)(2,1)}, bf16[8,96,512]{2,1,0:T(8,128)(2,1)S(1)}, u32[]{:S(2)}) copy-start(bf16[8,96,512]{2,1,0:T(8,128)(2,1)S(1)} %collective-permute-done.8.refs_9_) | copy-start | bytes 2359300
  66.8 19.5 %copy-start.15 = (bf16[8,96,512]{2,1,0:T(8,128)(2,1)}, bf16[8,96,512]{2,1,0:T(8,128)(2,1)S(1)}, u32[]{:S(2)}) copy-start(bf16[8,96,512]{2,1,0:T(8,128)(2,1)S(1)} %collective-permute-done.9.refs_11_) | copy-start | bytes 2359300
  66.8 19.5 %collective-permute-start.11 = (bf16[8,96,512]{2,1,0:T(8,128)(2,1)S(1)}, bf16[8,96,512]{2,1,0:T(8,128)(2,1)}, u32[]{:S(2)}, u32[]{:S(2)}) collective-permute-start(bf16[8,96,512]{2,1,0:T(8,128)(2,1)S(1)} %collective-permute-done.7.refs_8_), channel_id=1, source_target_pairs={{0,6},{1,7},{2,0},{3,1},{4,2},{5,3},{6,4},{7,5},{8,14},{9,15},{10,... | collective-permute-start | bytes 2359304 | tf_op jit(solution)/shard_map/ppermute | solution.py:48
  70.1 21.1 %collective-permute-start.10 = (bf16[8,96,512]{2,1,0:T(8,128)(2,1)S(1)}, bf16[8,96,512]{2,1,0:T(8,128)(2,1)}, u32[]{:S(2)}, u32[]{:S(2)}) collective-permute-start(bf16[8,96,512]{2,1,0:T(8,128)(2,1)S(1)} %collective-permute-done.7.refs_8_), channel_id=1, source_target_pairs={{0,2},{1,3},{2,4},{3,5},{4,6},{5,7},{6,0},{7,1},{8,10},{9,11},{10,... | collective-permute-start | bytes 2359304 | tf_op jit(solution)/shard_map/ppermute | solution.py:48
  70.1 36.2 %collective-permute-start.12 = (bf16[8,96,512]{2,1,0:T(8,128)(2,1)S(1)}, bf16[8,96,512]{2,1,0:T(8,128)(2,1)}, u32[]{:S(2)}, u32[]{:S(2)}) collective-permute-start(bf16[8,96,512]{2,1,0:T(8,128)(2,1)S(1)} %collective-permute-done.8.refs_9_), channel_id=1, source_target_pairs={{0,2},{1,3},{2,4},{3,5},{4,6},{5,7},{6,0},{7,1},{8,10},{9,11},{10,... | collective-permute-start | bytes 2359304 | tf_op jit(solution)/shard_map/ppermute | solution.py:48
  86.3 20.1 %collective-permute-start.13 = (bf16[8,96,512]{2,1,0:T(8,128)(2,1)}, bf16[8,96,512]{2,1,0:T(8,128)(2,1)}, u32[]{:S(2)}, u32[]{:S(2)}) collective-permute-start(bf16[8,96,512]{2,1,0:T(8,128)(2,1)} %collective-permute-done.11.refs_12_), channel_id=1, source_target_pairs={{0,6},{1,7},{2,0},{3,1},{4,2},{5,3},{6,4},{7,5},{8,14},{9,15},{10,... | collective-permute-start | bytes 2359304 | tf_op jit(solution)/shard_map/ppermute | solution.py:48
  129.1 48.8 %all-to-all-start.3 = ((bf16[64,48,512]{2,1,0:T(8,128)(2,1)}), bf16[64,48,512]{2,1,0:T(8,128)(2,1)S(1)}, u32[]{:S(2)}, u32[]{:S(2)}) async-start(bf16[64,48,512]{2,1,0:T(8,128)(2,1)} %bitcast.37), calls=%async_computation.3 | async-start | bytes 6291456 | tf_op jit(solution)/shard_map/all_to_all | solution.py:39
  177.9 47.3 %all-to-all-start.2 = ((bf16[64,48,512]{2,1,0:T(8,128)(2,1)}), bf16[64,48,512]{2,1,0:T(8,128)(2,1)}, u32[]{:S(2)}, u32[]{:S(2)}) async-start(bf16[64,48,512]{2,1,0:T(8,128)(2,1)} %bitcast.36), calls=%async_computation.2 | async-start | bytes 6291456 | tf_op jit(solution)/shard_map/all_to_all | solution.py:39
  185.1 40.1 %copy-start.3 = (bf16[1,128,512]{2,1,0:T(8,128)(2,1)S(1)}, bf16[1,128,512]{2,1,0:T(8,128)(2,1)}, u32[]{:S(2)}) copy-start(bf16[1,128,512]{2,1,0:T(8,128)(2,1)} %param.11) | copy-start | bytes 393220
  229.3 6.7 %collective-permute-start.14 = (bf16[128,512]{1,0:T(8,128)(2,1)S(1)}, bf16[128,512]{1,0:T(8,128)(2,1)S(1)}, u32[]{:S(2)}, u32[]{:S(2)}) collective-permute-start(bf16[128,512]{1,0:T(8,128)(2,1)S(1)} %get-tuple-element.60), channel_id=1, source_target_pairs={{0,64},{64,0},{1,65},{65,1},{2,66},{66,2},{3,67},{67,3},{4,68},{68... | collective-permute-start | bytes 393224 | tf_op jit(solution)/shard_map/ppermute | solution.py:35
  (11 other events, 15.4 us)

commit v2 on v1

--- a/solution.py
+++ b/solution.py
@@ -48,13 +48,21 @@
     return lax.ppermute(block, "hid", route)
 
 
-def gather_groups(block):
+def gather_near(block):
     other = shift(block, 0, 1)
     right, left = shift(block, 1, 0), shift(block, -1, 0)
     other, right, left = lax.optimization_barrier((other, right, left))
     right_other, left_other = shift(other, 1, 0), shift(other, -1, 0)
-    far, far_other = shift(right, 1, 0), shift(left_other, -1, 0)
-    return [block, other, right, right_other, left, left_other, far, far_other]
+    return [block, other, right, right_other, left, left_other]
+
+
+def gather_far(near):
+    return [shift(near[2], 1, 0), shift(near[5], -1, 0)]
+
+
+def gather_groups(block):
+    near = gather_near(block)
+    return near + gather_far(near)
 
 
 def arrival_order():
@@ -74,6 +82,10 @@
     middle = rest.astype(jnp.bfloat16)
     low = (rest - middle.astype(jnp.float32)).astype(jnp.bfloat16)
     return high, middle, low
+
+
+def whole(shape):
+    return pl.BlockSpec(shape, lambda i: (0,) * len(shape))
 
 
 def pack_kernel(
@@ -140,8 +152,9 @@
     return pl.pallas_call(
         functools.partial(pack_kernel, capacity),
         out_shape=[jax.ShapeDtypeStruct(s, jnp.bfloat16) for s in shapes],
-        in_specs=[VMEM] * 7,
-        out_specs=[VMEM] * 4,
+        grid=(1,),
+        in_specs=[whole(a.shape) for a in (routes_s, routes_n, saved, cot, upcoming, gain, router)],
+        out_specs=[whole(s) for s in shapes],
         compiler_params=pltpu.CompilerParams(vmem_limit_bytes=LIMIT // 2),
     )(routes_s, routes_n, saved, cot, upcoming, gain, router)
 
@@ -221,7 +234,17 @@
     return copies
 
 
-def prepare(own, other_start, take, other, table, normed, scales, diffs, logits, width):
+def start(copies):
+    for copy in copies:
+        copy.start()
+
+
+def wait(copies):
+    for copy in copies:
+        copy.wait()
+
+
+def prepare(own, other_start, take, other, table, normed, scales, diffs, logits, width, between):
     blocks = other.shape[0]
     part = width // GROUPS
     for group in range(GROUPS):
@@ -231,6 +254,7 @@
             logits[...] = found
         else:
             logits[...] += found
+    start(between)
 
     @pl.loop(0, blocks)
     def _(block):
@@ -252,26 +276,43 @@
             ).astype(jnp.bfloat16)
 
 
+def fetch_blocks(source, target, sems):
+    return [
+        pltpu.make_async_copy(source.at[block], target.at[block], sems.at[block])
+        for block in range(source.shape[0])
+    ]
+
+
+def hand_out(group, place, source, target, sems):
+    return pltpu.make_async_copy(
+        source.at[:, group : group + 1], target.at[:, pl.ds(place, 1)], sems.at[group]
+    )
+
+
 def forward_kernel(
-    order, own, moved, other, table, gate_w, up_w, down_w, out,
-    gate_b, up_b, down_b, normed, gate, up, hidden, scales, diffs, logits, sem_g, sem_u, sem_d
+    order, own, moved_in, other, table, gate_w, up_w, down_w, out_to,
+    moved, out, gate_b, up_b, down_b, normed, gate, up, hidden, scales, diffs, logits,
+    sem_m, sem_o, sem_g, sem_u, sem_d
 ):
     blocks, _, capacity, part = moved.shape
+    arrive = fetch_blocks(moved_in, moved, sem_m)
+    start(arrive)
     copies = fetch_rows(order, gate_w, gate_b, sem_g, part)
     copies_up = fetch_rows(order, up_w, up_b, sem_u, part)
     copies_down = fetch_columns(None, down_w, down_b, sem_d, part)
-    for copy in copies + copies_up + copies_down:
-        copy.start()
+    start(copies)
+    wait(arrive)
 
     def take(group, block):
         return moved[block, group]
 
-    prepare(own[0], capacity, take, other, table, normed, scales, diffs, logits, GROUPS * part)
-    for copy in copies:
-        copy.wait()
+    prepare(
+        own[0], capacity, take, other, table, normed, scales, diffs, logits, GROUPS * part, copies_up
+    )
+    wait(copies)
+    start(copies_down)
     gate[...] = product(normed[...], gate_b[...], INNER)
-    for copy in copies_up:
-        copy.wait()
+    wait(copies_up)
     up[...] = product(normed[...], up_b[...], INNER)
 
     @pl.loop(0, blocks)
@@ -285,6 +326,9 @@
         copies_down[group].wait()
         rows = product(hidden[...], down_b[:, group * part : (group + 1) * part], INNER)
         out[:, group] = (rows * share).astype(jnp.bfloat16).reshape(blocks, capacity, part)
+        hand_out(group, group, out, out_to, sem_o).start()
+    for group in range(GROUPS):
+        hand_out(group, group, out, out_to, sem_o).wait()
 
 
 def weight_scratch(width, units):
@@ -302,9 +346,10 @@
     return pl.pallas_call(
         forward_kernel,
         out_shape=jax.ShapeDtypeStruct(moved.shape, jnp.bfloat16),
-        in_specs=[SMEM, SMEM, VMEM, VMEM, VMEM, PLACE, PLACE, PLACE],
-        out_specs=VMEM,
-        scratch_shapes=weight_scratch(width, units)
+        in_specs=[SMEM, SMEM, PLACE, VMEM, VMEM, PLACE, PLACE, PLACE],
+        out_specs=PLACE,
+        scratch_shapes=[pltpu.VMEM(moved.shape, jnp.bfloat16)] * 2
+        + weight_scratch(width, units)
         + [
             pltpu.VMEM((total, width), jnp.bfloat16),
             pltpu.VMEM((total, units), jnp.float32),
@@ -314,7 +359,8 @@
             pltpu.VMEM((total, 128), jnp.float32),
             pltpu.VMEM((total, TABLE), jnp.float32),
         ]
-        + [pltpu.SemaphoreType.DMA((GROUPS,))] * 3,
+        + [pltpu.SemaphoreType.DMA((blocks,))]
+        + [pltpu.SemaphoreType.DMA((GROUPS,))] * 4,
         compiler_params=pltpu.CompilerParams(vmem_limit_bytes=LIMIT),
         cost_estimate=pl.CostEstimate(
             flops=6 * total * width * units,
@@ -326,23 +372,29 @@
 
 def backward_kernel(*refs):
     order, own, other, table, gate_w, up_w, down_w = refs[:7]
-    pieces = refs[7 : 7 + GROUPS]
+    pieces_in = refs[7 : 7 + GROUPS]
+    out_to, pieces = refs[7 + GROUPS], refs[8 + GROUPS : 8 + 2 * GROUPS]
     (
         out, gate_b, up_b, down_b, normed, cots, gate, up, grad, grad_gate, grad_up,
-        scales, diffs, ones, twos, logits, sem_g, sem_u, sem_d,
-    ) = refs[7 + GROUPS :]
+        scales, diffs, ones, twos, logits, sem_m, sem_o, sem_g, sem_u, sem_d,
+    ) = refs[8 + 2 * GROUPS :]
     blocks, _, capacity, part = out.shape
     width = GROUPS * part
+    arrive = [
+        pltpu.make_async_copy(pieces_in[group], pieces[group], sem_m.at[group])
+        for group in range(GROUPS)
+    ]
+    start(arrive)
     copies = fetch_rows(order, gate_w, gate_b, sem_g, part)
     copies_up = fetch_rows(order, up_w, up_b, sem_u, part)
     copies_down = fetch_columns(order, down_w, down_b, sem_d, part)
-    for copy in copies + copies_up + copies_down:
-        copy.start()
+    start(copies)
+    wait(arrive)
 
     def take(group, block):
         return pieces[group][block, 0:STEP, :]
 
-    prepare(own[0], 0, take, other, table, normed, scales, diffs, logits, width)
+    prepare(own[0], 0, take, other, table, normed, scales, diffs, logits, width, copies_up)
 
     @pl.loop(0, blocks)
     def _(block):
@@ -350,14 +402,12 @@
         for group in range(GROUPS):
             cots[at, group * part : (group + 1) * part] = pieces[group][block, STEP : 2 * STEP, :]
 
-    for copy in copies:
-        copy.wait()
+    wait(copies)
+    start(copies_down)
     gate[...] = product(normed[...], gate_b[...], INNER)
-    for copy in copies_up:
-        copy.wait()
+    wait(copies_up)
     up[...] = product(normed[...], up_b[...], INNER)
-    for copy in copies_down:
-        copy.wait()
+    wait(copies_down)
     grad[...] = product(cots[...], down_b[...], CONTRACT)
 
     @pl.loop(0, blocks)
@@ -399,7 +449,10 @@
             + turn * widen(ones[...], part)
             - values.astype(jnp.float32) * widen(twos[...], part)
         )
-        out[:, pl.ds(order[group], 1)] = rows.astype(jnp.bfloat16).reshape(blocks, 1, capacity, part)
+        out[:, group] = rows.astype(jnp.bfloat16).reshape(blocks, capacity, part)
+        hand_out(group, order[group], out, out_to, sem_o).start()
+    for group in range(GROUPS):
+        hand_out(group, order[group], out, out_to, sem_o).wait()
 
 
 def backward(order, own, other, table, gate_w, up_w, down_w, pieces):
@@ -411,9 +464,11 @@
     return pl.pallas_call(
         backward_kernel,
         out_shape=jax.ShapeDtypeStruct((blocks, GROUPS, capacity, part), jnp.bfloat16),
-        in_specs=[SMEM, SMEM, VMEM, VMEM, PLACE, PLACE, PLACE] + [VMEM] * GROUPS,
-        out_specs=VMEM,
-        scratch_shapes=weight_scratch(width, units)
+        in_specs=[SMEM, SMEM, VMEM, VMEM, PLACE, PLACE, PLACE] + [PLACE] * GROUPS,
+        out_specs=PLACE,
+        scratch_shapes=[pltpu.VMEM((blocks, double, part), jnp.bfloat16)] * GROUPS
+        + [pltpu.VMEM((blocks, GROUPS, capacity, part), jnp.bfloat16)]
+        + weight_scratch(width, units)
         + [
             pltpu.VMEM((total, width), jnp.bfloat16),
             pltpu.VMEM((total, width), jnp.bfloat16),
@@ -428,7 +483,7 @@
             small,
             pltpu.VMEM((total, TABLE), jnp.float32),
         ]
-        + [pltpu.SemaphoreType.DMA((GROUPS,))] * 3,
+        + [pltpu.SemaphoreType.DMA((GROUPS,))] * 5,
         compiler_params=pltpu.CompilerParams(vmem_limit_bytes=LIMIT),
         cost_estimate=pl.CostEstimate(
             flops=10 * total * width * units,
@@ -495,12 +550,14 @@
     moved_next, table = spread(sel_next, gather_groups(tokens_next), experts)
     moved_next = swap(moved_next, "expert")
     other = packed[:, :, part:]
-    pieces = gather_groups(packed[:, :, :part])
-
-    pieces, moved_next = lax.optimization_barrier((pieces, moved_next))
+    near = gather_near(packed[:, :, :part])
+
+    near, moved_next = lax.optimization_barrier((near, moved_next))
+    far = gather_far(near)
     out_next = forward(order, own, moved_next, other, table, gate_w, up_w, down_w)
+    far, out_next = lax.optimization_barrier((far, out_next))
+    pieces = near + far
     out_home = send_home(out_next)
-    pieces, out_next = lax.optimization_barrier((pieces, out_next))
     back_part = backward(order, own, other, table, gate_w, up_w, down_w, pieces)
     back_home = send_home(back_part)
 

time: 237 us -> 222 us (0.937)
  waiting for transfers between devices: 108 us -> 100 us
  Pallas kernels: 63 us -> 58.1 us
  starting transfers between devices: 52.3 us -> 48.5 us
    ppermute x14, waiting for transfers between devices: 57.9 us -> 47.6 us  [shift(): return lax.ppermute(block, 'hid', route)]
    ppermute x14, starting transfers between devices: 20.1 us -> 16.3 us  [shift(): return lax.ppermute(block, 'hid', route)]
    pallas_call x1, Pallas kernels: 22.7 us -> 20.1 us  [forward(): pl.pallas_call(forward_kernel, out_shape=jax.ShapeDtypeStruct(moved.shape...]
    unnamed x35 -> x39, local copies, waits for them, and re-layouts: 10.2 us -> 11.3 us
  transfers between devices with their start and end apart: 19 -> 19, of which waited for: 11 -> 11; matrix products, arithmetic and copies ran while one was open for 1% -> 1% of each run, Pallas kernels for 15% -> 24%
where the time goes in v2:
time: 222 us; the launch traced here: 221 us
  waiting for transfers between devices  100 us (45%)
  Pallas kernels  58.1 us (26%)
  starting transfers between devices  48.5 us (22%)
  local copies, waits for them, and re-layouts  12.7 us (6%)
    all_to_all x4, waiting for transfers between devices, swap(): return lax.all_to_all(block, axes, split_axis=0, concat_axis=0, tiled=True)  48.7 us
    ppermute x14, waiting for transfers between devices, shift(): return lax.ppermute(block, 'hid', route)  47.6 us
    pallas_call x1, Pallas kernels, backward(): pl.pallas_call(backward_kernel, out_shape=jax.ShapeDtypeStruct((blocks, G...  29.9 us
    all_to_all x4, starting transfers between devices, swap(): return lax.all_to_all(block, axes, split_axis=0, concat_axis=0, tiled=True)  29.5 us
    pallas_call x1, Pallas kernels, forward(): pl.pallas_call(forward_kernel, out_shape=jax.ShapeDtypeStruct(moved.shape...  20.1 us
    ppermute x14, starting transfers between devices, shift(): return lax.ppermute(block, 'hid', route)  16.3 us
    unnamed x39, local copies, waits for them, and re-layouts  11.3 us
  transfers between devices with their start and end apart: 19, of which 11 were waited for; matrix products, arithmetic and copies ran while one was open for 1% of the time, Pallas kernels for 24%

profile of v2, /device:TPU:1, one launch (start us, length us, event | category | flops | bytes accessed | tf_op | source)
XLA Modules:
  0.0 221.2 jit_solution(18173599778863534589)
XLA Ops:
  6.3 2.2 %shard_map.113 = (bf16[8,96,640]{2,1,0:T(8,128)(2,1)}, bf16[160,512]{1,0:T(8,128)(2,1)S(1)}, bf16[128,384]{1,0:T(8,128)(2,1)S(1)}, bf16[128,384]{1,0:T(8,128)(2,1)S(1)}) custom-call(s32[128,2]{1,0:T(8,128)S(1)} %bitcast.32, s32[128,2]{1,0:T(8,128)S(1)} %bitcast.33, bf16[128,512]{1,0:T(8,128)(2,1)S(1)} %bitcast.34, bf16[128,512]{1,0:T(8,128)(2,1)S(1)} %bitcast.30, ...), custom_call_target="tpu_custom_call" | custom-call | tf_op jit(solution)/shard_map/pallas_call | solution.py:152
  9.2 6.8 %all-to-all-start = ((bf16[8,96,640]{2,1,0:T(8,128)(2,1)}), bf16[8,96,640]{2,1,0:T(8,128)(2,1)S(1)}, u32[]{:S(2)}, u32[]{:S(2)}) async-start(bf16[8,96,640]{2,1,0:T(8,128)(2,1)} %get-tuple-element.25), calls=%async_computation | async-start | bytes 1966080 | tf_op jit(solution)/shard_map/all_to_all | solution.py:39
  16.0 2.5 %collective-permute-start.2 = (bf16[160,512]{1,0:T(8,128)(2,1)S(1)}, bf16[160,512]{1,0:T(8,128)(2,1)S(1)}, u32[]{:S(2)}, u32[]{:S(2)}) collective-permute-start(bf16[160,512]{1,0:T(8,128)(2,1)S(1)} %get-tuple-element.27.refs_0_), channel_id=1, source_target_pairs={{0,6},{1,7},{2,0},{3,1},{4,2},{5,3},{6,4},{7,5},{8,14},{9,15},{10,... | collective-permute-start | bytes 491528 | tf_op jit(solution)/shard_map/ppermute | solution.py:48
  19.8 2.3 %collective-permute-done.2.refs_4_ = bf16[160,512]{1,0:T(8,128)(2,1)S(1)} collective-permute-done((bf16[160,512]{1,0:T(8,128)(2,1)S(1)}, bf16[160,512]{1,0:T(8,128)(2,1)S(1)}, u32[]{:S(2)}, u32[]{:S(2)}) %collective-permute-start.2) | collective-permute-done | bytes 163872 | tf_op jit(solution)/shard_map/ppermute | solution.py:48
  22.1 3.1 %collective-permute-done.1.refs_2_ = bf16[160,512]{1,0:T(8,128)(2,1)S(1)} collective-permute-done((bf16[160,512]{1,0:T(8,128)(2,1)S(1)}, bf16[160,512]{1,0:T(8,128)(2,1)S(1)}, u32[]{:S(2)}, u32[]{:S(2)}) %collective-permute-start.1) | collective-permute-done | bytes 163872 | tf_op jit(solution)/shard_map/ppermute | solution.py:48
  26.7 3.1 %collective-permute-done.4.refs_5_ = bf16[160,512]{1,0:T(8,128)(2,1)S(1)} collective-permute-done((bf16[160,512]{1,0:T(8,128)(2,1)S(1)}, bf16[160,512]{1,0:T(8,128)(2,1)S(1)}, u32[]{:S(2)}, u32[]{:S(2)}) %collective-permute-start.4) | collective-permute-done | bytes 163872 | tf_op jit(solution)/shard_map/ppermute | solution.py:48
  29.8 2.2 %collective-permute-start.6 = (bf16[160,512]{1,0:T(8,128)(2,1)S(1)}, bf16[160,512]{1,0:T(8,128)(2,1)S(1)}, u32[]{:S(2)}, u32[]{:S(2)}) collective-permute-start(bf16[160,512]{1,0:T(8,128)(2,1)S(1)} %collective-permute-done.4.refs_5_), channel_id=1, source_target_pairs={{0,6},{1,7},{2,0},{3,1},{4,2},{5,3},{6,4},{7,5},{8,14},{9,15},{10,... | collective-permute-start | bytes 491528 | tf_op jit(solution)/shard_map/ppermute | solution.py:48
  32.0 3.0 %collective-permute-done.5.refs_6_ = bf16[160,512]{1,0:T(8,128)(2,1)S(1)} collective-permute-done((bf16[160,512]{1,0:T(8,128)(2,1)S(1)}, bf16[160,512]{1,0:T(8,128)(2,1)S(1)}, u32[]{:S(2)}, u32[]{:S(2)}) %collective-permute-start.5) | collective-permute-done | bytes 163872 | tf_op jit(solution)/shard_map/ppermute | solution.py:48
  35.1 2.6 %shard_map.114 = (bf16[8,8,48,512]{3,2,1,0:T(8,128)(2,1)}, bf16[8,32,512]{2,1,0:T(8,128)(2,1)S(1)}) custom-call(bf16[128,384]{1,0:T(8,128)(2,1)S(1)} %get-tuple-element.26.sel, bf16[160,512]{1,0:T(8,128)(2,1)S(1)} %get-tuple-element.27.refs_0_, bf16[160,512]{1,0:T(8,128)(2,1)S(1)} %collective-permute-done.refs_1_, ...), custom_call_target="tpu_custom_call" | custom-call | tf_op jit(solution)/shard_map/pallas_call | solution.py:175
  38.4 7.0 %all-to-all-start.1 = ((bf16[8,8,48,512]{3,2,1,0:T(8,128)(2,1)}), bf16[8,8,48,512]{3,2,1,0:T(8,128)(2,1)}, u32[]{:S(2)}, u32[]{:S(2)}) async-start(bf16[8,8,48,512]{3,2,1,0:T(8,128)(2,1)} %get-tuple-element.35), calls=%async_computation.1 | async-start | bytes 6291456 | tf_op jit(solution)/shard_map/all_to_all | solution.py:39
  45.5 3.3 %collective-permute-start.9 = (bf16[8,96,512]{2,1,0:T(8,128)(2,1)S(1)}, bf16[8,96,512]{2,1,0:T(8,128)(2,1)S(1)}, u32[]{:S(2)}, u32[]{:S(2)}) collective-permute-start(bf16[8,96,512]{2,1,0:T(8,128)(2,1)S(1)} %slice.9.refs_7_), channel_id=1, source_target_pairs={{0,6},{1,7},{2,0},{3,1},{4,2},{5,3},{6,4},{7,5},{8,14},{9,15},{10,... | collective-permute-start | bytes 2359304 | tf_op jit(solution)/shard_map/ppermute | solution.py:48
  50.1 15.7 %collective-permute-done.9.refs_11_ = bf16[8,96,512]{2,1,0:T(8,128)(2,1)S(1)} collective-permute-done((bf16[8,96,512]{2,1,0:T(8,128)(2,1)S(1)}, bf16[8,96,512]{2,1,0:T(8,128)(2,1)S(1)}, u32[]{:S(2)}, u32[]{:S(2)}) %collective-permute-start.9) | collective-permute-done | bytes 786464 | tf_op jit(solution)/shard_map/ppermute | solution.py:48
  65.8 3.2 %collective-permute-done.8.refs_9_ = bf16[8,96,512]{2,1,0:T(8,128)(2,1)S(1)} collective-permute-done((bf16[8,96,512]{2,1,0:T(8,128)(2,1)S(1)}, bf16[8,96,512]{2,1,0:T(8,128)(2,1)S(1)}, u32[]{:S(2)}, u32[]{:S(2)}) %collective-permute-start.8) | collective-permute-done | bytes 786464 | tf_op jit(solution)/shard_map/ppermute | solution.py:48
  71.8 15.4 %collective-permute-done.11.refs_12_ = bf16[8,96,512]{2,1,0:T(8,128)(2,1)} collective-permute-done((bf16[8,96,512]{2,1,0:T(8,128)(2,1)S(1)}, bf16[8,96,512]{2,1,0:T(8,128)(2,1)}, u32[]{:S(2)}, u32[]{:S(2)}) %collective-permute-start.11) | collective-permute-done | bytes 786464 | tf_op jit(solution)/shard_map/ppermute | solution.py:48
  89.0 2.7 %collective-permute-start.13 = (bf16[8,96,512]{2,1,0:T(8,128)(2,1)}, bf16[8,96,512]{2,1,0:T(8,128)(2,1)S(1)}, u32[]{:S(2)}, u32[]{:S(2)}) collective-permute-start(bf16[8,96,512]{2,1,0:T(8,128)(2,1)} %collective-permute-done.11.refs_12_), channel_id=1, source_target_pairs={{0,6},{1,7},{2,0},{3,1},{4,2},{5,3},{6,4},{7,5},{8,14},{9,15},{10,... | collective-permute-start | bytes 2359304 | tf_op jit(solution)/shard_map/ppermute | solution.py:48
  91.7 20.1 %shard_map.115 = bf16[8,8,48,512]{3,2,1,0:T(8,128)(2,1)} custom-call(s32[8]{0:T(128)} %stack.35.order.refs_0_, s32[1]{0:T(128)} %bitcast.15.own.refs_1_, bf16[8,8,48,512]{3,2,1,0:T(8,128)(2,1)} %all-to-all-done.1.moved_in, bf16[8,96,128]{2,1,0:T(8,128)(2,1)} %slice.8.other.refs_2_, bf16[8,32,512]{2,1,0:T(8,128)(2,1)} %copy-done.11, ...), custom_call_target="tpu_custom_call" | custom-call | flops 8455716864 | bytes 28311552 | tf_op jit(solution)/shard_map/pallas_call | solution.py:346
  113.6 8.6 %all-to-all-start.3 = ((bf16[64,48,512]{2,1,0:T(8,128)(2,1)}), bf16[64,48,512]{2,1,0:T(8,128)(2,1)S(1)}, u32[]{:S(2)}, u32[]{:S(2)}) async-start(bf16[64,48,512]{2,1,0:T(8,128)(2,1)} %bitcast.37), calls=%async_computation.3 | async-start | bytes 6291456 | tf_op jit(solution)/shard_map/all_to_all | solution.py:39
  122.2 29.9 %shard_map.116 = bf16[8,8,48,512]{3,2,1,0:T(8,128)(2,1)} custom-call(s32[8]{0:T(128)} %stack.35.order.refs_0_, s32[1]{0:T(128)} %bitcast.15.own.refs_1_, bf16[8,96,128]{2,1,0:T(8,128)(2,1)} %slice.8.other.refs_2_, bf16[8,32,512]{2,1,0:T(8,128)(2,1)} %copy-done.11, bf16[4096,896]{1,0:T(8,128)(2,1)} %bitcast.40, bf16[4096,896]{1,0:T(8,128)(2,1)} %bitcast.42, ...), custom_call_target="tpu_custom_call" | custom-call | flops 14092861440 | bytes 31457280 | tf_op jit(solution)/shard_map/pallas_call | solution.py:464
  152.1 10.3 %all-to-all-done.3 = bf16[64,48,512]{2,1,0:T(8,128)(2,1)S(1)} async-done(((bf16[64,48,512]{2,1,0:T(8,128)(2,1)}), bf16[64,48,512]{2,1,0:T(8,128)(2,1)S(1)}, u32[]{:S(2)}, u32[]{:S(2)}) %all-to-all-start.3) | async-done | bytes 3145760 | tf_op jit(solution)/shard_map/all_to_all | solution.py:39
  162.3 7.2 %all-to-all-start.2 = ((bf16[64,48,512]{2,1,0:T(8,128)(2,1)}), bf16[64,48,512]{2,1,0:T(8,128)(2,1)}, u32[]{:S(2)}, u32[]{:S(2)}) async-start(bf16[64,48,512]{2,1,0:T(8,128)(2,1)} %bitcast.36), calls=%async_computation.2 | async-start | bytes 6291456 | tf_op jit(solution)/shard_map/all_to_all | solution.py:39
  171.2 38.4 %all-to-all-done.2 = bf16[64,48,512]{2,1,0:T(8,128)(2,1)} async-done(((bf16[64,48,512]{2,1,0:T(8,128)(2,1)}), bf16[64,48,512]{2,1,0:T(8,128)(2,1)}, u32[]{:S(2)}, u32[]{:S(2)}) %all-to-all-start.2) | async-done | bytes 3145760 | tf_op jit(solution)/shard_map/all_to_all | solution.py:39
  210.5 2.6 %shard_map.117 = bf16[128,512]{1,0:T(8,128)(2,1)S(1)} custom-call(bf16[128,384]{1,0:T(8,128)(2,1)S(1)} %copy-done.8, bf16[8,8,48,512]{3,2,1,0:T(8,128)(2,1)} %bitcast.20.home, bf16[128,512]{1,0:T(8,128)(2,1)S(1)} %bitcast.31), custom_call_target="tpu_custom_call" | custom-call | tf_op jit(solution)/shard_map/pallas_call | solution.py:505
  213.8 2.6 %collective-permute-start.14 = (bf16[128,512]{1,0:T(8,128)(2,1)S(1)}, bf16[128,512]{1,0:T(8,128)(2,1)S(1)}, u32[]{:S(2)}, u32[]{:S(2)}) collective-permute-start(bf16[128,512]{1,0:T(8,128)(2,1)S(1)} %get-tuple-element.46), channel_id=1, source_target_pairs={{0,64},{64,0},{1,65},{65,1},{2,66},{66,2},{3,67},{67,3},{4,68},{68... | collective-permute-start | bytes 393224 | tf_op jit(solution)/shard_map/ppermute | solution.py:35
  216.4 4.1 %collective-permute-done.14 = bf16[128,512]{1,0:T(8,128)(2,1)S(1)} collective-permute-done((bf16[128,512]{1,0:T(8,128)(2,1)S(1)}, bf16[128,512]{1,0:T(8,128)(2,1)S(1)}, u32[]{:S(2)}, u32[]{:S(2)}) %collective-permute-start.14) | collective-permute-done | bytes 131104 | tf_op jit(solution)/shard_map/ppermute | solution.py:35
  (63 shorter events, 21.5 us)
Async XLA Ops:
  9.2 29.2 %copy-start.4 = (bf16[128,384]{1,0:T(8,128)(2,1)}, bf16[128,384]{1,0:T(8,128)(2,1)S(1)}, u32[]{:S(2)}) copy-start(bf16[128,384]{1,0:T(8,128)(2,1)S(1)} %get-tuple-element.26.sel) | copy-start | bytes 294916
  9.2 29.2 %all-to-all-start = ((bf16[8,96,640]{2,1,0:T(8,128)(2,1)}), bf16[8,96,640]{2,1,0:T(8,128)(2,1)S(1)}, u32[]{:S(2)}, u32[]{:S(2)}) async-start(bf16[8,96,640]{2,1,0:T(8,128)(2,1)} %get-tuple-element.25), calls=%async_computation | async-start | bytes 1966080 | tf_op jit(solution)/shard_map/all_to_all | solution.py:39
  16.0 6.1 %collective-permute-start.2 = (bf16[160,512]{1,0:T(8,128)(2,1)S(1)}, bf16[160,512]{1,0:T(8,128)(2,1)S(1)}, u32[]{:S(2)}, u32[]{:S(2)}) collective-permute-start(bf16[160,512]{1,0:T(8,128)(2,1)S(1)} %get-tuple-element.27.refs_0_), channel_id=1, source_target_pairs={{0,6},{1,7},{2,0},{3,1},{4,2},{5,3},{6,4},{7,5},{8,14},{9,15},{10,... | collective-permute-start | bytes 491528 | tf_op jit(solution)/shard_map/ppermute | solution.py:48
  18.5 6.7 %collective-permute-start.1 = (bf16[160,512]{1,0:T(8,128)(2,1)S(1)}, bf16[160,512]{1,0:T(8,128)(2,1)S(1)}, u32[]{:S(2)}, u32[]{:S(2)}) collective-permute-start(bf16[160,512]{1,0:T(8,128)(2,1)S(1)} %get-tuple-element.27.refs_0_), channel_id=1, source_target_pairs={{0,2},{1,3},{2,4},{3,5},{4,6},{5,7},{6,0},{7,1},{8,10},{9,11},{10,... | collective-permute-start | bytes 491528 | tf_op jit(solution)/shard_map/ppermute | solution.py:48
  18.5 6.7 %collective-permute-start = (bf16[160,512]{1,0:T(8,128)(2,1)S(1)}, bf16[160,512]{1,0:T(8,128)(2,1)S(1)}, u32[]{:S(2)}, u32[]{:S(2)}) collective-permute-start(bf16[160,512]{1,0:T(8,128)(2,1)S(1)} %get-tuple-element.27.refs_0_), channel_id=1, source_target_pairs={{0,1},{1,0},{2,3},{3,2},{4,5},{5,4},{6,7},{7,6},{8,9},{9,8},{10,11... | collective-permute-start | bytes 491528 | tf_op jit(solution)/shard_map/ppermute | solution.py:48
  25.2 4.6 %collective-permute-start.4 = (bf16[160,512]{1,0:T(8,128)(2,1)S(1)}, bf16[160,512]{1,0:T(8,128)(2,1)S(1)}, u32[]{:S(2)}, u32[]{:S(2)}) collective-permute-start(bf16[160,512]{1,0:T(8,128)(2,1)S(1)} %collective-permute-done.refs_1_), channel_id=1, source_target_pairs={{0,6},{1,7},{2,0},{3,1},{4,2},{5,3},{6,4},{7,5},{8,14},{9,15},{10,... | collective-permute-start | bytes 491528 | tf_op jit(solution)/shard_map/ppermute | solution.py:48
  26.4 8.7 %collective-permute-start.3 = (bf16[160,512]{1,0:T(8,128)(2,1)S(1)}, bf16[160,512]{1,0:T(8,128)(2,1)S(1)}, u32[]{:S(2)}, u32[]{:S(2)}) collective-permute-start(bf16[160,512]{1,0:T(8,128)(2,1)S(1)} %collective-permute-done.refs_1_), channel_id=1, source_target_pairs={{0,2},{1,3},{2,4},{3,5},{4,6},{5,7},{6,0},{7,1},{8,10},{9,11},{10,... | collective-permute-start | bytes 491528 | tf_op jit(solution)/shard_map/ppermute | solution.py:48
  26.7 8.4 %collective-permute-start.5 = (bf16[160,512]{1,0:T(8,128)(2,1)S(1)}, bf16[160,512]{1,0:T(8,128)(2,1)S(1)}, u32[]{:S(2)}, u32[]{:S(2)}) collective-permute-start(bf16[160,512]{1,0:T(8,128)(2,1)S(1)} %collective-permute-done.1.refs_2_), channel_id=1, source_target_pairs={{0,2},{1,3},{2,4},{3,5},{4,6},{5,7},{6,0},{7,1},{8,10},{9,11},{10,... | collective-permute-start | bytes 491528 | tf_op jit(solution)/shard_map/ppermute | solution.py:48
  29.8 5.3 %collective-permute-start.6 = (bf16[160,512]{1,0:T(8,128)(2,1)S(1)}, bf16[160,512]{1,0:T(8,128)(2,1)S(1)}, u32[]{:S(2)}, u32[]{:S(2)}) collective-permute-start(bf16[160,512]{1,0:T(8,128)(2,1)S(1)} %collective-permute-done.4.refs_5_), channel_id=1, source_target_pairs={{0,6},{1,7},{2,0},{3,1},{4,2},{5,3},{6,4},{7,5},{8,14},{9,15},{10,... | collective-permute-start | bytes 491528 | tf_op jit(solution)/shard_map/ppermute | solution.py:48
  38.4 50.6 %all-to-all-start.1 = ((bf16[8,8,48,512]{3,2,1,0:T(8,128)(2,1)}), bf16[8,8,48,512]{3,2,1,0:T(8,128)(2,1)}, u32[]{:S(2)}, u32[]{:S(2)}) async-start(bf16[8,8,48,512]{3,2,1,0:T(8,128)(2,1)} %get-tuple-element.35), calls=%async_computation.1 | async-start | bytes 6291456 | tf_op jit(solution)/shard_map/all_to_all | solution.py:39
  45.5 20.3 %collective-permute-start.9 = (bf16[8,96,512]{2,1,0:T(8,128)(2,1)S(1)}, bf16[8,96,512]{2,1,0:T(8,128)(2,1)S(1)}, u32[]{:S(2)}, u32[]{:S(2)}) collective-permute-start(bf16[8,96,512]{2,1,0:T(8,128)(2,1)S(1)} %slice.9.refs_7_), channel_id=1, source_target_pairs={{0,6},{1,7},{2,0},{3,1},{4,2},{5,3},{6,4},{7,5},{8,14},{9,15},{10,... | collective-permute-start | bytes 2359304 | tf_op jit(solution)/shard_map/ppermute | solution.py:48
  48.8 20.2 %collective-permute-start.8 = (bf16[8,96,512]{2,1,0:T(8,128)(2,1)S(1)}, bf16[8,96,512]{2,1,0:T(8,128)(2,1)S(1)}, u32[]{:S(2)}, u32[]{:S(2)}) collective-permute-start(bf16[8,96,512]{2,1,0:T(8,128)(2,1)S(1)} %slice.9.refs_7_), channel_id=1, source_target_pairs={{0,2},{1,3},{2,4},{3,5},{4,6},{5,7},{6,0},{7,1},{8,10},{9,11},{10,... | collective-permute-start | bytes 2359304 | tf_op jit(solution)/shard_map/ppermute | solution.py:48
  48.8 20.2 %collective-permute-start.7 = (bf16[8,96,512]{2,1,0:T(8,128)(2,1)S(1)}, bf16[8,96,512]{2,1,0:T(8,128)(2,1)S(1)}, u32[]{:S(2)}, u32[]{:S(2)}) collective-permute-start(bf16[8,96,512]{2,1,0:T(8,128)(2,1)S(1)} %slice.9.refs_7_), channel_id=1, source_target_pairs={{0,1},{1,0},{2,3},{3,2},{4,5},{5,4},{6,7},{7,6},{8,9},{9,8},{10,11... | collective-permute-start | bytes 2359304 | tf_op jit(solution)/shard_map/ppermute | solution.py:48
  69.0 42.8 %copy-start.14 = (bf16[8,96,512]{2,1,0:T(8,128)(2,1)}, bf16[8,96,512]{2,1,0:T(8,128)(2,1)S(1)}, u32[]{:S(2)}) copy-start(bf16[8,96,512]{2,1,0:T(8,128)(2,1)S(1)} %collective-permute-done.8.refs_9_) | copy-start | bytes 2359300
  69.0 42.8 %copy-start.15 = (bf16[8,96,512]{2,1,0:T(8,128)(2,1)}, bf16[8,96,512]{2,1,0:T(8,128)(2,1)S(1)}, u32[]{:S(2)}) copy-start(bf16[8,96,512]{2,1,0:T(8,128)(2,1)S(1)} %collective-permute-done.7.refs_8_) | copy-start | bytes 2359300
  69.0 18.2 %collective-permute-start.11 = (bf16[8,96,512]{2,1,0:T(8,128)(2,1)S(1)}, bf16[8,96,512]{2,1,0:T(8,128)(2,1)}, u32[]{:S(2)}, u32[]{:S(2)}) collective-permute-start(bf16[8,96,512]{2,1,0:T(8,128)(2,1)S(1)} %collective-permute-done.7.refs_8_), channel_id=1, source_target_pairs={{0,6},{1,7},{2,0},{3,1},{4,2},{5,3},{6,4},{7,5},{8,14},{9,15},{10,... | collective-permute-start | bytes 2359304 | tf_op jit(solution)/shard_map/ppermute | solution.py:48
  70.2 18.8 %collective-permute-start.10 = (bf16[8,96,512]{2,1,0:T(8,128)(2,1)S(1)}, bf16[8,96,512]{2,1,0:T(8,128)(2,1)}, u32[]{:S(2)}, u32[]{:S(2)}) collective-permute-start(bf16[8,96,512]{2,1,0:T(8,128)(2,1)S(1)} %collective-permute-done.7.refs_8_), channel_id=1, source_target_pairs={{0,2},{1,3},{2,4},{3,5},{4,6},{5,7},{6,0},{7,1},{8,10},{9,11},{10,... | collective-permute-start | bytes 2359304 | tf_op jit(solution)/shard_map/ppermute | solution.py:48
  89.0 22.8 %collective-permute-start.12 = (bf16[8,96,512]{2,1,0:T(8,128)(2,1)S(1)}, bf16[8,96,512]{2,1,0:T(8,128)(2,1)S(1)}, u32[]{:S(2)}, u32[]{:S(2)}) collective-permute-start(bf16[8,96,512]{2,1,0:T(8,128)(2,1)S(1)} %collective-permute-done.8.refs_9_), channel_id=1, source_target_pairs={{0,2},{1,3},{2,4},{3,5},{4,6},{5,7},{6,0},{7,1},{8,10},{9,11},{10,... | collective-permute-start | bytes 2359304 | tf_op jit(solution)/shard_map/ppermute | solution.py:48
  89.0 23.7 %collective-permute-start.13 = (bf16[8,96,512]{2,1,0:T(8,128)(2,1)}, bf16[8,96,512]{2,1,0:T(8,128)(2,1)S(1)}, u32[]{:S(2)}, u32[]{:S(2)}) collective-permute-start(bf16[8,96,512]{2,1,0:T(8,128)(2,1)} %collective-permute-done.11.refs_12_), channel_id=1, source_target_pairs={{0,6},{1,7},{2,0},{3,1},{4,2},{5,3},{6,4},{7,5},{8,14},{9,15},{10,... | collective-permute-start | bytes 2359304 | tf_op jit(solution)/shard_map/ppermute | solution.py:48
  113.6 48.7 %all-to-all-start.3 = ((bf16[64,48,512]{2,1,0:T(8,128)(2,1)}), bf16[64,48,512]{2,1,0:T(8,128)(2,1)S(1)}, u32[]{:S(2)}, u32[]{:S(2)}) async-start(bf16[64,48,512]{2,1,0:T(8,128)(2,1)} %bitcast.37), calls=%async_computation.3 | async-start | bytes 6291456 | tf_op jit(solution)/shard_map/all_to_all | solution.py:39
  162.3 7.2 %copy-start.1 = (bf16[1,128,512]{2,1,0:T(8,128)(2,1)S(1)}, bf16[1,128,512]{2,1,0:T(8,128)(2,1)}, u32[]{:S(2)}) copy-start(bf16[1,128,512]{2,1,0:T(8,128)(2,1)} %param.12) | copy-start | bytes 393220
  162.3 47.3 %all-to-all-start.2 = ((bf16[64,48,512]{2,1,0:T(8,128)(2,1)}), bf16[64,48,512]{2,1,0:T(8,128)(2,1)}, u32[]{:S(2)}, u32[]{:S(2)}) async-start(bf16[64,48,512]{2,1,0:T(8,128)(2,1)} %bitcast.36), calls=%async_computation.2 | async-start | bytes 6291456 | tf_op jit(solution)/shard_map/all_to_all | solution.py:39
  169.5 40.1 %copy-start.3 = (bf16[1,128,512]{2,1,0:T(8,128)(2,1)S(1)}, bf16[1,128,512]{2,1,0:T(8,128)(2,1)}, u32[]{:S(2)}) copy-start(bf16[1,128,512]{2,1,0:T(8,128)(2,1)} %param.11) | copy-start | bytes 393220
  213.8 6.7 %collective-permute-start.14 = (bf16[128,512]{1,0:T(8,128)(2,1)S(1)}, bf16[128,512]{1,0:T(8,128)(2,1)S(1)}, u32[]{:S(2)}, u32[]{:S(2)}) collective-permute-start(bf16[128,512]{1,0:T(8,128)(2,1)S(1)} %get-tuple-element.46), channel_id=1, source_target_pairs={{0,64},{64,0},{1,65},{65,1},{2,66},{66,2},{3,67},{67,3},{4,68},{68... | collective-permute-start | bytes 393224 | tf_op jit(solution)/shard_map/ppermute | solution.py:35
  (13 other events, 15.6 us)

commit v3 on v2

--- a/solution.py
+++ b/solution.py
@@ -16,6 +16,7 @@
 GROUPS = 8
 TABLE = 32
 LIMIT = 56 * 1024 * 1024
+MOST = 60 * 1024 * 1024
 VMEM = pl.BlockSpec(memory_space=pltpu.VMEM)
 SMEM = pl.BlockSpec(memory_space=pltpu.SMEM)
 PLACE = pl.BlockSpec(memory_space=pl.ANY)
@@ -48,21 +49,16 @@
     return lax.ppermute(block, "hid", route)
 
 
-def gather_near(block):
+def gather_near(block, after=()):
     other = shift(block, 0, 1)
     right, left = shift(block, 1, 0), shift(block, -1, 0)
-    other, right, left = lax.optimization_barrier((other, right, left))
+    other, right, left, after = lax.optimization_barrier((other, right, left, after))
     right_other, left_other = shift(other, 1, 0), shift(other, -1, 0)
-    return [block, other, right, right_other, left, left_other]
+    return [block, other, right, right_other, left, left_other], after
 
 
 def gather_far(near):
     return [shift(near[2], 1, 0), shift(near[5], -1, 0)]
-
-
-def gather_groups(block):
-    near = gather_near(block)
-    return near + gather_far(near)
 
 
 def arrival_order():
@@ -88,10 +84,8 @@
     return pl.BlockSpec(shape, lambda i: (0,) * len(shape))
 
 
-def pack_kernel(
-    capacity, routes_s, routes_n, saved, cot, upcoming, gain, router, packed, tokens_out, sel_s, sel_n
-):
-    tokens, part = saved.shape
+def table_kernel(upcoming, gain, router, tokens_out):
+    tokens, part = upcoming.shape
     experts = router.shape[0]
     tokens_out[0:tokens, :] = upcoming[...]
     gains = gain[...]
@@ -101,6 +95,22 @@
     rows.append(jnp.zeros((TABLE - 3 * experts - 3, part), jnp.float32))
     tokens_out[tokens : tokens + TABLE, :] = jnp.concatenate(rows, axis=0).astype(jnp.bfloat16)
 
+
+def with_table(upcoming, gain, router):
+    tokens, part = upcoming.shape
+    shape = (tokens + TABLE, part)
+    return pl.pallas_call(
+        table_kernel,
+        out_shape=jax.ShapeDtypeStruct(shape, jnp.bfloat16),
+        grid=(1,),
+        in_specs=[whole(a.shape) for a in (upcoming, gain, router)],
+        out_specs=whole(shape),
+        compiler_params=pltpu.CompilerParams(vmem_limit_bytes=MOST),
+    )(upcoming, gain, router)
+
+
+def pack_kernel(experts, capacity, routes_s, routes_n, saved, cot, packed, sel_s, sel_n):
+    tokens, part = saved.shape
     row = lax.broadcasted_iota(jnp.int32, (tokens, tokens), 0)
     lane = lax.broadcasted_iota(jnp.int32, (tokens, tokens), 1)
     earlier = jnp.where(lane < row, 1.0, 0.0).astype(jnp.bfloat16)
@@ -139,24 +149,18 @@
     put(capacity, part, 128, other)
 
 
-def pack(routes_s, routes_n, saved, cot, upcoming, gain, router, capacity):
+def pack(routes_s, routes_n, saved, cot, experts, capacity):
     tokens, part = saved.shape
-    experts = router.shape[0]
     total = experts * capacity
-    shapes = [
-        (experts, 2 * capacity, part + 128),
-        (tokens + TABLE, part),
-        (tokens, total),
-        (tokens, total),
-    ]
+    shapes = [(experts, 2 * capacity, part + 128), (tokens, total), (tokens, total)]
     return pl.pallas_call(
-        functools.partial(pack_kernel, capacity),
+        functools.partial(pack_kernel, experts, capacity),
         out_shape=[jax.ShapeDtypeStruct(s, jnp.bfloat16) for s in shapes],
         grid=(1,),
-        in_specs=[whole(a.shape) for a in (routes_s, routes_n, saved, cot, upcoming, gain, router)],
+        in_specs=[whole(a.shape) for a in (routes_s, routes_n, saved, cot)],
         out_specs=[whole(s) for s in shapes],
-        compiler_params=pltpu.CompilerParams(vmem_limit_bytes=LIMIT // 2),
-    )(routes_s, routes_n, saved, cot, upcoming, gain, router)
+        compiler_params=pltpu.CompilerParams(vmem_limit_bytes=MOST),
+    )(routes_s, routes_n, saved, cot)
 
 
 def spread_kernel(sel, *refs):
@@ -536,22 +540,15 @@
     own = lax.axis_index("expert").astype(jnp.int32).reshape(1)
     order = arrival_order()
 
-    packed, tokens_next, sel_saved, sel_next = pack(
-        routes_saved[0],
-        routes_next[0],
-        saved_input[0],
-        cotangent[0],
-        next_input[0],
-        norm_gain,
-        router[0].T,
-        capacity,
-    )
+    tokens_next = with_table(next_input[0], norm_gain, router[0].T)
+    tokens_next, routes = lax.optimization_barrier((tokens_next, (routes_saved[0], routes_next[0])))
+    packed, sel_saved, sel_next = pack(*routes, saved_input[0], cotangent[0], experts, capacity)
+    near, packed = gather_near(tokens_next, packed)
     packed = swap(packed, "expert")
-    moved_next, table = spread(sel_next, gather_groups(tokens_next), experts)
+    moved_next, table = spread(sel_next, near + gather_far(near), experts)
     moved_next = swap(moved_next, "expert")
     other = packed[:, :, part:]
-    near = gather_near(packed[:, :, :part])
-
+    near, _ = gather_near(packed[:, :, :part])
     near, moved_next = lax.optimization_barrier((near, moved_next))
     far = gather_far(near)
     out_next = forward(order, own, moved_next, other, table, gate_w, up_w, down_w)

time: 222 us -> 221 us (level)
  Pallas kernels: 58.1 us -> 60.8 us
  waiting for transfers between devices: 100 us -> 97.6 us
    ppermute x14, waiting for transfers between devices: 47.6 us -> 44.9 us  [shift(): return lax.ppermute(block, 'hid', route)]
    pallas_call x1 -> x2, Pallas kernels: 2.24 us -> 4.88 us  [the longest x1 3.26 us: pack(): pl.pallas_call(functools.partial(pack_kernel, experts, capacity), out_sha...]
    unnamed x39 -> x29, local copies, waits for them, and re-layouts: 11.3 us -> 9.65 us
  transfers between devices with their start and end apart: 19 -> 19, of which waited for: 11 -> 10; matrix products, arithmetic and copies ran while one was open for 1% -> 1% of each run, Pallas kernels for 24% -> 26%
where the time goes in v3:
time: 221 us; the launch traced here: 220 us
  waiting for transfers between devices  97.6 us (44%)
  Pallas kernels  60.8 us (28%)
  starting transfers between devices  49.2 us (22%)
  local copies, waits for them, and re-layouts  11 us (5%)
    all_to_all x4, waiting for transfers between devices, swap(): return lax.all_to_all(block, axes, split_axis=0, concat_axis=0, tiled=True)  48.7 us
    ppermute x14, waiting for transfers between devices, shift(): return lax.ppermute(block, 'hid', route)  44.9 us
    pallas_call x1, Pallas kernels, backward(): pl.pallas_call(backward_kernel, out_shape=jax.ShapeDtypeStruct((blocks, G...  29.9 us
    all_to_all x4, starting transfers between devices, swap(): return lax.all_to_all(block, axes, split_axis=0, concat_axis=0, tiled=True)  28.8 us
    pallas_call x1, Pallas kernels, forward(): pl.pallas_call(forward_kernel, out_shape=jax.ShapeDtypeStruct(moved.shape...  20.1 us
    ppermute x14, starting transfers between devices, shift(): return lax.ppermute(block, 'hid', route)  17.8 us
    unnamed x29, local copies, waits for them, and re-layouts  9.65 us
  transfers between devices with their start and end apart: 19, of which 10 were waited for; matrix products, arithmetic and copies ran while one was open for 1% of the time, Pallas kernels for 26%

profile of v3, /device:TPU:1, one launch (start us, length us, event | category | flops | bytes accessed | tf_op | source)
XLA Modules:
  0.0 220.1 jit_solution(18336223105752613149)
XLA Ops:
  3.5 1.6 shard_map.113.refs_0_
  5.1 3.3 %collective-permute-start.2 = (bf16[160,512]{1,0:T(8,128)(2,1)}, bf16[160,512]{1,0:T(8,128)(2,1)S(1)}, u32[]{:S(2)}, u32[]{:S(2)}) collective-permute-start(bf16[160,512]{1,0:T(8,128)(2,1)} %shard_map.113.refs_0_), channel_id=1, source_target_pairs={{0,6},{1,7},{2,0},{3,1},{4,2},{5,3},{6,4},{7,5},{8,14},{9,15},{10,... | collective-permute-start | bytes 491528 | tf_op jit(solution)/shard_map/ppermute | solution.py:49
  9.7 3.3 %shard_map.114 = (bf16[8,96,640]{2,1,0:T(8,128)(2,1)}, bf16[128,384]{1,0:T(8,128)(2,1)}, bf16[128,384]{1,0:T(8,128)(2,1)}) custom-call(s32[128,2]{1,0:T(8,128)} %bitcast.34, s32[128,2]{1,0:T(8,128)} %bitcast.35, bf16[128,512]{1,0:T(8,128)(2,1)} %bitcast.36, bf16[128,512]{1,0:T(8,128)(2,1)} %bitcast.28), custom_call_target="tpu_custom_call" | custom-call | tf_op jit(solution)/shard_map/pallas_call | solution.py:156
  14.6 7.2 %all-to-all-start = ((bf16[8,96,640]{2,1,0:T(8,128)(2,1)}), bf16[8,96,640]{2,1,0:T(8,128)(2,1)S(1)}, u32[]{:S(2)}, u32[]{:S(2)}) async-start(bf16[8,96,640]{2,1,0:T(8,128)(2,1)} %get-tuple-element.32), calls=%async_computation | async-start | bytes 1966080 | tf_op jit(solution)/shard_map/all_to_all | solution.py:40
  23.2 4.3 %collective-permute-done.4.refs_5_ = bf16[160,512]{1,0:T(8,128)(2,1)S(1)} collective-permute-done((bf16[160,512]{1,0:T(8,128)(2,1)S(1)}, bf16[160,512]{1,0:T(8,128)(2,1)S(1)}, u32[]{:S(2)}, u32[]{:S(2)}) %collective-permute-start.4) | collective-permute-done | bytes 163872 | tf_op jit(solution)/shard_map/ppermute | solution.py:49
  27.6 2.7 %collective-permute-start.6 = (bf16[160,512]{1,0:T(8,128)(2,1)S(1)}, bf16[160,512]{1,0:T(8,128)(2,1)S(1)}, u32[]{:S(2)}, u32[]{:S(2)}) collective-permute-start(bf16[160,512]{1,0:T(8,128)(2,1)S(1)} %collective-permute-done.4.refs_5_), channel_id=1, source_target_pairs={{0,6},{1,7},{2,0},{3,1},{4,2},{5,3},{6,4},{7,5},{8,14},{9,15},{10,... | collective-permute-start | bytes 491528 | tf_op jit(solution)/shard_map/ppermute | solution.py:49
  30.2 3.2 %collective-permute-done.5.refs_6_ = bf16[160,512]{1,0:T(8,128)(2,1)S(1)} collective-permute-done((bf16[160,512]{1,0:T(8,128)(2,1)S(1)}, bf16[160,512]{1,0:T(8,128)(2,1)S(1)}, u32[]{:S(2)}, u32[]{:S(2)}) %collective-permute-start.5) | collective-permute-done | bytes 163872 | tf_op jit(solution)/shard_map/ppermute | solution.py:49
  35.2 2.6 %shard_map.115 = (bf16[8,8,48,512]{3,2,1,0:T(8,128)(2,1)}, bf16[8,32,512]{2,1,0:T(8,128)(2,1)S(1)}) custom-call(bf16[128,384]{1,0:T(8,128)(2,1)S(1)} %copy-done.3, bf16[160,512]{1,0:T(8,128)(2,1)S(1)} %copy-done, bf16[160,512]{1,0:T(8,128)(2,1)S(1)} %collective-permute-done.refs_1_, bf16[160,512]{1,0:T(8,128)(2,1)S(1)} %collective-permute-done.1.refs_2_, ...), custom_call_target="tpu_custom_call" | custom-call | tf_op jit(solution)/shard_map/pallas_call | solution.py:179
  38.6 5.6 %all-to-all-start.1 = ((bf16[8,8,48,512]{3,2,1,0:T(8,128)(2,1)}), bf16[8,8,48,512]{3,2,1,0:T(8,128)(2,1)}, u32[]{:S(2)}, u32[]{:S(2)}) async-start(bf16[8,8,48,512]{3,2,1,0:T(8,128)(2,1)} %get-tuple-element.41), calls=%async_computation.1 | async-start | bytes 6291456 | tf_op jit(solution)/shard_map/all_to_all | solution.py:40
  44.3 3.5 %collective-permute-start.9 = (bf16[8,96,512]{2,1,0:T(8,128)(2,1)S(1)}, bf16[8,96,512]{2,1,0:T(8,128)(2,1)S(1)}, u32[]{:S(2)}, u32[]{:S(2)}) collective-permute-start(bf16[8,96,512]{2,1,0:T(8,128)(2,1)S(1)} %slice.9.refs_7_), channel_id=1, source_target_pairs={{0,6},{1,7},{2,0},{3,1},{4,2},{5,3},{6,4},{7,5},{8,14},{9,15},{10,... | collective-permute-start | bytes 2359304 | tf_op jit(solution)/shard_map/ppermute | solution.py:49
  49.0 15.5 %collective-permute-done.9.refs_11_ = bf16[8,96,512]{2,1,0:T(8,128)(2,1)S(1)} collective-permute-done((bf16[8,96,512]{2,1,0:T(8,128)(2,1)S(1)}, bf16[8,96,512]{2,1,0:T(8,128)(2,1)S(1)}, u32[]{:S(2)}, u32[]{:S(2)}) %collective-permute-start.9) | collective-permute-done | bytes 786464 | tf_op jit(solution)/shard_map/ppermute | solution.py:49
  64.5 3.2 %collective-permute-done.8.refs_9_ = bf16[8,96,512]{2,1,0:T(8,128)(2,1)S(1)} collective-permute-done((bf16[8,96,512]{2,1,0:T(8,128)(2,1)S(1)}, bf16[8,96,512]{2,1,0:T(8,128)(2,1)S(1)}, u32[]{:S(2)}, u32[]{:S(2)}) %collective-permute-start.8) | collective-permute-done | bytes 786464 | tf_op jit(solution)/shard_map/ppermute | solution.py:49
  70.6 15.2 %collective-permute-done.11.refs_12_ = bf16[8,96,512]{2,1,0:T(8,128)(2,1)} collective-permute-done((bf16[8,96,512]{2,1,0:T(8,128)(2,1)S(1)}, bf16[8,96,512]{2,1,0:T(8,128)(2,1)}, u32[]{:S(2)}, u32[]{:S(2)}) %collective-permute-start.11) | collective-permute-done | bytes 786464 | tf_op jit(solution)/shard_map/ppermute | solution.py:49
  85.8 1.8 collective-permute-done.10.refs_10_
  87.6 2.7 %collective-permute-start.13 = (bf16[8,96,512]{2,1,0:T(8,128)(2,1)}, bf16[8,96,512]{2,1,0:T(8,128)(2,1)S(1)}, u32[]{:S(2)}, u32[]{:S(2)}) collective-permute-start(bf16[8,96,512]{2,1,0:T(8,128)(2,1)} %collective-permute-done.11.refs_12_), channel_id=1, source_target_pairs={{0,6},{1,7},{2,0},{3,1},{4,2},{5,3},{6,4},{7,5},{8,14},{9,15},{10,... | collective-permute-start | bytes 2359304 | tf_op jit(solution)/shard_map/ppermute | solution.py:49
  90.3 20.1 %shard_map.116 = bf16[8,8,48,512]{3,2,1,0:T(8,128)(2,1)} custom-call(s32[8]{0:T(128)} %stack.35.order.refs_0_, s32[1]{0:T(128)} %bitcast.15.own.refs_1_, bf16[8,8,48,512]{3,2,1,0:T(8,128)(2,1)} %all-to-all-done.1.moved_in, bf16[8,96,128]{2,1,0:T(8,128)(2,1)} %slice.8.other.refs_2_, bf16[8,32,512]{2,1,0:T(8,128)(2,1)} %copy-done.6, ...), custom_call_target="tpu_custom_call" | custom-call | flops 8455716864 | bytes 28311552 | tf_op jit(solution)/shard_map/pallas_call | solution.py:350
  112.2 8.9 %all-to-all-start.3 = ((bf16[64,48,512]{2,1,0:T(8,128)(2,1)}), bf16[64,48,512]{2,1,0:T(8,128)(2,1)S(1)}, u32[]{:S(2)}, u32[]{:S(2)}) async-start(bf16[64,48,512]{2,1,0:T(8,128)(2,1)} %bitcast.33), calls=%async_computation.3 | async-start | bytes 6291456 | tf_op jit(solution)/shard_map/all_to_all | solution.py:40
  121.1 29.9 %shard_map.117 = bf16[8,8,48,512]{3,2,1,0:T(8,128)(2,1)} custom-call(s32[8]{0:T(128)} %stack.35.order.refs_0_, s32[1]{0:T(128)} %bitcast.15.own.refs_1_, bf16[8,96,128]{2,1,0:T(8,128)(2,1)} %slice.8.other.refs_2_, bf16[8,32,512]{2,1,0:T(8,128)(2,1)} %copy-done.6, bf16[4096,896]{1,0:T(8,128)(2,1)} %bitcast.40, bf16[4096,896]{1,0:T(8,128)(2,1)} %bitcast.42, ...), custom_call_target="tpu_custom_call" | custom-call | flops 14092861440 | bytes 31457280 | tf_op jit(solution)/shard_map/pallas_call | solution.py:468
  151.0 10.2 %all-to-all-done.3 = bf16[64,48,512]{2,1,0:T(8,128)(2,1)S(1)} async-done(((bf16[64,48,512]{2,1,0:T(8,128)(2,1)}), bf16[64,48,512]{2,1,0:T(8,128)(2,1)S(1)}, u32[]{:S(2)}, u32[]{:S(2)}) %all-to-all-start.3) | async-done | bytes 3145760 | tf_op jit(solution)/shard_map/all_to_all | solution.py:40
  161.3 7.2 %all-to-all-start.2 = ((bf16[64,48,512]{2,1,0:T(8,128)(2,1)}), bf16[64,48,512]{2,1,0:T(8,128)(2,1)}, u32[]{:S(2)}, u32[]{:S(2)}) async-start(bf16[64,48,512]{2,1,0:T(8,128)(2,1)} %bitcast.32), calls=%async_computation.2 | async-start | bytes 6291456 | tf_op jit(solution)/shard_map/all_to_all | solution.py:40
  170.1 38.4 %all-to-all-done.2 = bf16[64,48,512]{2,1,0:T(8,128)(2,1)} async-done(((bf16[64,48,512]{2,1,0:T(8,128)(2,1)}), bf16[64,48,512]{2,1,0:T(8,128)(2,1)}, u32[]{:S(2)}, u32[]{:S(2)}) %all-to-all-start.2) | async-done | bytes 3145760 | tf_op jit(solution)/shard_map/all_to_all | solution.py:40
  209.4 2.6 %shard_map.118 = bf16[128,512]{1,0:T(8,128)(2,1)S(1)} custom-call(bf16[128,384]{1,0:T(8,128)(2,1)S(1)} %copy-done.5, bf16[8,8,48,512]{3,2,1,0:T(8,128)(2,1)} %bitcast.20.home, bf16[128,512]{1,0:T(8,128)(2,1)S(1)} %bitcast.29), custom_call_target="tpu_custom_call" | custom-call | tf_op jit(solution)/shard_map/pallas_call | solution.py:509
  212.7 2.6 %collective-permute-start.14 = (bf16[128,512]{1,0:T(8,128)(2,1)S(1)}, bf16[128,512]{1,0:T(8,128)(2,1)S(1)}, u32[]{:S(2)}, u32[]{:S(2)}) collective-permute-start(bf16[128,512]{1,0:T(8,128)(2,1)S(1)} %get-tuple-element.52), channel_id=1, source_target_pairs={{0,64},{64,0},{1,65},{65,1},{2,66},{66,2},{3,67},{67,3},{4,68},{68... | collective-permute-start | bytes 393224 | tf_op jit(solution)/shard_map/ppermute | solution.py:36
  215.4 4.1 %collective-permute-done.14 = bf16[128,512]{1,0:T(8,128)(2,1)S(1)} collective-permute-done((bf16[128,512]{1,0:T(8,128)(2,1)S(1)}, bf16[128,512]{1,0:T(8,128)(2,1)S(1)}, u32[]{:S(2)}, u32[]{:S(2)}) %collective-permute-start.14) | collective-permute-done | bytes 131104 | tf_op jit(solution)/shard_map/ppermute | solution.py:36
  (54 shorter events, 19.6 us)
Async XLA Ops:
  5.1 7.9 %collective-permute-start.2 = (bf16[160,512]{1,0:T(8,128)(2,1)}, bf16[160,512]{1,0:T(8,128)(2,1)S(1)}, u32[]{:S(2)}, u32[]{:S(2)}) collective-permute-start(bf16[160,512]{1,0:T(8,128)(2,1)} %shard_map.113.refs_0_), channel_id=1, source_target_pairs={{0,6},{1,7},{2,0},{3,1},{4,2},{5,3},{6,4},{7,5},{8,14},{9,15},{10,... | collective-permute-start | bytes 491528 | tf_op jit(solution)/shard_map/ppermute | solution.py:49
  8.4 6.2 %collective-permute-start.1 = (bf16[160,512]{1,0:T(8,128)(2,1)}, bf16[160,512]{1,0:T(8,128)(2,1)S(1)}, u32[]{:S(2)}, u32[]{:S(2)}) collective-permute-start(bf16[160,512]{1,0:T(8,128)(2,1)} %shard_map.113.refs_0_), channel_id=1, source_target_pairs={{0,2},{1,3},{2,4},{3,5},{4,6},{5,7},{6,0},{7,1},{8,10},{9,11},{10,... | collective-permute-start | bytes 491528 | tf_op jit(solution)/shard_map/ppermute | solution.py:49
  8.4 6.2 %collective-permute-start = (bf16[160,512]{1,0:T(8,128)(2,1)}, bf16[160,512]{1,0:T(8,128)(2,1)S(1)}, u32[]{:S(2)}, u32[]{:S(2)}) collective-permute-start(bf16[160,512]{1,0:T(8,128)(2,1)} %shard_map.113.refs_0_), channel_id=1, source_target_pairs={{0,1},{1,0},{2,3},{3,2},{4,5},{5,4},{6,7},{7,6},{8,9},{9,8},{10,11... | collective-permute-start | bytes 491528 | tf_op jit(solution)/shard_map/ppermute | solution.py:49
  14.6 24.1 %all-to-all-start = ((bf16[8,96,640]{2,1,0:T(8,128)(2,1)}), bf16[8,96,640]{2,1,0:T(8,128)(2,1)S(1)}, u32[]{:S(2)}, u32[]{:S(2)}) async-start(bf16[8,96,640]{2,1,0:T(8,128)(2,1)} %get-tuple-element.32), calls=%async_computation | async-start | bytes 1966080 | tf_op jit(solution)/shard_map/all_to_all | solution.py:40
  21.7 5.8 %collective-permute-start.4 = (bf16[160,512]{1,0:T(8,128)(2,1)S(1)}, bf16[160,512]{1,0:T(8,128)(2,1)S(1)}, u32[]{:S(2)}, u32[]{:S(2)}) collective-permute-start(bf16[160,512]{1,0:T(8,128)(2,1)S(1)} %collective-permute-done.refs_1_), channel_id=1, source_target_pairs={{0,6},{1,7},{2,0},{3,1},{4,2},{5,3},{6,4},{7,5},{8,14},{9,15},{10,... | collective-permute-start | bytes 491528 | tf_op jit(solution)/shard_map/ppermute | solution.py:49
  23.2 10.2 %collective-permute-start.3 = (bf16[160,512]{1,0:T(8,128)(2,1)S(1)}, bf16[160,512]{1,0:T(8,128)(2,1)S(1)}, u32[]{:S(2)}, u32[]{:S(2)}) collective-permute-start(bf16[160,512]{1,0:T(8,128)(2,1)S(1)} %collective-permute-done.refs_1_), channel_id=1, source_target_pairs={{0,2},{1,3},{2,4},{3,5},{4,6},{5,7},{6,0},{7,1},{8,10},{9,11},{10,... | collective-permute-start | bytes 491528 | tf_op jit(solution)/shard_map/ppermute | solution.py:49
  23.2 10.2 %collective-permute-start.5 = (bf16[160,512]{1,0:T(8,128)(2,1)S(1)}, bf16[160,512]{1,0:T(8,128)(2,1)S(1)}, u32[]{:S(2)}, u32[]{:S(2)}) collective-permute-start(bf16[160,512]{1,0:T(8,128)(2,1)S(1)} %collective-permute-done.1.refs_2_), channel_id=1, source_target_pairs={{0,2},{1,3},{2,4},{3,5},{4,6},{5,7},{6,0},{7,1},{8,10},{9,11},{10,... | collective-permute-start | bytes 491528 | tf_op jit(solution)/shard_map/ppermute | solution.py:49
  27.6 5.9 %collective-permute-start.6 = (bf16[160,512]{1,0:T(8,128)(2,1)S(1)}, bf16[160,512]{1,0:T(8,128)(2,1)S(1)}, u32[]{:S(2)}, u32[]{:S(2)}) collective-permute-start(bf16[160,512]{1,0:T(8,128)(2,1)S(1)} %collective-permute-done.4.refs_5_), channel_id=1, source_target_pairs={{0,6},{1,7},{2,0},{3,1},{4,2},{5,3},{6,4},{7,5},{8,14},{9,15},{10,... | collective-permute-start | bytes 491528 | tf_op jit(solution)/shard_map/ppermute | solution.py:49
  38.6 49.0 %all-to-all-start.1 = ((bf16[8,8,48,512]{3,2,1,0:T(8,128)(2,1)}), bf16[8,8,48,512]{3,2,1,0:T(8,128)(2,1)}, u32[]{:S(2)}, u32[]{:S(2)}) async-start(bf16[8,8,48,512]{3,2,1,0:T(8,128)(2,1)} %get-tuple-element.41), calls=%async_computation.1 | async-start | bytes 6291456 | tf_op jit(solution)/shard_map/all_to_all | solution.py:40
  44.2 3.5 %copy-start.7 = (bf16[8,96,512]{2,1,0:T(8,128)(2,1)}, bf16[8,96,512]{2,1,0:T(8,128)(2,1)S(1)}, u32[]{:S(2)}) copy-start(bf16[8,96,512]{2,1,0:T(8,128)(2,1)S(1)} %slice.9.refs_7_) | copy-start | bytes 2359300
  44.3 20.3 %collective-permute-start.9 = (bf16[8,96,512]{2,1,0:T(8,128)(2,1)S(1)}, bf16[8,96,512]{2,1,0:T(8,128)(2,1)S(1)}, u32[]{:S(2)}, u32[]{:S(2)}) collective-permute-start(bf16[8,96,512]{2,1,0:T(8,128)(2,1)S(1)} %slice.9.refs_7_), channel_id=1, source_target_pairs={{0,6},{1,7},{2,0},{3,1},{4,2},{5,3},{6,4},{7,5},{8,14},{9,15},{10,... | collective-permute-start | bytes 2359304 | tf_op jit(solution)/shard_map/ppermute | solution.py:49
  47.7 20.0 %collective-permute-start.8 = (bf16[8,96,512]{2,1,0:T(8,128)(2,1)S(1)}, bf16[8,96,512]{2,1,0:T(8,128)(2,1)S(1)}, u32[]{:S(2)}, u32[]{:S(2)}) collective-permute-start(bf16[8,96,512]{2,1,0:T(8,128)(2,1)S(1)} %slice.9.refs_7_), channel_id=1, source_target_pairs={{0,2},{1,3},{2,4},{3,5},{4,6},{5,7},{6,0},{7,1},{8,10},{9,11},{10,... | collective-permute-start | bytes 2359304 | tf_op jit(solution)/shard_map/ppermute | solution.py:49
  47.7 20.0 %collective-permute-start.7 = (bf16[8,96,512]{2,1,0:T(8,128)(2,1)S(1)}, bf16[8,96,512]{2,1,0:T(8,128)(2,1)S(1)}, u32[]{:S(2)}, u32[]{:S(2)}) collective-permute-start(bf16[8,96,512]{2,1,0:T(8,128)(2,1)S(1)} %slice.9.refs_7_), channel_id=1, source_target_pairs={{0,1},{1,0},{2,3},{3,2},{4,5},{5,4},{6,7},{7,6},{8,9},{9,8},{10,11... | collective-permute-start | bytes 2359304 | tf_op jit(solution)/shard_map/ppermute | solution.py:49
  67.7 42.7 %copy-start.9 = (bf16[8,96,512]{2,1,0:T(8,128)(2,1)}, bf16[8,96,512]{2,1,0:T(8,128)(2,1)S(1)}, u32[]{:S(2)}) copy-start(bf16[8,96,512]{2,1,0:T(8,128)(2,1)S(1)} %collective-permute-done.8.refs_9_) | copy-start | bytes 2359300
  67.7 42.7 %copy-start.10 = (bf16[8,96,512]{2,1,0:T(8,128)(2,1)}, bf16[8,96,512]{2,1,0:T(8,128)(2,1)S(1)}, u32[]{:S(2)}) copy-start(bf16[8,96,512]{2,1,0:T(8,128)(2,1)S(1)} %collective-permute-done.7.refs_8_) | copy-start | bytes 2359300
  67.8 18.0 %collective-permute-start.11 = (bf16[8,96,512]{2,1,0:T(8,128)(2,1)S(1)}, bf16[8,96,512]{2,1,0:T(8,128)(2,1)}, u32[]{:S(2)}, u32[]{:S(2)}) collective-permute-start(bf16[8,96,512]{2,1,0:T(8,128)(2,1)S(1)} %collective-permute-done.7.refs_8_), channel_id=1, source_target_pairs={{0,6},{1,7},{2,0},{3,1},{4,2},{5,3},{6,4},{7,5},{8,14},{9,15},{10,... | collective-permute-start | bytes 2359304 | tf_op jit(solution)/shard_map/ppermute | solution.py:49
  69.0 18.7 %collective-permute-start.10 = (bf16[8,96,512]{2,1,0:T(8,128)(2,1)S(1)}, bf16[8,96,512]{2,1,0:T(8,128)(2,1)}, u32[]{:S(2)}, u32[]{:S(2)}) collective-permute-start(bf16[8,96,512]{2,1,0:T(8,128)(2,1)S(1)} %collective-permute-done.7.refs_8_), channel_id=1, source_target_pairs={{0,2},{1,3},{2,4},{3,5},{4,6},{5,7},{6,0},{7,1},{8,10},{9,11},{10,... | collective-permute-start | bytes 2359304 | tf_op jit(solution)/shard_map/ppermute | solution.py:49
  87.6 22.8 %collective-permute-start.12 = (bf16[8,96,512]{2,1,0:T(8,128)(2,1)S(1)}, bf16[8,96,512]{2,1,0:T(8,128)(2,1)S(1)}, u32[]{:S(2)}, u32[]{:S(2)}) collective-permute-start(bf16[8,96,512]{2,1,0:T(8,128)(2,1)S(1)} %collective-permute-done.8.refs_9_), channel_id=1, source_target_pairs={{0,2},{1,3},{2,4},{3,5},{4,6},{5,7},{6,0},{7,1},{8,10},{9,11},{10,... | collective-permute-start | bytes 2359304 | tf_op jit(solution)/shard_map/ppermute | solution.py:49
  87.6 23.7 %collective-permute-start.13 = (bf16[8,96,512]{2,1,0:T(8,128)(2,1)}, bf16[8,96,512]{2,1,0:T(8,128)(2,1)S(1)}, u32[]{:S(2)}, u32[]{:S(2)}) collective-permute-start(bf16[8,96,512]{2,1,0:T(8,128)(2,1)} %collective-permute-done.11.refs_12_), channel_id=1, source_target_pairs={{0,6},{1,7},{2,0},{3,1},{4,2},{5,3},{6,4},{7,5},{8,14},{9,15},{10,... | collective-permute-start | bytes 2359304 | tf_op jit(solution)/shard_map/ppermute | solution.py:49
  112.2 49.0 %all-to-all-start.3 = ((bf16[64,48,512]{2,1,0:T(8,128)(2,1)}), bf16[64,48,512]{2,1,0:T(8,128)(2,1)S(1)}, u32[]{:S(2)}, u32[]{:S(2)}) async-start(bf16[64,48,512]{2,1,0:T(8,128)(2,1)} %bitcast.33), calls=%async_computation.3 | async-start | bytes 6291456 | tf_op jit(solution)/shard_map/all_to_all | solution.py:40
  161.3 7.2 %copy-start.2 = (bf16[1,128,512]{2,1,0:T(8,128)(2,1)S(1)}, bf16[1,128,512]{2,1,0:T(8,128)(2,1)}, u32[]{:S(2)}) copy-start(bf16[1,128,512]{2,1,0:T(8,128)(2,1)} %param.12) | copy-start | bytes 393220
  161.3 47.3 %all-to-all-start.2 = ((bf16[64,48,512]{2,1,0:T(8,128)(2,1)}), bf16[64,48,512]{2,1,0:T(8,128)(2,1)}, u32[]{:S(2)}, u32[]{:S(2)}) async-start(bf16[64,48,512]{2,1,0:T(8,128)(2,1)} %bitcast.32), calls=%async_computation.2 | async-start | bytes 6291456 | tf_op jit(solution)/shard_map/all_to_all | solution.py:40
  168.5 40.1 %copy-start.1 = (bf16[1,128,512]{2,1,0:T(8,128)(2,1)S(1)}, bf16[1,128,512]{2,1,0:T(8,128)(2,1)}, u32[]{:S(2)}) copy-start(bf16[1,128,512]{2,1,0:T(8,128)(2,1)} %param.11) | copy-start | bytes 393220
  212.7 6.7 %collective-permute-start.14 = (bf16[128,512]{1,0:T(8,128)(2,1)S(1)}, bf16[128,512]{1,0:T(8,128)(2,1)S(1)}, u32[]{:S(2)}, u32[]{:S(2)}) collective-permute-start(bf16[128,512]{1,0:T(8,128)(2,1)S(1)} %get-tuple-element.52), channel_id=1, source_target_pairs={{0,64},{64,0},{1,65},{65,1},{2,66},{66,2},{3,67},{67,3},{4,68},{68... | collective-permute-start | bytes 393224 | tf_op jit(solution)/shard_map/ppermute | solution.py:36
  (8 other events, 9.4 us)

commit v4 on v3

--- a/solution.py
+++ b/solution.py
@@ -87,18 +87,20 @@
 def table_kernel(upcoming, gain, router, tokens_out):
     tokens, part = upcoming.shape
     experts = router.shape[0]
-    tokens_out[0:tokens, :] = upcoming[...]
     gains = gain[...]
     scaled = router[...] * gains
     rows = [p.astype(jnp.float32) for p in three_parts(scaled)]
     rows += [p.astype(jnp.float32) for p in three_parts(gains)]
     rows.append(jnp.zeros((TABLE - 3 * experts - 3, part), jnp.float32))
-    tokens_out[tokens : tokens + TABLE, :] = jnp.concatenate(rows, axis=0).astype(jnp.bfloat16)
+    table = jnp.concatenate(rows, axis=0).astype(jnp.bfloat16)
+    for copy in range(tokens_out.shape[0]):
+        tokens_out[copy, 0:tokens, :] = upcoming[...]
+        tokens_out[copy, tokens : tokens + TABLE, :] = table
 
 
 def with_table(upcoming, gain, router):
     tokens, part = upcoming.shape
-    shape = (tokens + TABLE, part)
+    shape = (GROUPS, tokens + TABLE, part)
     return pl.pallas_call(
         table_kernel,
         out_shape=jax.ShapeDtypeStruct(shape, jnp.bfloat16),
@@ -163,18 +165,18 @@
     )(routes_s, routes_n, saved, cot)
 
 
-def spread_kernel(sel, *refs):
-    pieces, (moved, table) = refs[:GROUPS], refs[GROUPS:]
+def spread_kernel(order, sel, pieces, moved, table):
     tokens = sel.shape[0]
     blocks, _, capacity, part = moved.shape
-    for group, piece in enumerate(pieces):
+    for group in range(GROUPS):
+        piece = pieces[order[group]]
         rows = product(sel[...], piece[0:tokens, :], LEADING).astype(jnp.bfloat16)
         moved[:, group] = rows.reshape(blocks, capacity, part)
         table[group] = piece[tokens : tokens + TABLE, :]
 
 
-def spread(sel, pieces, blocks):
-    part = pieces[0].shape[1]
+def spread(order, sel, pieces, blocks):
+    part = pieces.shape[2]
     capacity = sel.shape[1] // blocks
     return pl.pallas_call(
         spread_kernel,
@@ -182,10 +184,11 @@
             jax.ShapeDtypeStruct((blocks, GROUPS, capacity, part), jnp.bfloat16),
             jax.ShapeDtypeStruct((GROUPS, TABLE, part), jnp.bfloat16),
         ),
-        in_specs=[VMEM] * (1 + GROUPS),
-        out_specs=(VMEM, VMEM),
-        compiler_params=pltpu.CompilerParams(vmem_limit_bytes=LIMIT // 2),
-    )(sel, *pieces)
+        grid=(1,),
+        in_specs=[SMEM, whole(sel.shape), whole(pieces.shape)],
+        out_specs=(whole((blocks, GROUPS, capacity, part)), whole((GROUPS, TABLE, part))),
+        compiler_params=pltpu.CompilerParams(vmem_limit_bytes=MOST),
+    )(order, sel, pieces)
 
 
 def widen(value, width):
@@ -543,9 +546,9 @@
     tokens_next = with_table(next_input[0], norm_gain, router[0].T)
     tokens_next, routes = lax.optimization_barrier((tokens_next, (routes_saved[0], routes_next[0])))
     packed, sel_saved, sel_next = pack(*routes, saved_input[0], cotangent[0], experts, capacity)
-    near, packed = gather_near(tokens_next, packed)
+    tokens_next = swap(tokens_next, "hid")
     packed = swap(packed, "expert")
-    moved_next, table = spread(sel_next, near + gather_far(near), experts)
+    moved_next, table = spread(order, sel_next, tokens_next, experts)
     moved_next = swap(moved_next, "expert")
     other = packed[:, :, part:]
     near, _ = gather_near(packed[:, :, :part])

time: 221 us -> 229 us (1.036)
  waiting for transfers between devices: 97.6 us -> 115 us
  starting transfers between devices: 49.2 us -> 41.3 us
  local copies, waits for them, and re-layouts: 11 us -> 7.58 us
    all_to_all x4 -> x5, waiting for transfers between devices: 48.7 us -> 74.4 us  [swap(): return lax.all_to_all(block, axes, split_axis=0, concat_axis=0, tiled=True)]
    ppermute x14 -> x7, starting transfers between devices: 17.8 us -> 5.74 us  [shift(): return lax.ppermute(block, 'hid', route)]
    ppermute x14 -> x7, waiting for transfers between devices: 44.9 us -> 36.7 us  [shift(): return lax.ppermute(block, 'hid', route)]
    all_to_all x4 -> x5, starting transfers between devices: 28.8 us -> 32.9 us  [swap(): return lax.all_to_all(block, axes, split_axis=0, concat_axis=0, tiled=True)]
    unnamed x29 -> x23, local copies, waits for them, and re-layouts: 9.65 us -> 6.21 us
  transfers between devices with their start and end apart: 19 -> 13, of which waited for: 10 -> 9; matrix products, arithmetic and copies ran while one was open for 1% -> 1% of each run, Pallas kernels for 26% -> 25%
where the time goes in v4:
time: 229 us; the launch traced here: 228 us
  waiting for transfers between devices  115 us (50%)
  Pallas kernels  62.6 us (27%)
  starting transfers between devices  41.3 us (18%)
  local copies, waits for them, and re-layouts  7.58 us (3%)
    all_to_all x5, waiting for transfers between devices, swap(): return lax.all_to_all(block, axes, split_axis=0, concat_axis=0, tiled=True)  74.4 us
    ppermute x7, waiting for transfers between devices, shift(): return lax.ppermute(block, 'hid', route)  36.7 us
    all_to_all x5, starting transfers between devices, swap(): return lax.all_to_all(block, axes, split_axis=0, concat_axis=0, tiled=True)  32.9 us
    pallas_call x1, Pallas kernels, backward(): pl.pallas_call(backward_kernel, out_shape=jax.ShapeDtypeStruct((blocks, G...  29.9 us
    pallas_call x1, Pallas kernels, forward(): pl.pallas_call(forward_kernel, out_shape=jax.ShapeDtypeStruct(moved.shape...  20 us
    unnamed x23, local copies, waits for them, and re-layouts  6.21 us
    ppermute x7, starting transfers between devices, shift(): return lax.ppermute(block, 'hid', route)  5.74 us
  transfers between devices with their start and end apart: 13, of which 9 were waited for; matrix products, arithmetic and copies ran while one was open for 1% of the time, Pallas kernels for 25%

profile of v4, /device:TPU:1, one launch (start us, length us, event | category | flops | bytes accessed | tf_op | source)
XLA Modules:
  0.0 228.2 jit_solution(16977676125151504908)
XLA Ops:
  0.6 1.4 copy.12
  2.0 1.4 copy.13
  3.5 2.1 shard_map.113
  5.6 5.9 %all-to-all-start.1 = ((bf16[8,160,512]{2,1,0:T(8,128)(2,1)}), bf16[8,160,512]{2,1,0:T(8,128)(2,1)S(1)}, u32[]{:S(2)}, u32[]{:S(2)}) async-start(bf16[8,160,512]{2,1,0:T(8,128)(2,1)} %shard_map.113), calls=%async_computation.1 | async-start | bytes 2621440 | tf_op jit(solution)/shard_map/all_to_all | solution.py:40
  11.4 3.3 %shard_map.114 = (bf16[8,96,640]{2,1,0:T(8,128)(2,1)}, bf16[128,384]{1,0:T(8,128)(2,1)}, bf16[128,384]{1,0:T(8,128)(2,1)}) custom-call(s32[128,2]{1,0:T(8,128)} %bitcast.34, s32[128,2]{1,0:T(8,128)} %bitcast.35, bf16[128,512]{1,0:T(8,128)(2,1)} %bitcast.36, bf16[128,512]{1,0:T(8,128)(2,1)} %bitcast.30), custom_call_target="tpu_custom_call" | custom-call | tf_op jit(solution)/shard_map/pallas_call | solution.py:158
  14.7 16.0 %all-to-all-done.1.pieces = bf16[8,160,512]{2,1,0:T(8,128)(2,1)S(1)} async-done(((bf16[8,160,512]{2,1,0:T(8,128)(2,1)}), bf16[8,160,512]{2,1,0:T(8,128)(2,1)S(1)}, u32[]{:S(2)}, u32[]{:S(2)}) %all-to-all-start.1) | async-done | bytes 1310752 | tf_op jit(solution)/shard_map/all_to_all | solution.py:40
  30.7 6.9 %all-to-all-start = ((bf16[8,96,640]{2,1,0:T(8,128)(2,1)}), bf16[8,96,640]{2,1,0:T(8,128)(2,1)S(1)}, u32[]{:S(2)}, u32[]{:S(2)}) async-start(bf16[8,96,640]{2,1,0:T(8,128)(2,1)} %get-tuple-element.26), calls=%async_computation | async-start | bytes 1966080 | tf_op jit(solution)/shard_map/all_to_all | solution.py:40
  38.2 4.0 %shard_map.115 = (bf16[8,8,48,512]{3,2,1,0:T(8,128)(2,1)}, bf16[8,32,512]{2,1,0:T(8,128)(2,1)}) custom-call(s32[8]{0:T(128)} %stack.35.order.refs_0_, bf16[128,384]{1,0:T(8,128)(2,1)} %get-tuple-element.27.sel, bf16[8,160,512]{2,1,0:T(8,128)(2,1)} %copy-done.4), custom_call_target="tpu_custom_call" | custom-call | tf_op jit(solution)/shard_map/pallas_call | solution.py:181
  42.2 9.8 %all-to-all-done = bf16[8,96,640]{2,1,0:T(8,128)(2,1)S(1)} async-done(((bf16[8,96,640]{2,1,0:T(8,128)(2,1)}), bf16[8,96,640]{2,1,0:T(8,128)(2,1)S(1)}, u32[]{:S(2)}, u32[]{:S(2)}) %all-to-all-start) | async-done | bytes 983072 | tf_op jit(solution)/shard_map/all_to_all | solution.py:40
  52.0 5.2 %all-to-all-start.2 = ((bf16[8,8,48,512]{3,2,1,0:T(8,128)(2,1)}), bf16[8,8,48,512]{3,2,1,0:T(8,128)(2,1)}, u32[]{:S(2)}, u32[]{:S(2)}) async-start(bf16[8,8,48,512]{3,2,1,0:T(8,128)(2,1)} %get-tuple-element.33), calls=%async_computation.2 | async-start | bytes 6291456 | tf_op jit(solution)/shard_map/all_to_all | solution.py:40
  57.4 1.5 collective-permute-start.1
  58.8 17.6 %collective-permute-done.2.refs_11_ = bf16[8,96,512]{2,1,0:T(8,128)(2,1)S(1)} collective-permute-done((bf16[8,96,512]{2,1,0:T(8,128)(2,1)S(1)}, bf16[8,96,512]{2,1,0:T(8,128)(2,1)S(1)}, u32[]{:S(2)}, u32[]{:S(2)}) %collective-permute-start.2) | collective-permute-done | bytes 786464 | tf_op jit(solution)/shard_map/ppermute | solution.py:49
  80.0 16.0 %collective-permute-done.4.refs_12_ = bf16[8,96,512]{2,1,0:T(8,128)(2,1)} collective-permute-done((bf16[8,96,512]{2,1,0:T(8,128)(2,1)S(1)}, bf16[8,96,512]{2,1,0:T(8,128)(2,1)}, u32[]{:S(2)}, u32[]{:S(2)}) %collective-permute-start.4) | collective-permute-done | bytes 786464 | tf_op jit(solution)/shard_map/ppermute | solution.py:49
  96.1 1.8 collective-permute-done.3.refs_10_
  97.8 2.7 %collective-permute-start.6 = (bf16[8,96,512]{2,1,0:T(8,128)(2,1)}, bf16[8,96,512]{2,1,0:T(8,128)(2,1)}, u32[]{:S(2)}, u32[]{:S(2)}) collective-permute-start(bf16[8,96,512]{2,1,0:T(8,128)(2,1)} %collective-permute-done.4.refs_12_), channel_id=1, source_target_pairs={{0,6},{1,7},{2,0},{3,1},{4,2},{5,3},{6,4},{7,5},{8,14},{9,15},{10,... | collective-permute-start | bytes 2359304 | tf_op jit(solution)/shard_map/ppermute | solution.py:49
  100.5 20.0 %shard_map.116 = bf16[8,8,48,512]{3,2,1,0:T(8,128)(2,1)} custom-call(s32[8]{0:T(128)} %stack.35.order.refs_0_, s32[1]{0:T(128)} %bitcast.15.own.refs_1_, bf16[8,8,48,512]{3,2,1,0:T(8,128)(2,1)} %all-to-all-done.2.moved_in, bf16[8,96,128]{2,1,0:T(8,128)(2,1)} %slice.8.other.refs_2_, bf16[8,32,512]{2,1,0:T(8,128)(2,1)} %get-tuple-element.29.table.refs_3_, ...), custom_call_target="tpu_custom_call" | custom-call | flops 8455716864 | bytes 28311552 | tf_op jit(solution)/shard_map/pallas_call | solution.py:353
  121.5 7.7 %all-to-all-start.4 = ((bf16[64,48,512]{2,1,0:T(8,128)(2,1)}), bf16[64,48,512]{2,1,0:T(8,128)(2,1)S(1)}, u32[]{:S(2)}, u32[]{:S(2)}) async-start(bf16[64,48,512]{2,1,0:T(8,128)(2,1)} %bitcast.33), calls=%async_computation.4 | async-start | bytes 6291456 | tf_op jit(solution)/shard_map/all_to_all | solution.py:40
  129.2 29.9 %shard_map.117 = bf16[8,8,48,512]{3,2,1,0:T(8,128)(2,1)} custom-call(s32[8]{0:T(128)} %stack.35.order.refs_0_, s32[1]{0:T(128)} %bitcast.15.own.refs_1_, bf16[8,96,128]{2,1,0:T(8,128)(2,1)} %slice.8.other.refs_2_, bf16[8,32,512]{2,1,0:T(8,128)(2,1)} %get-tuple-element.29.table.refs_3_, bf16[4096,896]{1,0:T(8,128)(2,1)} %bitcast.40, ...), custom_call_target="tpu_custom_call" | custom-call | flops 14092861440 | bytes 31457280 | tf_op jit(solution)/shard_map/pallas_call | solution.py:471
  159.1 10.3 %all-to-all-done.4 = bf16[64,48,512]{2,1,0:T(8,128)(2,1)S(1)} async-done(((bf16[64,48,512]{2,1,0:T(8,128)(2,1)}), bf16[64,48,512]{2,1,0:T(8,128)(2,1)S(1)}, u32[]{:S(2)}, u32[]{:S(2)}) %all-to-all-start.4) | async-done | bytes 3145760 | tf_op jit(solution)/shard_map/all_to_all | solution.py:40
  169.3 7.2 %all-to-all-start.3 = ((bf16[64,48,512]{2,1,0:T(8,128)(2,1)}), bf16[64,48,512]{2,1,0:T(8,128)(2,1)}, u32[]{:S(2)}, u32[]{:S(2)}) async-start(bf16[64,48,512]{2,1,0:T(8,128)(2,1)} %bitcast.32), calls=%async_computation.3 | async-start | bytes 6291456 | tf_op jit(solution)/shard_map/all_to_all | solution.py:40
  178.2 38.4 %all-to-all-done.3 = bf16[64,48,512]{2,1,0:T(8,128)(2,1)} async-done(((bf16[64,48,512]{2,1,0:T(8,128)(2,1)}), bf16[64,48,512]{2,1,0:T(8,128)(2,1)}, u32[]{:S(2)}, u32[]{:S(2)}) %all-to-all-start.3) | async-done | bytes 3145760 | tf_op jit(solution)/shard_map/all_to_all | solution.py:40
  217.5 2.6 %shard_map.118 = bf16[128,512]{1,0:T(8,128)(2,1)S(1)} custom-call(bf16[128,384]{1,0:T(8,128)(2,1)S(1)} %copy-done.3, bf16[8,8,48,512]{3,2,1,0:T(8,128)(2,1)} %bitcast.20.home, bf16[128,512]{1,0:T(8,128)(2,1)S(1)} %bitcast.31), custom_call_target="tpu_custom_call" | custom-call | tf_op jit(solution)/shard_map/pallas_call | solution.py:512
  220.8 2.6 %collective-permute-start.7 = (bf16[128,512]{1,0:T(8,128)(2,1)S(1)}, bf16[128,512]{1,0:T(8,128)(2,1)S(1)}, u32[]{:S(2)}, u32[]{:S(2)}) collective-permute-start(bf16[128,512]{1,0:T(8,128)(2,1)S(1)} %get-tuple-element.44), channel_id=1, source_target_pairs={{0,64},{64,0},{1,65},{65,1},{2,66},{66,2},{3,67},{67,3},{4,68},{68... | collective-permute-start | bytes 393224 | tf_op jit(solution)/shard_map/ppermute | solution.py:36
  223.4 4.1 %collective-permute-done.7 = bf16[128,512]{1,0:T(8,128)(2,1)S(1)} collective-permute-done((bf16[128,512]{1,0:T(8,128)(2,1)S(1)}, bf16[128,512]{1,0:T(8,128)(2,1)S(1)}, u32[]{:S(2)}, u32[]{:S(2)}) %collective-permute-start.7) | collective-permute-done | bytes 131104 | tf_op jit(solution)/shard_map/ppermute | solution.py:36
  (36 shorter events, 9.1 us)
Async XLA Ops:
  5.6 25.1 %all-to-all-start.1 = ((bf16[8,160,512]{2,1,0:T(8,128)(2,1)}), bf16[8,160,512]{2,1,0:T(8,128)(2,1)S(1)}, u32[]{:S(2)}, u32[]{:S(2)}) async-start(bf16[8,160,512]{2,1,0:T(8,128)(2,1)} %shard_map.113), calls=%async_computation.1 | async-start | bytes 2621440 | tf_op jit(solution)/shard_map/all_to_all | solution.py:40
  30.7 7.5 %copy-start.4 = (bf16[8,160,512]{2,1,0:T(8,128)(2,1)}, bf16[8,160,512]{2,1,0:T(8,128)(2,1)S(1)}, u32[]{:S(2)}) copy-start(bf16[8,160,512]{2,1,0:T(8,128)(2,1)S(1)} %all-to-all-done.1.pieces) | copy-start | bytes 3932164
  30.7 21.3 %all-to-all-start = ((bf16[8,96,640]{2,1,0:T(8,128)(2,1)}), bf16[8,96,640]{2,1,0:T(8,128)(2,1)S(1)}, u32[]{:S(2)}, u32[]{:S(2)}) async-start(bf16[8,96,640]{2,1,0:T(8,128)(2,1)} %get-tuple-element.26), calls=%async_computation | async-start | bytes 1966080 | tf_op jit(solution)/shard_map/all_to_all | solution.py:40
  52.0 45.8 %all-to-all-start.2 = ((bf16[8,8,48,512]{3,2,1,0:T(8,128)(2,1)}), bf16[8,8,48,512]{3,2,1,0:T(8,128)(2,1)}, u32[]{:S(2)}, u32[]{:S(2)}) async-start(bf16[8,8,48,512]{3,2,1,0:T(8,128)(2,1)} %get-tuple-element.33), calls=%async_computation.2 | async-start | bytes 6291456 | tf_op jit(solution)/shard_map/all_to_all | solution.py:40
  57.3 1.5 copy-start.5
  57.3 19.2 %collective-permute-start.2 = (bf16[8,96,512]{2,1,0:T(8,128)(2,1)S(1)}, bf16[8,96,512]{2,1,0:T(8,128)(2,1)S(1)}, u32[]{:S(2)}, u32[]{:S(2)}) collective-permute-start(bf16[8,96,512]{2,1,0:T(8,128)(2,1)S(1)} %slice.9.refs_7_), channel_id=1, source_target_pairs={{0,6},{1,7},{2,0},{3,1},{4,2},{5,3},{6,4},{7,5},{8,14},{9,15},{10,... | collective-permute-start | bytes 2359304 | tf_op jit(solution)/shard_map/ppermute | solution.py:49
  57.4 20.4 %collective-permute-start.1 = (bf16[8,96,512]{2,1,0:T(8,128)(2,1)S(1)}, bf16[8,96,512]{2,1,0:T(8,128)(2,1)S(1)}, u32[]{:S(2)}, u32[]{:S(2)}) collective-permute-start(bf16[8,96,512]{2,1,0:T(8,128)(2,1)S(1)} %slice.9.refs_7_), channel_id=1, source_target_pairs={{0,2},{1,3},{2,4},{3,5},{4,6},{5,7},{6,0},{7,1},{8,10},{9,11},{10,... | collective-permute-start | bytes 2359304 | tf_op jit(solution)/shard_map/ppermute | solution.py:49
  58.8 18.9 %collective-permute-start = (bf16[8,96,512]{2,1,0:T(8,128)(2,1)S(1)}, bf16[8,96,512]{2,1,0:T(8,128)(2,1)S(1)}, u32[]{:S(2)}, u32[]{:S(2)}) collective-permute-start(bf16[8,96,512]{2,1,0:T(8,128)(2,1)S(1)} %slice.9.refs_7_), channel_id=1, source_target_pairs={{0,1},{1,0},{2,3},{3,2},{4,5},{5,4},{6,7},{7,6},{8,9},{9,8},{10,11... | collective-permute-start | bytes 2359304 | tf_op jit(solution)/shard_map/ppermute | solution.py:49
  76.5 1.3 copy-start.6
  77.8 42.8 %copy-start.7 = (bf16[8,96,512]{2,1,0:T(8,128)(2,1)}, bf16[8,96,512]{2,1,0:T(8,128)(2,1)S(1)}, u32[]{:S(2)}) copy-start(bf16[8,96,512]{2,1,0:T(8,128)(2,1)S(1)} %collective-permute-done.1.refs_9_) | copy-start | bytes 2359300
  77.8 42.8 %copy-start.8 = (bf16[8,96,512]{2,1,0:T(8,128)(2,1)}, bf16[8,96,512]{2,1,0:T(8,128)(2,1)S(1)}, u32[]{:S(2)}) copy-start(bf16[8,96,512]{2,1,0:T(8,128)(2,1)S(1)} %collective-permute-done.refs_8_) | copy-start | bytes 2359300
  77.8 18.3 %collective-permute-start.4 = (bf16[8,96,512]{2,1,0:T(8,128)(2,1)S(1)}, bf16[8,96,512]{2,1,0:T(8,128)(2,1)}, u32[]{:S(2)}, u32[]{:S(2)}) collective-permute-start(bf16[8,96,512]{2,1,0:T(8,128)(2,1)S(1)} %collective-permute-done.refs_8_), channel_id=1, source_target_pairs={{0,6},{1,7},{2,0},{3,1},{4,2},{5,3},{6,4},{7,5},{8,14},{9,15},{10,... | collective-permute-start | bytes 2359304 | tf_op jit(solution)/shard_map/ppermute | solution.py:49
  78.9 18.9 %collective-permute-start.3 = (bf16[8,96,512]{2,1,0:T(8,128)(2,1)S(1)}, bf16[8,96,512]{2,1,0:T(8,128)(2,1)}, u32[]{:S(2)}, u32[]{:S(2)}) collective-permute-start(bf16[8,96,512]{2,1,0:T(8,128)(2,1)S(1)} %collective-permute-done.refs_8_), channel_id=1, source_target_pairs={{0,2},{1,3},{2,4},{3,5},{4,6},{5,7},{6,0},{7,1},{8,10},{9,11},{10,... | collective-permute-start | bytes 2359304 | tf_op jit(solution)/shard_map/ppermute | solution.py:49
  97.8 22.7 %collective-permute-start.5 = (bf16[8,96,512]{2,1,0:T(8,128)(2,1)S(1)}, bf16[8,96,512]{2,1,0:T(8,128)(2,1)S(1)}, u32[]{:S(2)}, u32[]{:S(2)}) collective-permute-start(bf16[8,96,512]{2,1,0:T(8,128)(2,1)S(1)} %collective-permute-done.1.refs_9_), channel_id=1, source_target_pairs={{0,2},{1,3},{2,4},{3,5},{4,6},{5,7},{6,0},{7,1},{8,10},{9,11},{10,... | collective-permute-start | bytes 2359304 | tf_op jit(solution)/shard_map/ppermute | solution.py:49
  97.8 22.8 %collective-permute-start.6 = (bf16[8,96,512]{2,1,0:T(8,128)(2,1)}, bf16[8,96,512]{2,1,0:T(8,128)(2,1)}, u32[]{:S(2)}, u32[]{:S(2)}) collective-permute-start(bf16[8,96,512]{2,1,0:T(8,128)(2,1)} %collective-permute-done.4.refs_12_), channel_id=1, source_target_pairs={{0,6},{1,7},{2,0},{3,1},{4,2},{5,3},{6,4},{7,5},{8,14},{9,15},{10,... | collective-permute-start | bytes 2359304 | tf_op jit(solution)/shard_map/ppermute | solution.py:49
  120.6 0.9 copy-start.9
  121.5 47.9 %all-to-all-start.4 = ((bf16[64,48,512]{2,1,0:T(8,128)(2,1)}), bf16[64,48,512]{2,1,0:T(8,128)(2,1)S(1)}, u32[]{:S(2)}, u32[]{:S(2)}) async-start(bf16[64,48,512]{2,1,0:T(8,128)(2,1)} %bitcast.33), calls=%async_computation.4 | async-start | bytes 6291456 | tf_op jit(solution)/shard_map/all_to_all | solution.py:40
  169.3 7.2 %copy-start = (bf16[1,128,512]{2,1,0:T(8,128)(2,1)S(1)}, bf16[1,128,512]{2,1,0:T(8,128)(2,1)}, u32[]{:S(2)}) copy-start(bf16[1,128,512]{2,1,0:T(8,128)(2,1)} %param.12) | copy-start | bytes 393220
  169.3 47.3 %all-to-all-start.3 = ((bf16[64,48,512]{2,1,0:T(8,128)(2,1)}), bf16[64,48,512]{2,1,0:T(8,128)(2,1)}, u32[]{:S(2)}, u32[]{:S(2)}) async-start(bf16[64,48,512]{2,1,0:T(8,128)(2,1)} %bitcast.32), calls=%async_computation.3 | async-start | bytes 6291456 | tf_op jit(solution)/shard_map/all_to_all | solution.py:40
  176.6 40.1 %copy-start.1 = (bf16[1,128,512]{2,1,0:T(8,128)(2,1)S(1)}, bf16[1,128,512]{2,1,0:T(8,128)(2,1)}, u32[]{:S(2)}) copy-start(bf16[1,128,512]{2,1,0:T(8,128)(2,1)} %param.11) | copy-start | bytes 393220
  176.6 0.9 copy-start.2
  216.6 0.9 copy-start.3
  220.8 6.7 %collective-permute-start.7 = (bf16[128,512]{1,0:T(8,128)(2,1)S(1)}, bf16[128,512]{1,0:T(8,128)(2,1)S(1)}, u32[]{:S(2)}, u32[]{:S(2)}) collective-permute-start(bf16[128,512]{1,0:T(8,128)(2,1)S(1)} %get-tuple-element.44), channel_id=1, source_target_pairs={{0,64},{64,0},{1,65},{65,1},{2,66},{66,2},{3,67},{67,3},{4,68},{68... | collective-permute-start | bytes 393224 | tf_op jit(solution)/shard_map/ppermute | solution.py:36

commit v5 on v3

--- a/solution.py
+++ b/solution.py
@@ -109,7 +109,7 @@
     )(upcoming, gain, router)
 
 
-def pack_kernel(experts, capacity, routes_s, routes_n, saved, cot, packed, sel_s, sel_n):
+def pack_kernel(experts, capacity, routes_s, routes_n, saved, cot, packed, sel_s, one_n, two_n):
     tokens, part = saved.shape
     row = lax.broadcasted_iota(jnp.int32, (tokens, tokens), 0)
     lane = lax.broadcasted_iota(jnp.int32, (tokens, tokens), 1)
@@ -127,32 +127,33 @@
         rank_two = jnp.sum(counts * hit_two, axis=1, keepdims=True).astype(jnp.int32)
         first = jnp.where(slots == one * capacity + rank_one, 1.0, 0.0)
         second = jnp.where(slots == two * capacity + rank_two, 1.0, 0.0)
-        inside = wide < 3 * experts
-        wide_one = jnp.where(inside & (lax.rem(wide, experts) == one), 1.0, 0.0).astype(jnp.bfloat16)
-        wide_two = jnp.where(inside & (lax.rem(wide, experts) == two), 1.0, 0.0).astype(jnp.bfloat16)
-        other = product(first.astype(jnp.bfloat16), wide_two, LEADING)
-        other = other + product(second.astype(jnp.bfloat16), wide_one, LEADING)
-        return (first + second).astype(jnp.bfloat16), other.astype(jnp.bfloat16)
+        return one, two, first.astype(jnp.bfloat16), second.astype(jnp.bfloat16)
 
     def put(start, lanes, width, value):
         packed[:, start : start + capacity, lanes : lanes + width] = value.reshape(
             experts, capacity, width
         )
 
-    both, other = select(routes_s)
+    one, two, first, second = select(routes_s)
+    inside = wide < 3 * experts
+    wide_one = jnp.where(inside & (lax.rem(wide, experts) == one), 1.0, 0.0).astype(jnp.bfloat16)
+    wide_two = jnp.where(inside & (lax.rem(wide, experts) == two), 1.0, 0.0).astype(jnp.bfloat16)
+    both = first + second
     sel_s[...] = both
     put(0, 0, part, product(both, saved[...], LEADING).astype(jnp.bfloat16))
     put(capacity, 0, part, product(both, cot[...], LEADING).astype(jnp.bfloat16))
-    put(0, part, 128, other)
-    both, other = select(routes_n)
-    sel_n[...] = both
-    put(capacity, part, 128, other)
+    other = product(first, wide_two, LEADING) + product(second, wide_one, LEADING)
+    put(0, part, 128, other.astype(jnp.bfloat16))
+    put(capacity, part, 128, jnp.zeros(other.shape, jnp.bfloat16))
+    _, _, first, second = select(routes_n)
+    one_n[...] = first
+    two_n[...] = second
 
 
 def pack(routes_s, routes_n, saved, cot, experts, capacity):
     tokens, part = saved.shape
     total = experts * capacity
-    shapes = [(experts, 2 * capacity, part + 128), (tokens, total), (tokens, total)]
+    shapes = [(experts, 2 * capacity, part + 128)] + [(tokens, total)] * 3
     return pl.pallas_call(
         functools.partial(pack_kernel, experts, capacity),
         out_shape=[jax.ShapeDtypeStruct(s, jnp.bfloat16) for s in shapes],
@@ -163,29 +164,48 @@
     )(routes_s, routes_n, saved, cot)
 
 
-def spread_kernel(sel, *refs):
-    pieces, (moved, table) = refs[:GROUPS], refs[GROUPS:]
-    tokens = sel.shape[0]
+def spread_kernel(routes, one_n, two_n, *refs):
+    pieces, (moved, table, ones, twos) = refs[:GROUPS], refs[GROUPS:]
+    tokens = one_n.shape[0]
     blocks, _, capacity, part = moved.shape
+    total = jnp.zeros((tokens, 128), jnp.float32)
+    logits = jnp.zeros((tokens, TABLE), jnp.float32)
     for group, piece in enumerate(pieces):
-        rows = product(sel[...], piece[0:tokens, :], LEADING).astype(jnp.bfloat16)
+        table[group] = piece[tokens : tokens + TABLE, :]
+        values = piece[0:tokens, :].astype(jnp.float32)
+        total = total + lanes(values * values)
+        logits = logits + product(piece[0:tokens, :], piece[tokens : tokens + TABLE, :], CONTRACT)
+    scale = lax.rsqrt(even(total) / (GROUPS * part) + EPSILON)
+    ids = routes[...]
+    place = lax.broadcasted_iota(jnp.int32, (tokens, TABLE), 1)
+    first = jnp.where((place < 24) & (lax.rem(place, 8) == ids[:, 0:1]), 1.0, 0.0)
+    second = jnp.where((place < 24) & (lax.rem(place, 8) == ids[:, 1:2]), 1.0, 0.0)
+    diff = even(logits * (first - second)) * scale
+    ones[...] = jax.nn.sigmoid(diff)
+    twos[...] = jax.nn.sigmoid(-diff)
+    both = one_n[...] + two_n[...]
+    for group, piece in enumerate(pieces):
+        values = piece[0:tokens, :].astype(jnp.float32)
+        normed = (values * widen(scale, part) * gains_of(table, group)).astype(jnp.bfloat16)
+        rows = product(both, normed, LEADING).astype(jnp.bfloat16)
         moved[:, group] = rows.reshape(blocks, capacity, part)
-        table[group] = piece[tokens : tokens + TABLE, :]
-
-
-def spread(sel, pieces, blocks):
+
+
+def spread(routes, one_n, two_n, pieces, blocks):
     part = pieces[0].shape[1]
-    capacity = sel.shape[1] // blocks
+    tokens, total = one_n.shape
     return pl.pallas_call(
         spread_kernel,
         out_shape=(
-            jax.ShapeDtypeStruct((blocks, GROUPS, capacity, part), jnp.bfloat16),
+            jax.ShapeDtypeStruct((blocks, GROUPS, total // blocks, part), jnp.bfloat16),
             jax.ShapeDtypeStruct((GROUPS, TABLE, part), jnp.bfloat16),
+            jax.ShapeDtypeStruct((tokens, 128), jnp.float32),
+            jax.ShapeDtypeStruct((tokens, 128), jnp.float32),
         ),
-        in_specs=[VMEM] * (1 + GROUPS),
-        out_specs=(VMEM, VMEM),
+        in_specs=[VMEM] * (3 + GROUPS),
+        out_specs=(VMEM,) * 4,
         compiler_params=pltpu.CompilerParams(vmem_limit_bytes=LIMIT // 2),
-    )(sel, *pieces)
+    )(routes, one_n, two_n, *pieces)
 
 
 def widen(value, width):
@@ -280,13 +300,6 @@
             ).astype(jnp.bfloat16)
 
 
-def fetch_blocks(source, target, sems):
-    return [
-        pltpu.make_async_copy(source.at[block], target.at[block], sems.at[block])
-        for block in range(source.shape[0])
-    ]
-
-
 def hand_out(group, place, source, target, sems):
     return pltpu.make_async_copy(
         source.at[:, group : group + 1], target.at[:, pl.ds(place, 1)], sems.at[group]
@@ -294,30 +307,29 @@
 
 
 def forward_kernel(
-    order, own, moved_in, other, table, gate_w, up_w, down_w, out_to,
-    moved, out, gate_b, up_b, down_b, normed, gate, up, hidden, scales, diffs, logits,
-    sem_m, sem_o, sem_g, sem_u, sem_d
+    order, moved, gate_w, up_w, down_w, out_to,
+    rows, out, gate_b, up_b, down_b, gate, up, hidden, sem_m, sem_o, sem_g, sem_u, sem_d
 ):
     blocks, _, capacity, part = moved.shape
-    arrive = fetch_blocks(moved_in, moved, sem_m)
-    start(arrive)
+    total, width = blocks * capacity, GROUPS * part
+    arrive = [
+        pltpu.make_async_copy(
+            moved.at[:, group], rows.at[:, :, pl.ds(group * part, part)], sem_m.at[group]
+        )
+        for group in range(GROUPS)
+    ]
     copies = fetch_rows(order, gate_w, gate_b, sem_g, part)
     copies_up = fetch_rows(order, up_w, up_b, sem_u, part)
     copies_down = fetch_columns(None, down_w, down_b, sem_d, part)
+    start(arrive)
     start(copies)
     wait(arrive)
-
-    def take(group, block):
-        return moved[block, group]
-
-    prepare(
-        own[0], capacity, take, other, table, normed, scales, diffs, logits, GROUPS * part, copies_up
-    )
+    start(copies_up)
     wait(copies)
     start(copies_down)
-    gate[...] = product(normed[...], gate_b[...], INNER)
+    gate[...] = product(rows[...].reshape(total, width), gate_b[...], INNER)
     wait(copies_up)
-    up[...] = product(normed[...], up_b[...], INNER)
+    up[...] = product(rows[...].reshape(total, width), up_b[...], INNER)
 
     @pl.loop(0, blocks)
     def _(block):
@@ -325,11 +337,10 @@
         value = gate[at, :]
         hidden[at, :] = (value * jax.nn.sigmoid(value) * up[at, :]).astype(jnp.bfloat16)
 
-    share = widen(jax.nn.sigmoid(diffs[...]), part)
     for group in range(GROUPS):
         copies_down[group].wait()
-        rows = product(hidden[...], down_b[:, group * part : (group + 1) * part], INNER)
-        out[:, group] = (rows * share).astype(jnp.bfloat16).reshape(blocks, capacity, part)
+        part_out = product(hidden[...], down_b[:, group * part : (group + 1) * part], INNER)
+        out[:, group] = part_out.astype(jnp.bfloat16).reshape(blocks, capacity, part)
         hand_out(group, group, out, out_to, sem_o).start()
     for group in range(GROUPS):
         hand_out(group, group, out, out_to, sem_o).wait()
@@ -343,35 +354,33 @@
     ]
 
 
-def forward(order, own, moved, other, table, gate_w, up_w, down_w):
+def forward(order, moved, gate_w, up_w, down_w):
     blocks, _, capacity, part = moved.shape
     width, units = gate_w.shape
     total = blocks * capacity
     return pl.pallas_call(
         forward_kernel,
         out_shape=jax.ShapeDtypeStruct(moved.shape, jnp.bfloat16),
-        in_specs=[SMEM, SMEM, PLACE, VMEM, VMEM, PLACE, PLACE, PLACE],
+        in_specs=[SMEM] + [PLACE] * 4,
         out_specs=PLACE,
-        scratch_shapes=[pltpu.VMEM(moved.shape, jnp.bfloat16)] * 2
+        scratch_shapes=[
+            pltpu.VMEM((blocks, capacity, width), jnp.bfloat16),
+            pltpu.VMEM(moved.shape, jnp.bfloat16),
+        ]
         + weight_scratch(width, units)
         + [
-            pltpu.VMEM((total, width), jnp.bfloat16),
             pltpu.VMEM((total, units), jnp.float32),
             pltpu.VMEM((total, units), jnp.float32),
             pltpu.VMEM((total, units), jnp.bfloat16),
-            pltpu.VMEM((total, 128), jnp.float32),
-            pltpu.VMEM((total, 128), jnp.float32),
-            pltpu.VMEM((total, TABLE), jnp.float32),
         ]
-        + [pltpu.SemaphoreType.DMA((blocks,))]
-        + [pltpu.SemaphoreType.DMA((GROUPS,))] * 4,
+        + [pltpu.SemaphoreType.DMA((GROUPS,))] * 5,
         compiler_params=pltpu.CompilerParams(vmem_limit_bytes=LIMIT),
         cost_estimate=pl.CostEstimate(
             flops=6 * total * width * units,
             bytes_accessed=6 * width * units + 4 * total * width,
             transcendentals=total * units,
         ),
-    )(order, own, moved, other, table, gate_w, up_w, down_w)
+    )(order, moved, gate_w, up_w, down_w)
 
 
 def backward_kernel(*refs):
@@ -515,6 +524,28 @@
     )(sel, home, base)
 
 
+def finish_weighted_kernel(one_n, two_n, ones, twos, home, base, out):
+    blocks, groups, capacity, part = home.shape
+    first = jnp.zeros(base.shape, jnp.float32)
+    second = jnp.zeros(base.shape, jnp.float32)
+    for group in range(groups):
+        rows = home[:, group].reshape(blocks * capacity, part)
+        first = first + product(one_n[...], rows, INNER)
+        second = second + product(two_n[...], rows, INNER)
+    total = base[...].astype(jnp.float32) + first * widen(ones[...], part)
+    out[...] = (total + second * widen(twos[...], part)).astype(jnp.bfloat16)
+
+
+def finish_weighted(one_n, two_n, ones, twos, home, base):
+    return pl.pallas_call(
+        finish_weighted_kernel,
+        out_shape=jax.ShapeDtypeStruct(base.shape, jnp.bfloat16),
+        in_specs=[VMEM] * 6,
+        out_specs=VMEM,
+        compiler_params=pltpu.CompilerParams(vmem_limit_bytes=LIMIT // 2),
+    )(one_n, two_n, ones, twos, home, base)
+
+
 def send_home(pieces):
     experts, hids, capacity, part = pieces.shape
     home = swap(pieces.reshape(experts * hids, capacity, part), BOTH)
@@ -542,23 +573,28 @@
 
     tokens_next = with_table(next_input[0], norm_gain, router[0].T)
     tokens_next, routes = lax.optimization_barrier((tokens_next, (routes_saved[0], routes_next[0])))
-    packed, sel_saved, sel_next = pack(*routes, saved_input[0], cotangent[0], experts, capacity)
+    packed, sel_saved, one_next, two_next = pack(
+        *routes, saved_input[0], cotangent[0], experts, capacity
+    )
     near, packed = gather_near(tokens_next, packed)
     packed = swap(packed, "expert")
-    moved_next, table = spread(sel_next, near + gather_far(near), experts)
+    moved_next, table, ones, twos = spread(
+        routes[1], one_next, two_next, near + gather_far(near), experts
+    )
     moved_next = swap(moved_next, "expert")
     other = packed[:, :, part:]
     near, _ = gather_near(packed[:, :, :part])
     near, moved_next = lax.optimization_barrier((near, moved_next))
     far = gather_far(near)
-    out_next = forward(order, own, moved_next, other, table, gate_w, up_w, down_w)
+    out_next = forward(order, moved_next, gate_w, up_w, down_w)
     far, out_next = lax.optimization_barrier((far, out_next))
     pieces = near + far
     out_home = send_home(out_next)
     back_part = backward(order, own, other, table, gate_w, up_w, down_w, pieces)
+    back_part, out_home = lax.optimization_barrier((back_part, out_home))
     back_home = send_home(back_part)
 
-    forward_out = finish(sel_next, out_home, next_input[0])
+    forward_out = finish_weighted(one_next, two_next, ones, twos, out_home, next_input[0])
     grad_input = finish(sel_saved, back_home, cotangent[0])
 
     first_section = lax.axis_index("section") == 0

time: 221 us -> 222 us (level)
  local copies, waits for them, and re-layouts: 11 us -> 17.5 us
  waiting for transfers between devices: 97.6 us -> 93.8 us
    unnamed x29 -> x49, local copies, waits for them, and re-layouts: 9.65 us -> 15.2 us
    all_to_all x4, waiting for transfers between devices: 48.7 us -> 43.9 us  [swap(): return lax.all_to_all(block, axes, split_axis=0, concat_axis=0, tiled=True)]
    pallas_call x1, Pallas kernels: 20.1 us -> 17.5 us  [forward(): pl.pallas_call(forward_kernel, out_shape=jax.ShapeDtypeStruct(moved.shape...]
  transfers between devices with their start and end apart: 19 -> 19, of which waited for: 10 -> 10; matrix products, arithmetic and copies ran while one was open for 1% -> 1% of each run, Pallas kernels for 26% -> 25%
where the time goes in v5:
time: 222 us; the launch traced here: 221 us
  waiting for transfers between devices  93.8 us (42%)
  Pallas kernels  58.9 us (27%)
  starting transfers between devices  49.2 us (22%)
  local copies, waits for them, and re-layouts  17.5 us (8%)
    ppermute x14, waiting for transfers between devices, shift(): return lax.ppermute(block, 'hid', route)  45.7 us
    all_to_all x4, waiting for transfers between devices, swap(): return lax.all_to_all(block, axes, split_axis=0, concat_axis=0, tiled=True)  43.9 us
    pallas_call x1, Pallas kernels, backward(): pl.pallas_call(backward_kernel, out_shape=jax.ShapeDtypeStruct((blocks, G...  29.9 us
    all_to_all x4, starting transfers between devices, swap(): return lax.all_to_all(block, axes, split_axis=0, concat_axis=0, tiled=True)  28.9 us
    ppermute x14, starting transfers between devices, shift(): return lax.ppermute(block, 'hid', route)  17.7 us
    pallas_call x1, Pallas kernels, forward(): pl.pallas_call(forward_kernel, out_shape=jax.ShapeDtypeStruct(moved.shape...  17.5 us
    unnamed x49, local copies, waits for them, and re-layouts  15.2 us
  transfers between devices with their start and end apart: 19, of which 10 were waited for; matrix products, arithmetic and copies ran while one was open for 1% of the time, Pallas kernels for 25%

profile of v5, /device:TPU:1, one launch (start us, length us, event | category | flops | bytes accessed | tf_op | source)
XLA Modules:
  0.0 221.0 jit_solution(6549597561097353681)
XLA Ops:
  5.1 3.3 %collective-permute-start.2 = (bf16[160,512]{1,0:T(8,128)(2,1)}, bf16[160,512]{1,0:T(8,128)(2,1)S(1)}, u32[]{:S(2)}, u32[]{:S(2)}) collective-permute-start(bf16[160,512]{1,0:T(8,128)(2,1)} %shard_map.113.refs_0_), channel_id=1, source_target_pairs={{0,6},{1,7},{2,0},{3,1},{4,2},{5,3},{6,4},{7,5},{8,14},{9,15},{10,... | collective-permute-start | bytes 491528 | tf_op jit(solution)/shard_map/ppermute | solution.py:49
  9.7 3.0 %shard_map.114 = (bf16[8,96,640]{2,1,0:T(8,128)(2,1)}, bf16[128,384]{1,0:T(8,128)(2,1)}, bf16[128,384]{1,0:T(8,128)(2,1)}, bf16[128,384]{1,0:T(8,128)(2,1)}) custom-call(s32[128,2]{1,0:T(8,128)} %bitcast.36, s32[128,2]{1,0:T(8,128)} %bitcast.28, bf16[128,512]{1,0:T(8,128)(2,1)} %bitcast.37, bf16[128,512]{1,0:T(8,128)(2,1)} %bitcast.32), custom_call_target="tpu_custom_call" | custom-call | tf_op jit(solution)/shard_map/pallas_call | solution.py:157
  12.7 1.9 collective-permute-done.1.refs_2_
  14.6 7.2 %all-to-all-start = ((bf16[8,96,640]{2,1,0:T(8,128)(2,1)}), bf16[8,96,640]{2,1,0:T(8,128)(2,1)S(1)}, u32[]{:S(2)}, u32[]{:S(2)}) async-start(bf16[8,96,640]{2,1,0:T(8,128)(2,1)} %get-tuple-element.37), calls=%async_computation | async-start | bytes 1966080 | tf_op jit(solution)/shard_map/all_to_all | solution.py:40
  23.2 4.3 %collective-permute-done.4.refs_5_ = bf16[160,512]{1,0:T(8,128)(2,1)S(1)} collective-permute-done((bf16[160,512]{1,0:T(8,128)(2,1)S(1)}, bf16[160,512]{1,0:T(8,128)(2,1)S(1)}, u32[]{:S(2)}, u32[]{:S(2)}) %collective-permute-start.4) | collective-permute-done | bytes 163872 | tf_op jit(solution)/shard_map/ppermute | solution.py:49
  27.6 2.7 %collective-permute-start.6 = (bf16[160,512]{1,0:T(8,128)(2,1)S(1)}, bf16[160,512]{1,0:T(8,128)(2,1)S(1)}, u32[]{:S(2)}, u32[]{:S(2)}) collective-permute-start(bf16[160,512]{1,0:T(8,128)(2,1)S(1)} %collective-permute-done.4.refs_5_), channel_id=1, source_target_pairs={{0,6},{1,7},{2,0},{3,1},{4,2},{5,3},{6,4},{7,5},{8,14},{9,15},{10,... | collective-permute-start | bytes 491528 | tf_op jit(solution)/shard_map/ppermute | solution.py:49
  30.2 3.2 %collective-permute-done.5.refs_6_ = bf16[160,512]{1,0:T(8,128)(2,1)S(1)} collective-permute-done((bf16[160,512]{1,0:T(8,128)(2,1)S(1)}, bf16[160,512]{1,0:T(8,128)(2,1)S(1)}, u32[]{:S(2)}, u32[]{:S(2)}) %collective-permute-start.5) | collective-permute-done | bytes 163872 | tf_op jit(solution)/shard_map/ppermute | solution.py:49
  37.0 3.1 %shard_map.115 = (bf16[8,8,48,512]{3,2,1,0:T(8,128)(2,1)}, bf16[8,32,512]{2,1,0:T(8,128)(2,1)S(1)}, f32[128,128]{1,0:T(8,128)S(1)}, f32[128,128]{1,0:T(8,128)S(1)}) custom-call(s32[128,2]{1,0:T(8,128)S(1)} %bitcast.29, bf16[128,384]{1,0:T(8,128)(2,1)S(1)} %copy-done.4, bf16[128,384]{1,0:T(8,128)(2,1)S(1)} %copy-done.6, bf16[160,512]{1,0:T(8,128)(2,1)S(1)} %copy-done, ...), custom_call_target="tpu_custom_call" | custom-call | tf_op jit(solution)/shard_map/pallas_call | solution.py:197
  42.1 5.5 %all-to-all-start.1 = ((bf16[8,8,48,512]{3,2,1,0:T(8,128)(2,1)}), bf16[8,8,48,512]{3,2,1,0:T(8,128)(2,1)}, u32[]{:S(2)}, u32[]{:S(2)}) async-start(bf16[8,8,48,512]{3,2,1,0:T(8,128)(2,1)} %get-tuple-element.47), calls=%async_computation.1 | async-start | bytes 6291456 | tf_op jit(solution)/shard_map/all_to_all | solution.py:40
  47.7 3.5 %collective-permute-start.9 = (bf16[8,96,512]{2,1,0:T(8,128)(2,1)S(1)}, bf16[8,96,512]{2,1,0:T(8,128)(2,1)S(1)}, u32[]{:S(2)}, u32[]{:S(2)}) collective-permute-start(bf16[8,96,512]{2,1,0:T(8,128)(2,1)S(1)} %slice.9.refs_7_), channel_id=1, source_target_pairs={{0,6},{1,7},{2,0},{3,1},{4,2},{5,3},{6,4},{7,5},{8,14},{9,15},{10,... | collective-permute-start | bytes 2359304 | tf_op jit(solution)/shard_map/ppermute | solution.py:49
  52.5 15.5 %collective-permute-done.9.refs_11_ = bf16[8,96,512]{2,1,0:T(8,128)(2,1)S(1)} collective-permute-done((bf16[8,96,512]{2,1,0:T(8,128)(2,1)S(1)}, bf16[8,96,512]{2,1,0:T(8,128)(2,1)S(1)}, u32[]{:S(2)}, u32[]{:S(2)}) %collective-permute-start.9) | collective-permute-done | bytes 786464 | tf_op jit(solution)/shard_map/ppermute | solution.py:49
  68.0 3.2 %collective-permute-done.8.refs_9_ = bf16[8,96,512]{2,1,0:T(8,128)(2,1)S(1)} collective-permute-done((bf16[8,96,512]{2,1,0:T(8,128)(2,1)S(1)}, bf16[8,96,512]{2,1,0:T(8,128)(2,1)S(1)}, u32[]{:S(2)}, u32[]{:S(2)}) %collective-permute-start.8) | collective-permute-done | bytes 786464 | tf_op jit(solution)/shard_map/ppermute | solution.py:49
  73.4 15.8 %collective-permute-done.11.refs_12_ = bf16[8,96,512]{2,1,0:T(8,128)(2,1)S(1)} collective-permute-done((bf16[8,96,512]{2,1,0:T(8,128)(2,1)S(1)}, bf16[8,96,512]{2,1,0:T(8,128)(2,1)S(1)}, u32[]{:S(2)}, u32[]{:S(2)}) %collective-permute-start.11) | collective-permute-done | bytes 786464 | tf_op jit(solution)/shard_map/ppermute | solution.py:49
  89.2 1.8 collective-permute-done.10.refs_10_
  91.0 2.7 %collective-permute-start.13 = (bf16[8,96,512]{2,1,0:T(8,128)(2,1)S(1)}, bf16[8,96,512]{2,1,0:T(8,128)(2,1)S(1)}, u32[]{:S(2)}, u32[]{:S(2)}) collective-permute-start(bf16[8,96,512]{2,1,0:T(8,128)(2,1)S(1)} %collective-permute-done.11.refs_12_), channel_id=1, source_target_pairs={{0,6},{1,7},{2,0},{3,1},{4,2},{5,3},{6,4},{7,5},{8,14},{9,15},{10,... | collective-permute-start | bytes 2359304 | tf_op jit(solution)/shard_map/ppermute | solution.py:49
  93.6 17.5 %shard_map.116 = bf16[8,8,48,512]{3,2,1,0:T(8,128)(2,1)} custom-call(s32[8]{0:T(128)} %stack.35.order.refs_0_, bf16[8,8,48,512]{3,2,1,0:T(8,128)(2,1)} %all-to-all-done.1.moved, bf16[4096,896]{1,0:T(8,128)(2,1)} %bitcast.40, bf16[4096,896]{1,0:T(8,128)(2,1)} %bitcast.42, bf16[896,4096]{1,0:T(8,128)(2,1)} %bitcast.44), custom_call_target="tpu_custom_call" | custom-call | flops 8455716864 | bytes 28311552 | tf_op jit(solution)/shard_map/pallas_call | solution.py:361
  113.1 8.9 %all-to-all-start.2 = ((bf16[64,48,512]{2,1,0:T(8,128)(2,1)}), bf16[64,48,512]{2,1,0:T(8,128)(2,1)S(1)}, u32[]{:S(2)}, u32[]{:S(2)}) async-start(bf16[64,48,512]{2,1,0:T(8,128)(2,1)} %bitcast.35), calls=%async_computation.2 | async-start | bytes 6291456 | tf_op jit(solution)/shard_map/all_to_all | solution.py:40
  123.6 29.9 %shard_map.117 = bf16[8,8,48,512]{3,2,1,0:T(8,128)(2,1)} custom-call(s32[8]{0:T(128)} %stack.35.order.refs_0_, s32[1]{0:T(128)} %bitcast.15.refs_1_, bf16[8,96,128]{2,1,0:T(8,128)(2,1)} %slice.8.refs_2_, bf16[8,32,512]{2,1,0:T(8,128)(2,1)} %copy-done.13, bf16[4096,896]{1,0:T(8,128)(2,1)} %bitcast.41, bf16[4096,896]{1,0:T(8,128)(2,1)} %bitcast.43, ...), custom_call_target="tpu_custom_call" | custom-call | flops 14092861440 | bytes 31457280 | tf_op jit(solution)/shard_map/pallas_call | solution.py:477
  153.5 8.6 %all-to-all-done.2 = bf16[64,48,512]{2,1,0:T(8,128)(2,1)S(1)} async-done(((bf16[64,48,512]{2,1,0:T(8,128)(2,1)}), bf16[64,48,512]{2,1,0:T(8,128)(2,1)S(1)}, u32[]{:S(2)}, u32[]{:S(2)}) %all-to-all-start.2) | async-done | bytes 3145760 | tf_op jit(solution)/shard_map/all_to_all | solution.py:40
  162.1 7.2 %all-to-all-start.3 = ((bf16[64,48,512]{2,1,0:T(8,128)(2,1)}), bf16[64,48,512]{2,1,0:T(8,128)(2,1)}, u32[]{:S(2)}, u32[]{:S(2)}) async-start(bf16[64,48,512]{2,1,0:T(8,128)(2,1)} %bitcast.34), calls=%async_computation.3 | async-start | bytes 6291456 | tf_op jit(solution)/shard_map/all_to_all | solution.py:40
  174.1 35.3 %all-to-all-done.3 = bf16[64,48,512]{2,1,0:T(8,128)(2,1)} async-done(((bf16[64,48,512]{2,1,0:T(8,128)(2,1)}), bf16[64,48,512]{2,1,0:T(8,128)(2,1)}, u32[]{:S(2)}, u32[]{:S(2)}) %all-to-all-start.3) | async-done | bytes 3145760 | tf_op jit(solution)/shard_map/all_to_all | solution.py:40
  210.3 2.6 %shard_map.118 = bf16[128,512]{1,0:T(8,128)(2,1)S(1)} custom-call(bf16[128,384]{1,0:T(8,128)(2,1)S(1)} %copy-done.8, bf16[8,8,48,512]{3,2,1,0:T(8,128)(2,1)} %bitcast.22.home, bf16[128,512]{1,0:T(8,128)(2,1)S(1)} %bitcast.33), custom_call_target="tpu_custom_call" | custom-call | tf_op jit(solution)/shard_map/pallas_call | solution.py:518
  213.6 2.6 %collective-permute-start.14 = (bf16[128,512]{1,0:T(8,128)(2,1)S(1)}, bf16[128,512]{1,0:T(8,128)(2,1)S(1)}, u32[]{:S(2)}, u32[]{:S(2)}) collective-permute-start(bf16[128,512]{1,0:T(8,128)(2,1)S(1)} %get-tuple-element.62), channel_id=1, source_target_pairs={{0,64},{64,0},{1,65},{65,1},{2,66},{66,2},{3,67},{67,3},{4,68},{68... | collective-permute-start | bytes 393224 | tf_op jit(solution)/shard_map/ppermute | solution.py:36
  216.2 4.1 %collective-permute-done.14 = bf16[128,512]{1,0:T(8,128)(2,1)S(1)} collective-permute-done((bf16[128,512]{1,0:T(8,128)(2,1)S(1)}, bf16[128,512]{1,0:T(8,128)(2,1)S(1)}, u32[]{:S(2)}, u32[]{:S(2)}) %collective-permute-start.14) | collective-permute-done | bytes 131104 | tf_op jit(solution)/shard_map/ppermute | solution.py:36
  (74 shorter events, 26.7 us)
Async XLA Ops:
  5.1 7.6 %collective-permute-start.2 = (bf16[160,512]{1,0:T(8,128)(2,1)}, bf16[160,512]{1,0:T(8,128)(2,1)S(1)}, u32[]{:S(2)}, u32[]{:S(2)}) collective-permute-start(bf16[160,512]{1,0:T(8,128)(2,1)} %shard_map.113.refs_0_), channel_id=1, source_target_pairs={{0,6},{1,7},{2,0},{3,1},{4,2},{5,3},{6,4},{7,5},{8,14},{9,15},{10,... | collective-permute-start | bytes 491528 | tf_op jit(solution)/shard_map/ppermute | solution.py:49
  8.4 6.2 %collective-permute-start.1 = (bf16[160,512]{1,0:T(8,128)(2,1)}, bf16[160,512]{1,0:T(8,128)(2,1)S(1)}, u32[]{:S(2)}, u32[]{:S(2)}) collective-permute-start(bf16[160,512]{1,0:T(8,128)(2,1)} %shard_map.113.refs_0_), channel_id=1, source_target_pairs={{0,2},{1,3},{2,4},{3,5},{4,6},{5,7},{6,0},{7,1},{8,10},{9,11},{10,... | collective-permute-start | bytes 491528 | tf_op jit(solution)/shard_map/ppermute | solution.py:49
  8.4 6.2 %collective-permute-start = (bf16[160,512]{1,0:T(8,128)(2,1)}, bf16[160,512]{1,0:T(8,128)(2,1)S(1)}, u32[]{:S(2)}, u32[]{:S(2)}) collective-permute-start(bf16[160,512]{1,0:T(8,128)(2,1)} %shard_map.113.refs_0_), channel_id=1, source_target_pairs={{0,1},{1,0},{2,3},{3,2},{4,5},{5,4},{6,7},{7,6},{8,9},{9,8},{10,11... | collective-permute-start | bytes 491528 | tf_op jit(solution)/shard_map/ppermute | solution.py:49
  14.6 27.6 %all-to-all-start = ((bf16[8,96,640]{2,1,0:T(8,128)(2,1)}), bf16[8,96,640]{2,1,0:T(8,128)(2,1)S(1)}, u32[]{:S(2)}, u32[]{:S(2)}) async-start(bf16[8,96,640]{2,1,0:T(8,128)(2,1)} %get-tuple-element.37), calls=%async_computation | async-start | bytes 1966080 | tf_op jit(solution)/shard_map/all_to_all | solution.py:40
  21.7 5.8 %collective-permute-start.4 = (bf16[160,512]{1,0:T(8,128)(2,1)S(1)}, bf16[160,512]{1,0:T(8,128)(2,1)S(1)}, u32[]{:S(2)}, u32[]{:S(2)}) collective-permute-start(bf16[160,512]{1,0:T(8,128)(2,1)S(1)} %collective-permute-done.refs_1_), channel_id=1, source_target_pairs={{0,6},{1,7},{2,0},{3,1},{4,2},{5,3},{6,4},{7,5},{8,14},{9,15},{10,... | collective-permute-start | bytes 491528 | tf_op jit(solution)/shard_map/ppermute | solution.py:49
  23.2 10.2 %collective-permute-start.3 = (bf16[160,512]{1,0:T(8,128)(2,1)S(1)}, bf16[160,512]{1,0:T(8,128)(2,1)S(1)}, u32[]{:S(2)}, u32[]{:S(2)}) collective-permute-start(bf16[160,512]{1,0:T(8,128)(2,1)S(1)} %collective-permute-done.refs_1_), channel_id=1, source_target_pairs={{0,2},{1,3},{2,4},{3,5},{4,6},{5,7},{6,0},{7,1},{8,10},{9,11},{10,... | collective-permute-start | bytes 491528 | tf_op jit(solution)/shard_map/ppermute | solution.py:49
  23.2 10.2 %collective-permute-start.5 = (bf16[160,512]{1,0:T(8,128)(2,1)S(1)}, bf16[160,512]{1,0:T(8,128)(2,1)S(1)}, u32[]{:S(2)}, u32[]{:S(2)}) collective-permute-start(bf16[160,512]{1,0:T(8,128)(2,1)S(1)} %collective-permute-done.1.refs_2_), channel_id=1, source_target_pairs={{0,2},{1,3},{2,4},{3,5},{4,6},{5,7},{6,0},{7,1},{8,10},{9,11},{10,... | collective-permute-start | bytes 491528 | tf_op jit(solution)/shard_map/ppermute | solution.py:49
  27.6 5.9 %collective-permute-start.6 = (bf16[160,512]{1,0:T(8,128)(2,1)S(1)}, bf16[160,512]{1,0:T(8,128)(2,1)S(1)}, u32[]{:S(2)}, u32[]{:S(2)}) collective-permute-start(bf16[160,512]{1,0:T(8,128)(2,1)S(1)} %collective-permute-done.4.refs_5_), channel_id=1, source_target_pairs={{0,6},{1,7},{2,0},{3,1},{4,2},{5,3},{6,4},{7,5},{8,14},{9,15},{10,... | collective-permute-start | bytes 491528 | tf_op jit(solution)/shard_map/ppermute | solution.py:49
  42.1 48.9 %all-to-all-start.1 = ((bf16[8,8,48,512]{3,2,1,0:T(8,128)(2,1)}), bf16[8,8,48,512]{3,2,1,0:T(8,128)(2,1)}, u32[]{:S(2)}, u32[]{:S(2)}) async-start(bf16[8,8,48,512]{3,2,1,0:T(8,128)(2,1)} %get-tuple-element.47), calls=%async_computation.1 | async-start | bytes 6291456 | tf_op jit(solution)/shard_map/all_to_all | solution.py:40
  47.7 20.3 %collective-permute-start.9 = (bf16[8,96,512]{2,1,0:T(8,128)(2,1)S(1)}, bf16[8,96,512]{2,1,0:T(8,128)(2,1)S(1)}, u32[]{:S(2)}, u32[]{:S(2)}) collective-permute-start(bf16[8,96,512]{2,1,0:T(8,128)(2,1)S(1)} %slice.9.refs_7_), channel_id=1, source_target_pairs={{0,6},{1,7},{2,0},{3,1},{4,2},{5,3},{6,4},{7,5},{8,14},{9,15},{10,... | collective-permute-start | bytes 2359304 | tf_op jit(solution)/shard_map/ppermute | solution.py:49
  51.2 20.0 %collective-permute-start.8 = (bf16[8,96,512]{2,1,0:T(8,128)(2,1)S(1)}, bf16[8,96,512]{2,1,0:T(8,128)(2,1)S(1)}, u32[]{:S(2)}, u32[]{:S(2)}) collective-permute-start(bf16[8,96,512]{2,1,0:T(8,128)(2,1)S(1)} %slice.9.refs_7_), channel_id=1, source_target_pairs={{0,2},{1,3},{2,4},{3,5},{4,6},{5,7},{6,0},{7,1},{8,10},{9,11},{10,... | collective-permute-start | bytes 2359304 | tf_op jit(solution)/shard_map/ppermute | solution.py:49
  51.2 20.0 %collective-permute-start.7 = (bf16[8,96,512]{2,1,0:T(8,128)(2,1)S(1)}, bf16[8,96,512]{2,1,0:T(8,128)(2,1)S(1)}, u32[]{:S(2)}, u32[]{:S(2)}) collective-permute-start(bf16[8,96,512]{2,1,0:T(8,128)(2,1)S(1)} %slice.9.refs_7_), channel_id=1, source_target_pairs={{0,1},{1,0},{2,3},{3,2},{4,5},{5,4},{6,7},{7,6},{8,9},{9,8},{10,11... | collective-permute-start | bytes 2359304 | tf_op jit(solution)/shard_map/ppermute | solution.py:49
  71.2 40.0 %copy-start.17 = (bf16[8,96,512]{2,1,0:T(8,128)(2,1)}, bf16[8,96,512]{2,1,0:T(8,128)(2,1)S(1)}, u32[]{:S(2)}) copy-start(bf16[8,96,512]{2,1,0:T(8,128)(2,1)S(1)} %collective-permute-done.8.refs_9_) | copy-start | bytes 2359300
  71.2 40.0 %copy-start.18 = (bf16[8,96,512]{2,1,0:T(8,128)(2,1)}, bf16[8,96,512]{2,1,0:T(8,128)(2,1)S(1)}, u32[]{:S(2)}) copy-start(bf16[8,96,512]{2,1,0:T(8,128)(2,1)S(1)} %collective-permute-done.7.refs_8_) | copy-start | bytes 2359300
  71.2 17.9 %collective-permute-start.11 = (bf16[8,96,512]{2,1,0:T(8,128)(2,1)S(1)}, bf16[8,96,512]{2,1,0:T(8,128)(2,1)S(1)}, u32[]{:S(2)}, u32[]{:S(2)}) collective-permute-start(bf16[8,96,512]{2,1,0:T(8,128)(2,1)S(1)} %collective-permute-done.7.refs_8_), channel_id=1, source_target_pairs={{0,6},{1,7},{2,0},{3,1},{4,2},{5,3},{6,4},{7,5},{8,14},{9,15},{10,... | collective-permute-start | bytes 2359304 | tf_op jit(solution)/shard_map/ppermute | solution.py:49
  72.4 18.5 %collective-permute-start.10 = (bf16[8,96,512]{2,1,0:T(8,128)(2,1)S(1)}, bf16[8,96,512]{2,1,0:T(8,128)(2,1)S(1)}, u32[]{:S(2)}, u32[]{:S(2)}) collective-permute-start(bf16[8,96,512]{2,1,0:T(8,128)(2,1)S(1)} %collective-permute-done.7.refs_8_), channel_id=1, source_target_pairs={{0,2},{1,3},{2,4},{3,5},{4,6},{5,7},{6,0},{7,1},{8,10},{9,11},{10,... | collective-permute-start | bytes 2359304 | tf_op jit(solution)/shard_map/ppermute | solution.py:49
  89.2 22.0 %copy-start.19 = (bf16[8,96,512]{2,1,0:T(8,128)(2,1)}, bf16[8,96,512]{2,1,0:T(8,128)(2,1)S(1)}, u32[]{:S(2)}) copy-start(bf16[8,96,512]{2,1,0:T(8,128)(2,1)S(1)} %collective-permute-done.11.refs_12_) | copy-start | bytes 2359300
  91.0 20.2 %copy-start.20 = (bf16[8,96,512]{2,1,0:T(8,128)(2,1)}, bf16[8,96,512]{2,1,0:T(8,128)(2,1)S(1)}, u32[]{:S(2)}) copy-start(bf16[8,96,512]{2,1,0:T(8,128)(2,1)S(1)} %collective-permute-done.10.refs_10_) | copy-start | bytes 2359300
  91.0 20.3 %collective-permute-start.12 = (bf16[8,96,512]{2,1,0:T(8,128)(2,1)S(1)}, bf16[8,96,512]{2,1,0:T(8,128)(2,1)S(1)}, u32[]{:S(2)}, u32[]{:S(2)}) collective-permute-start(bf16[8,96,512]{2,1,0:T(8,128)(2,1)S(1)} %collective-permute-done.8.refs_9_), channel_id=1, source_target_pairs={{0,2},{1,3},{2,4},{3,5},{4,6},{5,7},{6,0},{7,1},{8,10},{9,11},{10,... | collective-permute-start | bytes 2359304 | tf_op jit(solution)/shard_map/ppermute | solution.py:49
  91.0 20.3 %collective-permute-start.13 = (bf16[8,96,512]{2,1,0:T(8,128)(2,1)S(1)}, bf16[8,96,512]{2,1,0:T(8,128)(2,1)S(1)}, u32[]{:S(2)}, u32[]{:S(2)}) collective-permute-start(bf16[8,96,512]{2,1,0:T(8,128)(2,1)S(1)} %collective-permute-done.11.refs_12_), channel_id=1, source_target_pairs={{0,6},{1,7},{2,0},{3,1},{4,2},{5,3},{6,4},{7,5},{8,14},{9,15},{10,... | collective-permute-start | bytes 2359304 | tf_op jit(solution)/shard_map/ppermute | solution.py:49
  113.1 49.1 %all-to-all-start.2 = ((bf16[64,48,512]{2,1,0:T(8,128)(2,1)}), bf16[64,48,512]{2,1,0:T(8,128)(2,1)S(1)}, u32[]{:S(2)}, u32[]{:S(2)}) async-start(bf16[64,48,512]{2,1,0:T(8,128)(2,1)} %bitcast.35), calls=%async_computation.2 | async-start | bytes 6291456 | tf_op jit(solution)/shard_map/all_to_all | solution.py:40
  162.1 47.3 %all-to-all-start.3 = ((bf16[64,48,512]{2,1,0:T(8,128)(2,1)}), bf16[64,48,512]{2,1,0:T(8,128)(2,1)}, u32[]{:S(2)}, u32[]{:S(2)}) async-start(bf16[64,48,512]{2,1,0:T(8,128)(2,1)} %bitcast.34), calls=%async_computation.3 | async-start | bytes 6291456 | tf_op jit(solution)/shard_map/all_to_all | solution.py:40
  169.4 40.1 %copy-start.3 = (bf16[1,128,512]{2,1,0:T(8,128)(2,1)S(1)}, bf16[1,128,512]{2,1,0:T(8,128)(2,1)}, u32[]{:S(2)}) copy-start(bf16[1,128,512]{2,1,0:T(8,128)(2,1)} %param.11) | copy-start | bytes 393220
  213.6 6.7 %collective-permute-start.14 = (bf16[128,512]{1,0:T(8,128)(2,1)S(1)}, bf16[128,512]{1,0:T(8,128)(2,1)S(1)}, u32[]{:S(2)}, u32[]{:S(2)}) collective-permute-start(bf16[128,512]{1,0:T(8,128)(2,1)S(1)} %get-tuple-element.62), channel_id=1, source_target_pairs={{0,64},{64,0},{1,65},{65,1},{2,66},{66,2},{3,67},{67,3},{4,68},{68... | collective-permute-start | bytes 393224 | tf_op jit(solution)/shard_map/ppermute | solution.py:36
  (18 other events, 31.2 us)

commit v6 on v5

--- a/solution.py
+++ b/solution.py
@@ -202,9 +202,15 @@
             jax.ShapeDtypeStruct((tokens, 128), jnp.float32),
             jax.ShapeDtypeStruct((tokens, 128), jnp.float32),
         ),
-        in_specs=[VMEM] * (3 + GROUPS),
-        out_specs=(VMEM,) * 4,
-        compiler_params=pltpu.CompilerParams(vmem_limit_bytes=LIMIT // 2),
+        grid=(1,),
+        in_specs=[whole(a.shape) for a in (routes, one_n, two_n)] + [VMEM] * GROUPS,
+        out_specs=(
+            whole((blocks, GROUPS, total // blocks, part)),
+            whole((GROUPS, TABLE, part)),
+            whole((tokens, 128)),
+            whole((tokens, 128)),
+        ),
+        compiler_params=pltpu.CompilerParams(vmem_limit_bytes=MOST),
     )(routes, one_n, two_n, *pieces)
 
 

time: 222 us -> 218 us (0.982)
  local copies, waits for them, and re-layouts: 17.5 us -> 12.8 us
    unnamed x49, local copies, waits for them, and re-layouts: 15.2 us -> 10.4 us
  transfers between devices with their start and end apart: 19 -> 19, of which waited for: 10 -> 10; matrix products, arithmetic and copies ran while one was open for 1% -> 1% of each run, Pallas kernels for 25% -> 26%
where the time goes in v6:
time: 218 us
  waiting for transfers between devices  93.7 us (43%)
  Pallas kernels  60.4 us (28%)
  starting transfers between devices  49.2 us (23%)
  local copies, waits for them, and re-layouts  12.8 us (6%)
    ppermute x14, waiting for transfers between devices, shift(): return lax.ppermute(block, 'hid', route)  45.7 us
    all_to_all x4, waiting for transfers between devices, swap(): return lax.all_to_all(block, axes, split_axis=0, concat_axis=0, tiled=True)  43.9 us
    pallas_call x1, Pallas kernels, backward(): pl.pallas_call(backward_kernel, out_shape=jax.ShapeDtypeStruct((blocks, G...  29.9 us
    all_to_all x4, starting transfers between devices, swap(): return lax.all_to_all(block, axes, split_axis=0, concat_axis=0, tiled=True)  28.9 us
    ppermute x14, starting transfers between devices, shift(): return lax.ppermute(block, 'hid', route)  17.7 us
    pallas_call x1, Pallas kernels, forward(): pl.pallas_call(forward_kernel, out_shape=jax.ShapeDtypeStruct(moved.shape...  17.5 us
    unnamed x49, local copies, waits for them, and re-layouts  10.4 us
    pallas_call x1, Pallas kernels, spread(): pl.pallas_call(spread_kernel, out_shape=(jax.ShapeDtypeStruct((blocks, GR...  4.62 us
  transfers between devices with their start and end apart: 19, of which 10 were waited for; matrix products, arithmetic and copies ran while one was open for 1% of the time, Pallas kernels for 26%

profile of v6, /device:TPU:1, one launch (start us, length us, event | category | flops | bytes accessed | tf_op | source)
XLA Modules:
  0.0 217.7 jit_solution(4705851127836694982)
XLA Ops:
  5.1 3.3 %collective-permute-start.2 = (bf16[160,512]{1,0:T(8,128)(2,1)}, bf16[160,512]{1,0:T(8,128)(2,1)S(1)}, u32[]{:S(2)}, u32[]{:S(2)}) collective-permute-start(bf16[160,512]{1,0:T(8,128)(2,1)} %shard_map.113.refs_0_), channel_id=1, source_target_pairs={{0,6},{1,7},{2,0},{3,1},{4,2},{5,3},{6,4},{7,5},{8,14},{9,15},{10,... | collective-permute-start | bytes 491528 | tf_op jit(solution)/shard_map/ppermute | solution.py:49
  9.7 3.0 %shard_map.114 = (bf16[8,96,640]{2,1,0:T(8,128)(2,1)}, bf16[128,384]{1,0:T(8,128)(2,1)}, bf16[128,384]{1,0:T(8,128)(2,1)}, bf16[128,384]{1,0:T(8,128)(2,1)}) custom-call(s32[128,2]{1,0:T(8,128)} %bitcast.36, s32[128,2]{1,0:T(8,128)} %bitcast.34, bf16[128,512]{1,0:T(8,128)(2,1)} %bitcast.37, bf16[128,512]{1,0:T(8,128)(2,1)} %bitcast.30), custom_call_target="tpu_custom_call" | custom-call | tf_op jit(solution)/shard_map/pallas_call | solution.py:157
  12.6 1.9 collective-permute-done.1.refs_2_
  14.6 7.2 %all-to-all-start = ((bf16[8,96,640]{2,1,0:T(8,128)(2,1)}), bf16[8,96,640]{2,1,0:T(8,128)(2,1)S(1)}, u32[]{:S(2)}, u32[]{:S(2)}) async-start(bf16[8,96,640]{2,1,0:T(8,128)(2,1)} %get-tuple-element.37), calls=%async_computation | async-start | bytes 1966080 | tf_op jit(solution)/shard_map/all_to_all | solution.py:40
  23.2 4.3 %collective-permute-done.4.refs_5_ = bf16[160,512]{1,0:T(8,128)(2,1)S(1)} collective-permute-done((bf16[160,512]{1,0:T(8,128)(2,1)S(1)}, bf16[160,512]{1,0:T(8,128)(2,1)S(1)}, u32[]{:S(2)}, u32[]{:S(2)}) %collective-permute-start.4) | collective-permute-done | bytes 163872 | tf_op jit(solution)/shard_map/ppermute | solution.py:49
  27.6 2.7 %collective-permute-start.6 = (bf16[160,512]{1,0:T(8,128)(2,1)S(1)}, bf16[160,512]{1,0:T(8,128)(2,1)S(1)}, u32[]{:S(2)}, u32[]{:S(2)}) collective-permute-start(bf16[160,512]{1,0:T(8,128)(2,1)S(1)} %collective-permute-done.4.refs_5_), channel_id=1, source_target_pairs={{0,6},{1,7},{2,0},{3,1},{4,2},{5,3},{6,4},{7,5},{8,14},{9,15},{10,... | collective-permute-start | bytes 491528 | tf_op jit(solution)/shard_map/ppermute | solution.py:49
  30.2 3.2 %collective-permute-done.5.refs_6_ = bf16[160,512]{1,0:T(8,128)(2,1)S(1)} collective-permute-done((bf16[160,512]{1,0:T(8,128)(2,1)S(1)}, bf16[160,512]{1,0:T(8,128)(2,1)S(1)}, u32[]{:S(2)}, u32[]{:S(2)}) %collective-permute-start.5) | collective-permute-done | bytes 163872 | tf_op jit(solution)/shard_map/ppermute | solution.py:49
  34.2 4.6 %shard_map.115 = (bf16[8,8,48,512]{3,2,1,0:T(8,128)(2,1)}, bf16[8,32,512]{2,1,0:T(8,128)(2,1)}, f32[128,128]{1,0:T(8,128)}, f32[128,128]{1,0:T(8,128)}) custom-call(s32[128,2]{1,0:T(8,128)} %bitcast.35, bf16[128,384]{1,0:T(8,128)(2,1)} %get-tuple-element.38.one_n, bf16[128,384]{1,0:T(8,128)(2,1)} %get-tuple-element.39.two_n, ...), custom_call_target="tpu_custom_call" | custom-call | tf_op jit(solution)/shard_map/pallas_call | solution.py:197
  38.9 5.6 %all-to-all-start.1 = ((bf16[8,8,48,512]{3,2,1,0:T(8,128)(2,1)}), bf16[8,8,48,512]{3,2,1,0:T(8,128)(2,1)}, u32[]{:S(2)}, u32[]{:S(2)}) async-start(bf16[8,8,48,512]{3,2,1,0:T(8,128)(2,1)} %get-tuple-element.47), calls=%async_computation.1 | async-start | bytes 6291456 | tf_op jit(solution)/shard_map/all_to_all | solution.py:40
  44.5 3.4 %collective-permute-start.9 = (bf16[8,96,512]{2,1,0:T(8,128)(2,1)S(1)}, bf16[8,96,512]{2,1,0:T(8,128)(2,1)S(1)}, u32[]{:S(2)}, u32[]{:S(2)}) collective-permute-start(bf16[8,96,512]{2,1,0:T(8,128)(2,1)S(1)} %slice.9.refs_7_), channel_id=1, source_target_pairs={{0,6},{1,7},{2,0},{3,1},{4,2},{5,3},{6,4},{7,5},{8,14},{9,15},{10,... | collective-permute-start | bytes 2359304 | tf_op jit(solution)/shard_map/ppermute | solution.py:49
  49.2 15.5 %collective-permute-done.9.refs_11_ = bf16[8,96,512]{2,1,0:T(8,128)(2,1)S(1)} collective-permute-done((bf16[8,96,512]{2,1,0:T(8,128)(2,1)S(1)}, bf16[8,96,512]{2,1,0:T(8,128)(2,1)S(1)}, u32[]{:S(2)}, u32[]{:S(2)}) %collective-permute-start.9) | collective-permute-done | bytes 786464 | tf_op jit(solution)/shard_map/ppermute | solution.py:49
  64.7 3.2 %collective-permute-done.8.refs_9_ = bf16[8,96,512]{2,1,0:T(8,128)(2,1)S(1)} collective-permute-done((bf16[8,96,512]{2,1,0:T(8,128)(2,1)S(1)}, bf16[8,96,512]{2,1,0:T(8,128)(2,1)S(1)}, u32[]{:S(2)}, u32[]{:S(2)}) %collective-permute-start.8) | collective-permute-done | bytes 786464 | tf_op jit(solution)/shard_map/ppermute | solution.py:49
  70.1 15.7 %collective-permute-done.11.refs_12_ = bf16[8,96,512]{2,1,0:T(8,128)(2,1)S(1)} collective-permute-done((bf16[8,96,512]{2,1,0:T(8,128)(2,1)S(1)}, bf16[8,96,512]{2,1,0:T(8,128)(2,1)S(1)}, u32[]{:S(2)}, u32[]{:S(2)}) %collective-permute-start.11) | collective-permute-done | bytes 786464 | tf_op jit(solution)/shard_map/ppermute | solution.py:49
  85.9 1.8 collective-permute-done.10.refs_10_
  87.6 2.7 %collective-permute-start.13 = (bf16[8,96,512]{2,1,0:T(8,128)(2,1)S(1)}, bf16[8,96,512]{2,1,0:T(8,128)(2,1)S(1)}, u32[]{:S(2)}, u32[]{:S(2)}) collective-permute-start(bf16[8,96,512]{2,1,0:T(8,128)(2,1)S(1)} %collective-permute-done.11.refs_12_), channel_id=1, source_target_pairs={{0,6},{1,7},{2,0},{3,1},{4,2},{5,3},{6,4},{7,5},{8,14},{9,15},{10,... | collective-permute-start | bytes 2359304 | tf_op jit(solution)/shard_map/ppermute | solution.py:49
  90.3 17.5 %shard_map.116 = bf16[8,8,48,512]{3,2,1,0:T(8,128)(2,1)} custom-call(s32[8]{0:T(128)} %stack.35.order.refs_0_, bf16[8,8,48,512]{3,2,1,0:T(8,128)(2,1)} %all-to-all-done.1.moved, bf16[4096,896]{1,0:T(8,128)(2,1)} %bitcast.40, bf16[4096,896]{1,0:T(8,128)(2,1)} %bitcast.42, bf16[896,4096]{1,0:T(8,128)(2,1)} %bitcast.44), custom_call_target="tpu_custom_call" | custom-call | flops 8455716864 | bytes 28311552 | tf_op jit(solution)/shard_map/pallas_call | solution.py:367
  109.7 9.0 %all-to-all-start.2 = ((bf16[64,48,512]{2,1,0:T(8,128)(2,1)}), bf16[64,48,512]{2,1,0:T(8,128)(2,1)S(1)}, u32[]{:S(2)}, u32[]{:S(2)}) async-start(bf16[64,48,512]{2,1,0:T(8,128)(2,1)} %bitcast.33), calls=%async_computation.2 | async-start | bytes 6291456 | tf_op jit(solution)/shard_map/all_to_all | solution.py:40
  120.3 29.9 %shard_map.117 = bf16[8,8,48,512]{3,2,1,0:T(8,128)(2,1)} custom-call(s32[8]{0:T(128)} %stack.35.order.refs_0_, s32[1]{0:T(128)} %bitcast.15.refs_1_, bf16[8,96,128]{2,1,0:T(8,128)(2,1)} %slice.8.refs_2_, bf16[8,32,512]{2,1,0:T(8,128)(2,1)} %get-tuple-element.43.refs_3_, bf16[4096,896]{1,0:T(8,128)(2,1)} %bitcast.41, bf16[4096,896]{1,0:T(8,128)(2,1)} %bitcast.43, ...), custom_call_target="tpu_custom_call" | custom-call | flops 14092861440 | bytes 31457280 | tf_op jit(solution)/shard_map/pallas_call | solution.py:483
  150.2 8.6 %all-to-all-done.2 = bf16[64,48,512]{2,1,0:T(8,128)(2,1)S(1)} async-done(((bf16[64,48,512]{2,1,0:T(8,128)(2,1)}), bf16[64,48,512]{2,1,0:T(8,128)(2,1)S(1)}, u32[]{:S(2)}, u32[]{:S(2)}) %all-to-all-start.2) | async-done | bytes 3145760 | tf_op jit(solution)/shard_map/all_to_all | solution.py:40
  158.8 7.2 %all-to-all-start.3 = ((bf16[64,48,512]{2,1,0:T(8,128)(2,1)}), bf16[64,48,512]{2,1,0:T(8,128)(2,1)}, u32[]{:S(2)}, u32[]{:S(2)}) async-start(bf16[64,48,512]{2,1,0:T(8,128)(2,1)} %bitcast.32), calls=%async_computation.3 | async-start | bytes 6291456 | tf_op jit(solution)/shard_map/all_to_all | solution.py:40
  170.8 35.3 %all-to-all-done.3 = bf16[64,48,512]{2,1,0:T(8,128)(2,1)} async-done(((bf16[64,48,512]{2,1,0:T(8,128)(2,1)}), bf16[64,48,512]{2,1,0:T(8,128)(2,1)}, u32[]{:S(2)}, u32[]{:S(2)}) %all-to-all-start.3) | async-done | bytes 3145760 | tf_op jit(solution)/shard_map/all_to_all | solution.py:40
  207.0 2.6 %shard_map.118 = bf16[128,512]{1,0:T(8,128)(2,1)S(1)} custom-call(bf16[128,384]{1,0:T(8,128)(2,1)S(1)} %copy-done.4, bf16[8,8,48,512]{3,2,1,0:T(8,128)(2,1)} %bitcast.22.home, bf16[128,512]{1,0:T(8,128)(2,1)S(1)} %bitcast.31), custom_call_target="tpu_custom_call" | custom-call | tf_op jit(solution)/shard_map/pallas_call | solution.py:524
  210.3 2.6 %collective-permute-start.14 = (bf16[128,512]{1,0:T(8,128)(2,1)S(1)}, bf16[128,512]{1,0:T(8,128)(2,1)S(1)}, u32[]{:S(2)}, u32[]{:S(2)}) collective-permute-start(bf16[128,512]{1,0:T(8,128)(2,1)S(1)} %get-tuple-element.62), channel_id=1, source_target_pairs={{0,64},{64,0},{1,65},{65,1},{2,66},{66,2},{3,67},{67,3},{4,68},{68... | collective-permute-start | bytes 393224 | tf_op jit(solution)/shard_map/ppermute | solution.py:36
  212.9 4.1 %collective-permute-done.14 = bf16[128,512]{1,0:T(8,128)(2,1)S(1)} collective-permute-done((bf16[128,512]{1,0:T(8,128)(2,1)S(1)}, bf16[128,512]{1,0:T(8,128)(2,1)S(1)}, u32[]{:S(2)}, u32[]{:S(2)}) %collective-permute-start.14) | collective-permute-done | bytes 131104 | tf_op jit(solution)/shard_map/ppermute | solution.py:36
  (74 shorter events, 22.0 us)
Async XLA Ops:
  5.1 7.6 %collective-permute-start.2 = (bf16[160,512]{1,0:T(8,128)(2,1)}, bf16[160,512]{1,0:T(8,128)(2,1)S(1)}, u32[]{:S(2)}, u32[]{:S(2)}) collective-permute-start(bf16[160,512]{1,0:T(8,128)(2,1)} %shard_map.113.refs_0_), channel_id=1, source_target_pairs={{0,6},{1,7},{2,0},{3,1},{4,2},{5,3},{6,4},{7,5},{8,14},{9,15},{10,... | collective-permute-start | bytes 491528 | tf_op jit(solution)/shard_map/ppermute | solution.py:49
  8.4 6.2 %collective-permute-start.1 = (bf16[160,512]{1,0:T(8,128)(2,1)}, bf16[160,512]{1,0:T(8,128)(2,1)S(1)}, u32[]{:S(2)}, u32[]{:S(2)}) collective-permute-start(bf16[160,512]{1,0:T(8,128)(2,1)} %shard_map.113.refs_0_), channel_id=1, source_target_pairs={{0,2},{1,3},{2,4},{3,5},{4,6},{5,7},{6,0},{7,1},{8,10},{9,11},{10,... | collective-permute-start | bytes 491528 | tf_op jit(solution)/shard_map/ppermute | solution.py:49
  8.4 6.2 %collective-permute-start = (bf16[160,512]{1,0:T(8,128)(2,1)}, bf16[160,512]{1,0:T(8,128)(2,1)S(1)}, u32[]{:S(2)}, u32[]{:S(2)}) collective-permute-start(bf16[160,512]{1,0:T(8,128)(2,1)} %shard_map.113.refs_0_), channel_id=1, source_target_pairs={{0,1},{1,0},{2,3},{3,2},{4,5},{5,4},{6,7},{7,6},{8,9},{9,8},{10,11... | collective-permute-start | bytes 491528 | tf_op jit(solution)/shard_map/ppermute | solution.py:49
  12.6 20.8 %copy-start.9 = (bf16[160,512]{1,0:T(8,128)(2,1)}, bf16[160,512]{1,0:T(8,128)(2,1)S(1)}, u32[]{:S(2)}) copy-start(bf16[160,512]{1,0:T(8,128)(2,1)S(1)} %collective-permute-done.2.refs_4_) | copy-start | bytes 491524
  14.6 24.3 %all-to-all-start = ((bf16[8,96,640]{2,1,0:T(8,128)(2,1)}), bf16[8,96,640]{2,1,0:T(8,128)(2,1)S(1)}, u32[]{:S(2)}, u32[]{:S(2)}) async-start(bf16[8,96,640]{2,1,0:T(8,128)(2,1)} %get-tuple-element.37), calls=%async_computation | async-start | bytes 1966080 | tf_op jit(solution)/shard_map/all_to_all | solution.py:40
  21.7 5.8 %collective-permute-start.4 = (bf16[160,512]{1,0:T(8,128)(2,1)S(1)}, bf16[160,512]{1,0:T(8,128)(2,1)S(1)}, u32[]{:S(2)}, u32[]{:S(2)}) collective-permute-start(bf16[160,512]{1,0:T(8,128)(2,1)S(1)} %collective-permute-done.refs_1_), channel_id=1, source_target_pairs={{0,6},{1,7},{2,0},{3,1},{4,2},{5,3},{6,4},{7,5},{8,14},{9,15},{10,... | collective-permute-start | bytes 491528 | tf_op jit(solution)/shard_map/ppermute | solution.py:49
  23.2 10.2 %collective-permute-start.3 = (bf16[160,512]{1,0:T(8,128)(2,1)S(1)}, bf16[160,512]{1,0:T(8,128)(2,1)S(1)}, u32[]{:S(2)}, u32[]{:S(2)}) collective-permute-start(bf16[160,512]{1,0:T(8,128)(2,1)S(1)} %collective-permute-done.refs_1_), channel_id=1, source_target_pairs={{0,2},{1,3},{2,4},{3,5},{4,6},{5,7},{6,0},{7,1},{8,10},{9,11},{10,... | collective-permute-start | bytes 491528 | tf_op jit(solution)/shard_map/ppermute | solution.py:49
  23.2 10.2 %collective-permute-start.5 = (bf16[160,512]{1,0:T(8,128)(2,1)S(1)}, bf16[160,512]{1,0:T(8,128)(2,1)S(1)}, u32[]{:S(2)}, u32[]{:S(2)}) collective-permute-start(bf16[160,512]{1,0:T(8,128)(2,1)S(1)} %collective-permute-done.1.refs_2_), channel_id=1, source_target_pairs={{0,2},{1,3},{2,4},{3,5},{4,6},{5,7},{6,0},{7,1},{8,10},{9,11},{10,... | collective-permute-start | bytes 491528 | tf_op jit(solution)/shard_map/ppermute | solution.py:49
  27.6 5.9 %collective-permute-start.6 = (bf16[160,512]{1,0:T(8,128)(2,1)S(1)}, bf16[160,512]{1,0:T(8,128)(2,1)S(1)}, u32[]{:S(2)}, u32[]{:S(2)}) collective-permute-start(bf16[160,512]{1,0:T(8,128)(2,1)S(1)} %collective-permute-done.4.refs_5_), channel_id=1, source_target_pairs={{0,6},{1,7},{2,0},{3,1},{4,2},{5,3},{6,4},{7,5},{8,14},{9,15},{10,... | collective-permute-start | bytes 491528 | tf_op jit(solution)/shard_map/ppermute | solution.py:49
  38.9 48.8 %all-to-all-start.1 = ((bf16[8,8,48,512]{3,2,1,0:T(8,128)(2,1)}), bf16[8,8,48,512]{3,2,1,0:T(8,128)(2,1)}, u32[]{:S(2)}, u32[]{:S(2)}) async-start(bf16[8,8,48,512]{3,2,1,0:T(8,128)(2,1)} %get-tuple-element.47), calls=%async_computation.1 | async-start | bytes 6291456 | tf_op jit(solution)/shard_map/all_to_all | solution.py:40
  44.5 20.2 %collective-permute-start.9 = (bf16[8,96,512]{2,1,0:T(8,128)(2,1)S(1)}, bf16[8,96,512]{2,1,0:T(8,128)(2,1)S(1)}, u32[]{:S(2)}, u32[]{:S(2)}) collective-permute-start(bf16[8,96,512]{2,1,0:T(8,128)(2,1)S(1)} %slice.9.refs_7_), channel_id=1, source_target_pairs={{0,6},{1,7},{2,0},{3,1},{4,2},{5,3},{6,4},{7,5},{8,14},{9,15},{10,... | collective-permute-start | bytes 2359304 | tf_op jit(solution)/shard_map/ppermute | solution.py:49
  47.9 20.0 %collective-permute-start.8 = (bf16[8,96,512]{2,1,0:T(8,128)(2,1)S(1)}, bf16[8,96,512]{2,1,0:T(8,128)(2,1)S(1)}, u32[]{:S(2)}, u32[]{:S(2)}) collective-permute-start(bf16[8,96,512]{2,1,0:T(8,128)(2,1)S(1)} %slice.9.refs_7_), channel_id=1, source_target_pairs={{0,2},{1,3},{2,4},{3,5},{4,6},{5,7},{6,0},{7,1},{8,10},{9,11},{10,... | collective-permute-start | bytes 2359304 | tf_op jit(solution)/shard_map/ppermute | solution.py:49
  47.9 20.0 %collective-permute-start.7 = (bf16[8,96,512]{2,1,0:T(8,128)(2,1)S(1)}, bf16[8,96,512]{2,1,0:T(8,128)(2,1)S(1)}, u32[]{:S(2)}, u32[]{:S(2)}) collective-permute-start(bf16[8,96,512]{2,1,0:T(8,128)(2,1)S(1)} %slice.9.refs_7_), channel_id=1, source_target_pairs={{0,1},{1,0},{2,3},{3,2},{4,5},{5,4},{6,7},{7,6},{8,9},{9,8},{10,11... | collective-permute-start | bytes 2359304 | tf_op jit(solution)/shard_map/ppermute | solution.py:49
  67.9 40.0 %copy-start.17 = (bf16[8,96,512]{2,1,0:T(8,128)(2,1)}, bf16[8,96,512]{2,1,0:T(8,128)(2,1)S(1)}, u32[]{:S(2)}) copy-start(bf16[8,96,512]{2,1,0:T(8,128)(2,1)S(1)} %collective-permute-done.8.refs_9_) | copy-start | bytes 2359300
  67.9 40.0 %copy-start.18 = (bf16[8,96,512]{2,1,0:T(8,128)(2,1)}, bf16[8,96,512]{2,1,0:T(8,128)(2,1)S(1)}, u32[]{:S(2)}) copy-start(bf16[8,96,512]{2,1,0:T(8,128)(2,1)S(1)} %collective-permute-done.7.refs_8_) | copy-start | bytes 2359300
  67.9 17.9 %collective-permute-start.11 = (bf16[8,96,512]{2,1,0:T(8,128)(2,1)S(1)}, bf16[8,96,512]{2,1,0:T(8,128)(2,1)S(1)}, u32[]{:S(2)}, u32[]{:S(2)}) collective-permute-start(bf16[8,96,512]{2,1,0:T(8,128)(2,1)S(1)} %collective-permute-done.7.refs_8_), channel_id=1, source_target_pairs={{0,6},{1,7},{2,0},{3,1},{4,2},{5,3},{6,4},{7,5},{8,14},{9,15},{10,... | collective-permute-start | bytes 2359304 | tf_op jit(solution)/shard_map/ppermute | solution.py:49
  69.1 18.5 %collective-permute-start.10 = (bf16[8,96,512]{2,1,0:T(8,128)(2,1)S(1)}, bf16[8,96,512]{2,1,0:T(8,128)(2,1)S(1)}, u32[]{:S(2)}, u32[]{:S(2)}) collective-permute-start(bf16[8,96,512]{2,1,0:T(8,128)(2,1)S(1)} %collective-permute-done.7.refs_8_), channel_id=1, source_target_pairs={{0,2},{1,3},{2,4},{3,5},{4,6},{5,7},{6,0},{7,1},{8,10},{9,11},{10,... | collective-permute-start | bytes 2359304 | tf_op jit(solution)/shard_map/ppermute | solution.py:49
  85.9 22.0 %copy-start.19 = (bf16[8,96,512]{2,1,0:T(8,128)(2,1)}, bf16[8,96,512]{2,1,0:T(8,128)(2,1)S(1)}, u32[]{:S(2)}) copy-start(bf16[8,96,512]{2,1,0:T(8,128)(2,1)S(1)} %collective-permute-done.11.refs_12_) | copy-start | bytes 2359300
  87.6 20.3 %collective-permute-start.12 = (bf16[8,96,512]{2,1,0:T(8,128)(2,1)S(1)}, bf16[8,96,512]{2,1,0:T(8,128)(2,1)S(1)}, u32[]{:S(2)}, u32[]{:S(2)}) collective-permute-start(bf16[8,96,512]{2,1,0:T(8,128)(2,1)S(1)} %collective-permute-done.8.refs_9_), channel_id=1, source_target_pairs={{0,2},{1,3},{2,4},{3,5},{4,6},{5,7},{6,0},{7,1},{8,10},{9,11},{10,... | collective-permute-start | bytes 2359304 | tf_op jit(solution)/shard_map/ppermute | solution.py:49
  87.6 20.3 %collective-permute-start.13 = (bf16[8,96,512]{2,1,0:T(8,128)(2,1)S(1)}, bf16[8,96,512]{2,1,0:T(8,128)(2,1)S(1)}, u32[]{:S(2)}, u32[]{:S(2)}) collective-permute-start(bf16[8,96,512]{2,1,0:T(8,128)(2,1)S(1)} %collective-permute-done.11.refs_12_), channel_id=1, source_target_pairs={{0,6},{1,7},{2,0},{3,1},{4,2},{5,3},{6,4},{7,5},{8,14},{9,15},{10,... | collective-permute-start | bytes 2359304 | tf_op jit(solution)/shard_map/ppermute | solution.py:49
  109.7 49.1 %all-to-all-start.2 = ((bf16[64,48,512]{2,1,0:T(8,128)(2,1)}), bf16[64,48,512]{2,1,0:T(8,128)(2,1)S(1)}, u32[]{:S(2)}, u32[]{:S(2)}) async-start(bf16[64,48,512]{2,1,0:T(8,128)(2,1)} %bitcast.33), calls=%async_computation.2 | async-start | bytes 6291456 | tf_op jit(solution)/shard_map/all_to_all | solution.py:40
  158.8 47.3 %all-to-all-start.3 = ((bf16[64,48,512]{2,1,0:T(8,128)(2,1)}), bf16[64,48,512]{2,1,0:T(8,128)(2,1)}, u32[]{:S(2)}, u32[]{:S(2)}) async-start(bf16[64,48,512]{2,1,0:T(8,128)(2,1)} %bitcast.32), calls=%async_computation.3 | async-start | bytes 6291456 | tf_op jit(solution)/shard_map/all_to_all | solution.py:40
  166.0 40.1 %copy-start.1 = (bf16[1,128,512]{2,1,0:T(8,128)(2,1)S(1)}, bf16[1,128,512]{2,1,0:T(8,128)(2,1)}, u32[]{:S(2)}) copy-start(bf16[1,128,512]{2,1,0:T(8,128)(2,1)} %param.11) | copy-start | bytes 393220
  210.3 6.7 %collective-permute-start.14 = (bf16[128,512]{1,0:T(8,128)(2,1)S(1)}, bf16[128,512]{1,0:T(8,128)(2,1)S(1)}, u32[]{:S(2)}, u32[]{:S(2)}) collective-permute-start(bf16[128,512]{1,0:T(8,128)(2,1)S(1)} %get-tuple-element.62), channel_id=1, source_target_pairs={{0,64},{64,0},{1,65},{65,1},{2,66},{66,2},{3,67},{67,3},{4,68},{68... | collective-permute-start | bytes 393224 | tf_op jit(solution)/shard_map/ppermute | solution.py:36
  (18 other events, 91.8 us)

commit v7 on v6

--- a/solution.py
+++ b/solution.py
@@ -109,6 +109,14 @@
     )(upcoming, gain, router)
 
 
+def column(row, number):
+    width = row.shape[1]
+    down = lax.broadcasted_iota(jnp.int32, (width, width), 0)
+    across = lax.broadcasted_iota(jnp.int32, (width, width), 1)
+    values = row[number : number + 1, :].astype(jnp.float32)
+    return jnp.sum(jnp.where(down == across, values, 0.0), axis=1, keepdims=True).astype(jnp.int32)
+
+
 def pack_kernel(experts, capacity, routes_s, routes_n, saved, cot, packed, sel_s, one_n, two_n):
     tokens, part = saved.shape
     row = lax.broadcasted_iota(jnp.int32, (tokens, tokens), 0)
@@ -119,7 +127,7 @@
 
     def select(routes):
         ids = routes[...]
-        one, two = ids[:, 0:1], ids[:, 1:2]
+        one, two = column(ids, 0), column(ids, 1)
         hit_one = jnp.where(wide == one, 1.0, 0.0)
         hit_two = jnp.where(wide == two, 1.0, 0.0)
         counts = product(earlier, (hit_one + hit_two).astype(jnp.bfloat16), INNER)
@@ -178,8 +186,8 @@
     scale = lax.rsqrt(even(total) / (GROUPS * part) + EPSILON)
     ids = routes[...]
     place = lax.broadcasted_iota(jnp.int32, (tokens, TABLE), 1)
-    first = jnp.where((place < 24) & (lax.rem(place, 8) == ids[:, 0:1]), 1.0, 0.0)
-    second = jnp.where((place < 24) & (lax.rem(place, 8) == ids[:, 1:2]), 1.0, 0.0)
+    first = jnp.where((place < 24) & (lax.rem(place, 8) == column(ids, 0)), 1.0, 0.0)
+    second = jnp.where((place < 24) & (lax.rem(place, 8) == column(ids, 1)), 1.0, 0.0)
     diff = even(logits * (first - second)) * scale
     ones[...] = jax.nn.sigmoid(diff)
     twos[...] = jax.nn.sigmoid(-diff)
@@ -578,7 +586,7 @@
     order = arrival_order()
 
     tokens_next = with_table(next_input[0], norm_gain, router[0].T)
-    tokens_next, routes = lax.optimization_barrier((tokens_next, (routes_saved[0], routes_next[0])))
+    tokens_next, routes = lax.optimization_barrier((tokens_next, (routes_saved[0].T, routes_next[0].T)))
     packed, sel_saved, one_next, two_next = pack(
         *routes, saved_input[0], cotangent[0], experts, capacity
     )

time: 218 us -> 216 us (level)
  local copies, waits for them, and re-layouts: 12.8 us -> 9.95 us
    unnamed x49 -> x47, local copies, waits for them, and re-layouts: 10.4 us -> 7.62 us
where the time goes in v7:
time: 216 us; the launch traced here: 215 us
  waiting for transfers between devices  93.8 us (43%)
  Pallas kernels  60.3 us (28%)
  starting transfers between devices  49.2 us (23%)
  local copies, waits for them, and re-layouts  9.95 us (5%)
    ppermute x14, waiting for transfers between devices, shift(): return lax.ppermute(block, 'hid', route)  45.8 us
    all_to_all x4, waiting for transfers between devices, swap(): return lax.all_to_all(block, axes, split_axis=0, concat_axis=0, tiled=True)  43.9 us
    pallas_call x1, Pallas kernels, backward(): pl.pallas_call(backward_kernel, out_shape=jax.ShapeDtypeStruct((blocks, G...  29.9 us
    all_to_all x4, starting transfers between devices, swap(): return lax.all_to_all(block, axes, split_axis=0, concat_axis=0, tiled=True)  28.9 us
    ppermute x14, starting transfers between devices, shift(): return lax.ppermute(block, 'hid', route)  17.7 us
    pallas_call x1, Pallas kernels, forward(): pl.pallas_call(forward_kernel, out_shape=jax.ShapeDtypeStruct(moved.shape...  17.5 us
    unnamed x47, local copies, waits for them, and re-layouts  7.62 us
    pallas_call x1, Pallas kernels, spread(): pl.pallas_call(spread_kernel, out_shape=(jax.ShapeDtypeStruct((blocks, GR...  4.62 us
  transfers between devices with their start and end apart: 19, of which 10 were waited for; matrix products, arithmetic and copies ran while one was open for 1% of the time, Pallas kernels for 26%

profile of v7, /device:TPU:1, one launch (start us, length us, event | category | flops | bytes accessed | tf_op | source)
XLA Modules:
  0.0 214.8 jit_solution(15712431437771441589)
XLA Ops:
  2.2 3.3 %collective-permute-start.2 = (bf16[160,512]{1,0:T(8,128)(2,1)}, bf16[160,512]{1,0:T(8,128)(2,1)S(1)}, u32[]{:S(2)}, u32[]{:S(2)}) collective-permute-start(bf16[160,512]{1,0:T(8,128)(2,1)} %shard_map.113.refs_0_), channel_id=1, source_target_pairs={{0,6},{1,7},{2,0},{3,1},{4,2},{5,3},{6,4},{7,5},{8,14},{9,15},{10,... | collective-permute-start | bytes 491528 | tf_op jit(solution)/shard_map/ppermute | solution.py:49
  6.9 2.8 %shard_map.114 = (bf16[8,96,640]{2,1,0:T(8,128)(2,1)}, bf16[128,384]{1,0:T(8,128)(2,1)}, bf16[128,384]{1,0:T(8,128)(2,1)}, bf16[128,384]{1,0:T(8,128)(2,1)}) custom-call(s32[2,128]{1,0:T(2,128)} %bitcast.43, s32[2,128]{1,0:T(2,128)} %bitcast.41, bf16[128,512]{1,0:T(8,128)(2,1)} %bitcast.38, bf16[128,512]{1,0:T(8,128)(2,1)} %bitcast.34), custom_call_target="tpu_custom_call" | custom-call | tf_op jit(solution)/shard_map/pallas_call | solution.py:165
  9.7 2.1 collective-permute-done.1.refs_2_
  11.7 7.2 %all-to-all-start = ((bf16[8,96,640]{2,1,0:T(8,128)(2,1)}), bf16[8,96,640]{2,1,0:T(8,128)(2,1)S(1)}, u32[]{:S(2)}, u32[]{:S(2)}) async-start(bf16[8,96,640]{2,1,0:T(8,128)(2,1)} %get-tuple-element.37), calls=%async_computation | async-start | bytes 1966080 | tf_op jit(solution)/shard_map/all_to_all | solution.py:40
  20.4 4.3 %collective-permute-done.4.refs_5_ = bf16[160,512]{1,0:T(8,128)(2,1)S(1)} collective-permute-done((bf16[160,512]{1,0:T(8,128)(2,1)S(1)}, bf16[160,512]{1,0:T(8,128)(2,1)S(1)}, u32[]{:S(2)}, u32[]{:S(2)}) %collective-permute-start.4) | collective-permute-done | bytes 163872 | tf_op jit(solution)/shard_map/ppermute | solution.py:49
  24.7 2.7 %collective-permute-start.6 = (bf16[160,512]{1,0:T(8,128)(2,1)S(1)}, bf16[160,512]{1,0:T(8,128)(2,1)S(1)}, u32[]{:S(2)}, u32[]{:S(2)}) collective-permute-start(bf16[160,512]{1,0:T(8,128)(2,1)S(1)} %collective-permute-done.4.refs_5_), channel_id=1, source_target_pairs={{0,6},{1,7},{2,0},{3,1},{4,2},{5,3},{6,4},{7,5},{8,14},{9,15},{10,... | collective-permute-start | bytes 491528 | tf_op jit(solution)/shard_map/ppermute | solution.py:49
  27.4 3.2 %collective-permute-done.5.refs_6_ = bf16[160,512]{1,0:T(8,128)(2,1)S(1)} collective-permute-done((bf16[160,512]{1,0:T(8,128)(2,1)S(1)}, bf16[160,512]{1,0:T(8,128)(2,1)S(1)}, u32[]{:S(2)}, u32[]{:S(2)}) %collective-permute-start.5) | collective-permute-done | bytes 163872 | tf_op jit(solution)/shard_map/ppermute | solution.py:49
  31.4 4.6 %shard_map.115 = (bf16[8,8,48,512]{3,2,1,0:T(8,128)(2,1)}, bf16[8,32,512]{2,1,0:T(8,128)(2,1)}, f32[128,128]{1,0:T(8,128)}, f32[128,128]{1,0:T(8,128)}) custom-call(s32[2,128]{1,0:T(2,128)} %bitcast.42, bf16[128,384]{1,0:T(8,128)(2,1)} %get-tuple-element.38.one_n, bf16[128,384]{1,0:T(8,128)(2,1)} %get-tuple-element.39.two_n, ...), custom_call_target="tpu_custom_call" | custom-call | tf_op jit(solution)/shard_map/pallas_call | solution.py:205
  36.0 5.6 %all-to-all-start.1 = ((bf16[8,8,48,512]{3,2,1,0:T(8,128)(2,1)}), bf16[8,8,48,512]{3,2,1,0:T(8,128)(2,1)}, u32[]{:S(2)}, u32[]{:S(2)}) async-start(bf16[8,8,48,512]{3,2,1,0:T(8,128)(2,1)} %get-tuple-element.47), calls=%async_computation.1 | async-start | bytes 6291456 | tf_op jit(solution)/shard_map/all_to_all | solution.py:40
  41.7 3.4 %collective-permute-start.9 = (bf16[8,96,512]{2,1,0:T(8,128)(2,1)S(1)}, bf16[8,96,512]{2,1,0:T(8,128)(2,1)S(1)}, u32[]{:S(2)}, u32[]{:S(2)}) collective-permute-start(bf16[8,96,512]{2,1,0:T(8,128)(2,1)S(1)} %slice.9.refs_7_), channel_id=1, source_target_pairs={{0,6},{1,7},{2,0},{3,1},{4,2},{5,3},{6,4},{7,5},{8,14},{9,15},{10,... | collective-permute-start | bytes 2359304 | tf_op jit(solution)/shard_map/ppermute | solution.py:49
  46.4 15.5 %collective-permute-done.9.refs_11_ = bf16[8,96,512]{2,1,0:T(8,128)(2,1)S(1)} collective-permute-done((bf16[8,96,512]{2,1,0:T(8,128)(2,1)S(1)}, bf16[8,96,512]{2,1,0:T(8,128)(2,1)S(1)}, u32[]{:S(2)}, u32[]{:S(2)}) %collective-permute-start.9) | collective-permute-done | bytes 786464 | tf_op jit(solution)/shard_map/ppermute | solution.py:49
  61.9 3.2 %collective-permute-done.8.refs_9_ = bf16[8,96,512]{2,1,0:T(8,128)(2,1)S(1)} collective-permute-done((bf16[8,96,512]{2,1,0:T(8,128)(2,1)S(1)}, bf16[8,96,512]{2,1,0:T(8,128)(2,1)S(1)}, u32[]{:S(2)}, u32[]{:S(2)}) %collective-permute-start.8) | collective-permute-done | bytes 786464 | tf_op jit(solution)/shard_map/ppermute | solution.py:49
  67.3 15.7 %collective-permute-done.11.refs_12_ = bf16[8,96,512]{2,1,0:T(8,128)(2,1)S(1)} collective-permute-done((bf16[8,96,512]{2,1,0:T(8,128)(2,1)S(1)}, bf16[8,96,512]{2,1,0:T(8,128)(2,1)S(1)}, u32[]{:S(2)}, u32[]{:S(2)}) %collective-permute-start.11) | collective-permute-done | bytes 786464 | tf_op jit(solution)/shard_map/ppermute | solution.py:49
  83.0 1.8 collective-permute-done.10.refs_10_
  84.8 2.7 %collective-permute-start.13 = (bf16[8,96,512]{2,1,0:T(8,128)(2,1)S(1)}, bf16[8,96,512]{2,1,0:T(8,128)(2,1)S(1)}, u32[]{:S(2)}, u32[]{:S(2)}) collective-permute-start(bf16[8,96,512]{2,1,0:T(8,128)(2,1)S(1)} %collective-permute-done.11.refs_12_), channel_id=1, source_target_pairs={{0,6},{1,7},{2,0},{3,1},{4,2},{5,3},{6,4},{7,5},{8,14},{9,15},{10,... | collective-permute-start | bytes 2359304 | tf_op jit(solution)/shard_map/ppermute | solution.py:49
  87.5 17.5 %shard_map.116 = bf16[8,8,48,512]{3,2,1,0:T(8,128)(2,1)} custom-call(s32[8]{0:T(128)} %stack.35.order.refs_0_, bf16[8,8,48,512]{3,2,1,0:T(8,128)(2,1)} %all-to-all-done.1.moved, bf16[4096,896]{1,0:T(8,128)(2,1)} %bitcast.44, bf16[4096,896]{1,0:T(8,128)(2,1)} %bitcast.46, bf16[896,4096]{1,0:T(8,128)(2,1)} %bitcast.48), custom_call_target="tpu_custom_call" | custom-call | flops 8455716864 | bytes 28311552 | tf_op jit(solution)/shard_map/pallas_call | solution.py:375
  106.9 9.0 %all-to-all-start.2 = ((bf16[64,48,512]{2,1,0:T(8,128)(2,1)}), bf16[64,48,512]{2,1,0:T(8,128)(2,1)S(1)}, u32[]{:S(2)}, u32[]{:S(2)}) async-start(bf16[64,48,512]{2,1,0:T(8,128)(2,1)} %bitcast.37), calls=%async_computation.2 | async-start | bytes 6291456 | tf_op jit(solution)/shard_map/all_to_all | solution.py:40
  117.5 29.9 %shard_map.117 = bf16[8,8,48,512]{3,2,1,0:T(8,128)(2,1)} custom-call(s32[8]{0:T(128)} %stack.35.order.refs_0_, s32[1]{0:T(128)} %bitcast.17.refs_1_, bf16[8,96,128]{2,1,0:T(8,128)(2,1)} %slice.8.refs_2_, bf16[8,32,512]{2,1,0:T(8,128)(2,1)} %get-tuple-element.43.refs_3_, bf16[4096,896]{1,0:T(8,128)(2,1)} %bitcast.45, bf16[4096,896]{1,0:T(8,128)(2,1)} %bitcast.47, ...), custom_call_target="tpu_custom_call" | custom-call | flops 14092861440 | bytes 31457280 | tf_op jit(solution)/shard_map/pallas_call | solution.py:491
  147.4 8.6 %all-to-all-done.2 = bf16[64,48,512]{2,1,0:T(8,128)(2,1)S(1)} async-done(((bf16[64,48,512]{2,1,0:T(8,128)(2,1)}), bf16[64,48,512]{2,1,0:T(8,128)(2,1)S(1)}, u32[]{:S(2)}, u32[]{:S(2)}) %all-to-all-start.2) | async-done | bytes 3145760 | tf_op jit(solution)/shard_map/all_to_all | solution.py:40
  156.0 7.2 %all-to-all-start.3 = ((bf16[64,48,512]{2,1,0:T(8,128)(2,1)}), bf16[64,48,512]{2,1,0:T(8,128)(2,1)}, u32[]{:S(2)}, u32[]{:S(2)}) async-start(bf16[64,48,512]{2,1,0:T(8,128)(2,1)} %bitcast.36), calls=%async_computation.3 | async-start | bytes 6291456 | tf_op jit(solution)/shard_map/all_to_all | solution.py:40
  168.0 35.3 %all-to-all-done.3 = bf16[64,48,512]{2,1,0:T(8,128)(2,1)} async-done(((bf16[64,48,512]{2,1,0:T(8,128)(2,1)}), bf16[64,48,512]{2,1,0:T(8,128)(2,1)}, u32[]{:S(2)}, u32[]{:S(2)}) %all-to-all-start.3) | async-done | bytes 3145760 | tf_op jit(solution)/shard_map/all_to_all | solution.py:40
  204.2 2.6 %shard_map.118 = bf16[128,512]{1,0:T(8,128)(2,1)S(1)} custom-call(bf16[128,384]{1,0:T(8,128)(2,1)S(1)} %copy-done.4, bf16[8,8,48,512]{3,2,1,0:T(8,128)(2,1)} %bitcast.24.home, bf16[128,512]{1,0:T(8,128)(2,1)S(1)} %bitcast.35), custom_call_target="tpu_custom_call" | custom-call | tf_op jit(solution)/shard_map/pallas_call | solution.py:532
  207.5 2.6 %collective-permute-start.14 = (bf16[128,512]{1,0:T(8,128)(2,1)S(1)}, bf16[128,512]{1,0:T(8,128)(2,1)S(1)}, u32[]{:S(2)}, u32[]{:S(2)}) collective-permute-start(bf16[128,512]{1,0:T(8,128)(2,1)S(1)} %get-tuple-element.62), channel_id=1, source_target_pairs={{0,64},{64,0},{1,65},{65,1},{2,66},{66,2},{3,67},{67,3},{4,68},{68... | collective-permute-start | bytes 393224 | tf_op jit(solution)/shard_map/ppermute | solution.py:36
  210.1 4.1 %collective-permute-done.14 = bf16[128,512]{1,0:T(8,128)(2,1)S(1)} collective-permute-done((bf16[128,512]{1,0:T(8,128)(2,1)S(1)}, bf16[128,512]{1,0:T(8,128)(2,1)S(1)}, u32[]{:S(2)}, u32[]{:S(2)}) %collective-permute-start.14) | collective-permute-done | bytes 131104 | tf_op jit(solution)/shard_map/ppermute | solution.py:36
  (72 shorter events, 19.2 us)
Async XLA Ops:
  2.2 7.4 %collective-permute-start.2 = (bf16[160,512]{1,0:T(8,128)(2,1)}, bf16[160,512]{1,0:T(8,128)(2,1)S(1)}, u32[]{:S(2)}, u32[]{:S(2)}) collective-permute-start(bf16[160,512]{1,0:T(8,128)(2,1)} %shard_map.113.refs_0_), channel_id=1, source_target_pairs={{0,6},{1,7},{2,0},{3,1},{4,2},{5,3},{6,4},{7,5},{8,14},{9,15},{10,... | collective-permute-start | bytes 491528 | tf_op jit(solution)/shard_map/ppermute | solution.py:49
  5.6 6.2 %collective-permute-start.1 = (bf16[160,512]{1,0:T(8,128)(2,1)}, bf16[160,512]{1,0:T(8,128)(2,1)S(1)}, u32[]{:S(2)}, u32[]{:S(2)}) collective-permute-start(bf16[160,512]{1,0:T(8,128)(2,1)} %shard_map.113.refs_0_), channel_id=1, source_target_pairs={{0,2},{1,3},{2,4},{3,5},{4,6},{5,7},{6,0},{7,1},{8,10},{9,11},{10,... | collective-permute-start | bytes 491528 | tf_op jit(solution)/shard_map/ppermute | solution.py:49
  5.6 6.2 %collective-permute-start = (bf16[160,512]{1,0:T(8,128)(2,1)}, bf16[160,512]{1,0:T(8,128)(2,1)S(1)}, u32[]{:S(2)}, u32[]{:S(2)}) collective-permute-start(bf16[160,512]{1,0:T(8,128)(2,1)} %shard_map.113.refs_0_), channel_id=1, source_target_pairs={{0,1},{1,0},{2,3},{3,2},{4,5},{5,4},{6,7},{7,6},{8,9},{9,8},{10,11... | collective-permute-start | bytes 491528 | tf_op jit(solution)/shard_map/ppermute | solution.py:49
  9.7 21.0 %copy-start.9 = (bf16[160,512]{1,0:T(8,128)(2,1)}, bf16[160,512]{1,0:T(8,128)(2,1)S(1)}, u32[]{:S(2)}) copy-start(bf16[160,512]{1,0:T(8,128)(2,1)S(1)} %collective-permute-done.2.refs_4_) | copy-start | bytes 491524
  11.7 24.3 %all-to-all-start = ((bf16[8,96,640]{2,1,0:T(8,128)(2,1)}), bf16[8,96,640]{2,1,0:T(8,128)(2,1)S(1)}, u32[]{:S(2)}, u32[]{:S(2)}) async-start(bf16[8,96,640]{2,1,0:T(8,128)(2,1)} %get-tuple-element.37), calls=%async_computation | async-start | bytes 1966080 | tf_op jit(solution)/shard_map/all_to_all | solution.py:40
  18.9 5.8 %collective-permute-start.4 = (bf16[160,512]{1,0:T(8,128)(2,1)S(1)}, bf16[160,512]{1,0:T(8,128)(2,1)S(1)}, u32[]{:S(2)}, u32[]{:S(2)}) collective-permute-start(bf16[160,512]{1,0:T(8,128)(2,1)S(1)} %collective-permute-done.refs_1_), channel_id=1, source_target_pairs={{0,6},{1,7},{2,0},{3,1},{4,2},{5,3},{6,4},{7,5},{8,14},{9,15},{10,... | collective-permute-start | bytes 491528 | tf_op jit(solution)/shard_map/ppermute | solution.py:49
  20.4 10.2 %collective-permute-start.3 = (bf16[160,512]{1,0:T(8,128)(2,1)S(1)}, bf16[160,512]{1,0:T(8,128)(2,1)S(1)}, u32[]{:S(2)}, u32[]{:S(2)}) collective-permute-start(bf16[160,512]{1,0:T(8,128)(2,1)S(1)} %collective-permute-done.refs_1_), channel_id=1, source_target_pairs={{0,2},{1,3},{2,4},{3,5},{4,6},{5,7},{6,0},{7,1},{8,10},{9,11},{10,... | collective-permute-start | bytes 491528 | tf_op jit(solution)/shard_map/ppermute | solution.py:49
  20.4 10.2 %collective-permute-start.5 = (bf16[160,512]{1,0:T(8,128)(2,1)S(1)}, bf16[160,512]{1,0:T(8,128)(2,1)S(1)}, u32[]{:S(2)}, u32[]{:S(2)}) collective-permute-start(bf16[160,512]{1,0:T(8,128)(2,1)S(1)} %collective-permute-done.1.refs_2_), channel_id=1, source_target_pairs={{0,2},{1,3},{2,4},{3,5},{4,6},{5,7},{6,0},{7,1},{8,10},{9,11},{10,... | collective-permute-start | bytes 491528 | tf_op jit(solution)/shard_map/ppermute | solution.py:49
  24.7 5.9 %collective-permute-start.6 = (bf16[160,512]{1,0:T(8,128)(2,1)S(1)}, bf16[160,512]{1,0:T(8,128)(2,1)S(1)}, u32[]{:S(2)}, u32[]{:S(2)}) collective-permute-start(bf16[160,512]{1,0:T(8,128)(2,1)S(1)} %collective-permute-done.4.refs_5_), channel_id=1, source_target_pairs={{0,6},{1,7},{2,0},{3,1},{4,2},{5,3},{6,4},{7,5},{8,14},{9,15},{10,... | collective-permute-start | bytes 491528 | tf_op jit(solution)/shard_map/ppermute | solution.py:49
  36.0 48.8 %all-to-all-start.1 = ((bf16[8,8,48,512]{3,2,1,0:T(8,128)(2,1)}), bf16[8,8,48,512]{3,2,1,0:T(8,128)(2,1)}, u32[]{:S(2)}, u32[]{:S(2)}) async-start(bf16[8,8,48,512]{3,2,1,0:T(8,128)(2,1)} %get-tuple-element.47), calls=%async_computation.1 | async-start | bytes 6291456 | tf_op jit(solution)/shard_map/all_to_all | solution.py:40
  41.7 20.2 %collective-permute-start.9 = (bf16[8,96,512]{2,1,0:T(8,128)(2,1)S(1)}, bf16[8,96,512]{2,1,0:T(8,128)(2,1)S(1)}, u32[]{:S(2)}, u32[]{:S(2)}) collective-permute-start(bf16[8,96,512]{2,1,0:T(8,128)(2,1)S(1)} %slice.9.refs_7_), channel_id=1, source_target_pairs={{0,6},{1,7},{2,0},{3,1},{4,2},{5,3},{6,4},{7,5},{8,14},{9,15},{10,... | collective-permute-start | bytes 2359304 | tf_op jit(solution)/shard_map/ppermute | solution.py:49
  45.1 20.0 %collective-permute-start.8 = (bf16[8,96,512]{2,1,0:T(8,128)(2,1)S(1)}, bf16[8,96,512]{2,1,0:T(8,128)(2,1)S(1)}, u32[]{:S(2)}, u32[]{:S(2)}) collective-permute-start(bf16[8,96,512]{2,1,0:T(8,128)(2,1)S(1)} %slice.9.refs_7_), channel_id=1, source_target_pairs={{0,2},{1,3},{2,4},{3,5},{4,6},{5,7},{6,0},{7,1},{8,10},{9,11},{10,... | collective-permute-start | bytes 2359304 | tf_op jit(solution)/shard_map/ppermute | solution.py:49
  45.1 20.0 %collective-permute-start.7 = (bf16[8,96,512]{2,1,0:T(8,128)(2,1)S(1)}, bf16[8,96,512]{2,1,0:T(8,128)(2,1)S(1)}, u32[]{:S(2)}, u32[]{:S(2)}) collective-permute-start(bf16[8,96,512]{2,1,0:T(8,128)(2,1)S(1)} %slice.9.refs_7_), channel_id=1, source_target_pairs={{0,1},{1,0},{2,3},{3,2},{4,5},{5,4},{6,7},{7,6},{8,9},{9,8},{10,11... | collective-permute-start | bytes 2359304 | tf_op jit(solution)/shard_map/ppermute | solution.py:49
  65.1 40.0 %copy-start.17 = (bf16[8,96,512]{2,1,0:T(8,128)(2,1)}, bf16[8,96,512]{2,1,0:T(8,128)(2,1)S(1)}, u32[]{:S(2)}) copy-start(bf16[8,96,512]{2,1,0:T(8,128)(2,1)S(1)} %collective-permute-done.8.refs_9_) | copy-start | bytes 2359300
  65.1 40.0 %copy-start.18 = (bf16[8,96,512]{2,1,0:T(8,128)(2,1)}, bf16[8,96,512]{2,1,0:T(8,128)(2,1)S(1)}, u32[]{:S(2)}) copy-start(bf16[8,96,512]{2,1,0:T(8,128)(2,1)S(1)} %collective-permute-done.7.refs_8_) | copy-start | bytes 2359300
  65.1 17.9 %collective-permute-start.11 = (bf16[8,96,512]{2,1,0:T(8,128)(2,1)S(1)}, bf16[8,96,512]{2,1,0:T(8,128)(2,1)S(1)}, u32[]{:S(2)}, u32[]{:S(2)}) collective-permute-start(bf16[8,96,512]{2,1,0:T(8,128)(2,1)S(1)} %collective-permute-done.7.refs_8_), channel_id=1, source_target_pairs={{0,6},{1,7},{2,0},{3,1},{4,2},{5,3},{6,4},{7,5},{8,14},{9,15},{10,... | collective-permute-start | bytes 2359304 | tf_op jit(solution)/shard_map/ppermute | solution.py:49
  66.3 18.5 %collective-permute-start.10 = (bf16[8,96,512]{2,1,0:T(8,128)(2,1)S(1)}, bf16[8,96,512]{2,1,0:T(8,128)(2,1)S(1)}, u32[]{:S(2)}, u32[]{:S(2)}) collective-permute-start(bf16[8,96,512]{2,1,0:T(8,128)(2,1)S(1)} %collective-permute-done.7.refs_8_), channel_id=1, source_target_pairs={{0,2},{1,3},{2,4},{3,5},{4,6},{5,7},{6,0},{7,1},{8,10},{9,11},{10,... | collective-permute-start | bytes 2359304 | tf_op jit(solution)/shard_map/ppermute | solution.py:49
  83.0 22.0 %copy-start.19 = (bf16[8,96,512]{2,1,0:T(8,128)(2,1)}, bf16[8,96,512]{2,1,0:T(8,128)(2,1)S(1)}, u32[]{:S(2)}) copy-start(bf16[8,96,512]{2,1,0:T(8,128)(2,1)S(1)} %collective-permute-done.11.refs_12_) | copy-start | bytes 2359300
  84.8 20.3 %collective-permute-start.12 = (bf16[8,96,512]{2,1,0:T(8,128)(2,1)S(1)}, bf16[8,96,512]{2,1,0:T(8,128)(2,1)S(1)}, u32[]{:S(2)}, u32[]{:S(2)}) collective-permute-start(bf16[8,96,512]{2,1,0:T(8,128)(2,1)S(1)} %collective-permute-done.8.refs_9_), channel_id=1, source_target_pairs={{0,2},{1,3},{2,4},{3,5},{4,6},{5,7},{6,0},{7,1},{8,10},{9,11},{10,... | collective-permute-start | bytes 2359304 | tf_op jit(solution)/shard_map/ppermute | solution.py:49
  84.8 20.3 %collective-permute-start.13 = (bf16[8,96,512]{2,1,0:T(8,128)(2,1)S(1)}, bf16[8,96,512]{2,1,0:T(8,128)(2,1)S(1)}, u32[]{:S(2)}, u32[]{:S(2)}) collective-permute-start(bf16[8,96,512]{2,1,0:T(8,128)(2,1)S(1)} %collective-permute-done.11.refs_12_), channel_id=1, source_target_pairs={{0,6},{1,7},{2,0},{3,1},{4,2},{5,3},{6,4},{7,5},{8,14},{9,15},{10,... | collective-permute-start | bytes 2359304 | tf_op jit(solution)/shard_map/ppermute | solution.py:49
  106.9 49.1 %all-to-all-start.2 = ((bf16[64,48,512]{2,1,0:T(8,128)(2,1)}), bf16[64,48,512]{2,1,0:T(8,128)(2,1)S(1)}, u32[]{:S(2)}, u32[]{:S(2)}) async-start(bf16[64,48,512]{2,1,0:T(8,128)(2,1)} %bitcast.37), calls=%async_computation.2 | async-start | bytes 6291456 | tf_op jit(solution)/shard_map/all_to_all | solution.py:40
  156.0 47.3 %all-to-all-start.3 = ((bf16[64,48,512]{2,1,0:T(8,128)(2,1)}), bf16[64,48,512]{2,1,0:T(8,128)(2,1)}, u32[]{:S(2)}, u32[]{:S(2)}) async-start(bf16[64,48,512]{2,1,0:T(8,128)(2,1)} %bitcast.36), calls=%async_computation.3 | async-start | bytes 6291456 | tf_op jit(solution)/shard_map/all_to_all | solution.py:40
  163.2 40.1 %copy-start.1 = (bf16[1,128,512]{2,1,0:T(8,128)(2,1)S(1)}, bf16[1,128,512]{2,1,0:T(8,128)(2,1)}, u32[]{:S(2)}) copy-start(bf16[1,128,512]{2,1,0:T(8,128)(2,1)} %param.11) | copy-start | bytes 393220
  207.5 6.7 %collective-permute-start.14 = (bf16[128,512]{1,0:T(8,128)(2,1)S(1)}, bf16[128,512]{1,0:T(8,128)(2,1)S(1)}, u32[]{:S(2)}, u32[]{:S(2)}) collective-permute-start(bf16[128,512]{1,0:T(8,128)(2,1)S(1)} %get-tuple-element.62), channel_id=1, source_target_pairs={{0,64},{64,0},{1,65},{65,1},{2,66},{66,2},{3,67},{67,3},{4,68},{68... | collective-permute-start | bytes 393224 | tf_op jit(solution)/shard_map/ppermute | solution.py:36
  (18 other events, 91.8 us)

commit v8 on v7

--- a/solution.py
+++ b/solution.py
@@ -242,14 +242,14 @@
     return rows[0:1] + (rows[1:2] + rows[2:3])
 
 
-def fetch_rows(order, source, target, sems, part):
+def fetch_rows(order, source, target, sems, part, columns=slice(None)):
     copies = []
     for group in range(GROUPS):
         start = pl.multiple_of(order[group] * part, part)
         copies.append(
             pltpu.make_async_copy(
-                source.at[pl.ds(start, part), :],
-                target.at[pl.ds(group * part, part), :],
+                source.at[pl.ds(start, part), columns],
+                target.at[pl.ds(group * part, part), columns],
                 sems.at[group],
             )
         )
@@ -322,7 +322,7 @@
 
 def forward_kernel(
     order, moved, gate_w, up_w, down_w, out_to,
-    rows, out, gate_b, up_b, down_b, gate, up, hidden, sem_m, sem_o, sem_g, sem_u, sem_d
+    rows, out, gate_b, up_b, down_b, gate, up, hidden, sem_m, sem_o, sem_g, sem_h, sem_u, sem_d
 ):
     blocks, _, capacity, part = moved.shape
     total, width = blocks * capacity, GROUPS * part
@@ -332,16 +332,21 @@
         )
         for group in range(GROUPS)
     ]
-    copies = fetch_rows(order, gate_w, gate_b, sem_g, part)
+    near, rest = slice(0, part), slice(part, gate_w.shape[1])
+    copies = fetch_rows(order, gate_w, gate_b, sem_g, part, near)
+    copies_rest = fetch_rows(order, gate_w, gate_b, sem_h, part, rest)
     copies_up = fetch_rows(order, up_w, up_b, sem_u, part)
     copies_down = fetch_columns(None, down_w, down_b, sem_d, part)
     start(arrive)
     start(copies)
     wait(arrive)
+    start(copies_rest)
+    wait(copies)
     start(copies_up)
-    wait(copies)
+    gate[:, near] = product(rows[...].reshape(total, width), gate_b[:, near], INNER)
+    wait(copies_rest)
+    gate[:, rest] = product(rows[...].reshape(total, width), gate_b[:, rest], INNER)
     start(copies_down)
-    gate[...] = product(rows[...].reshape(total, width), gate_b[...], INNER)
     wait(copies_up)
     up[...] = product(rows[...].reshape(total, width), up_b[...], INNER)
 
@@ -387,7 +392,7 @@
             pltpu.VMEM((total, units), jnp.float32),
             pltpu.VMEM((total, units), jnp.bfloat16),
         ]
-        + [pltpu.SemaphoreType.DMA((GROUPS,))] * 5,
+        + [pltpu.SemaphoreType.DMA((GROUPS,))] * 6,
         compiler_params=pltpu.CompilerParams(vmem_limit_bytes=LIMIT),
         cost_estimate=pl.CostEstimate(
             flops=6 * total * width * units,

time: 216 us -> 215 us (level)
  no operation moved by 1% of the time
where the time goes in v8:
time: 215 us; the launch traced here: 214 us
  waiting for transfers between devices  93.8 us (44%)
  Pallas kernels  59.6 us (28%)
  starting transfers between devices  49.2 us (23%)
  local copies, waits for them, and re-layouts  9.95 us (5%)
    ppermute x14, waiting for transfers between devices, shift(): return lax.ppermute(block, 'hid', route)  45.8 us
    all_to_all x4, waiting for transfers between devices, swap(): return lax.all_to_all(block, axes, split_axis=0, concat_axis=0, tiled=True)  43.9 us
    pallas_call x1, Pallas kernels, backward(): pl.pallas_call(backward_kernel, out_shape=jax.ShapeDtypeStruct((blocks, G...  29.9 us
    all_to_all x4, starting transfers between devices, swap(): return lax.all_to_all(block, axes, split_axis=0, concat_axis=0, tiled=True)  28.9 us
    ppermute x14, starting transfers between devices, shift(): return lax.ppermute(block, 'hid', route)  17.7 us
    pallas_call x1, Pallas kernels, forward(): pl.pallas_call(forward_kernel, out_shape=jax.ShapeDtypeStruct(moved.shape...  16.9 us
    unnamed x47, local copies, waits for them, and re-layouts  7.62 us
    pallas_call x1, Pallas kernels, spread(): pl.pallas_call(spread_kernel, out_shape=(jax.ShapeDtypeStruct((blocks, GR...  4.62 us
  transfers between devices with their start and end apart: 19, of which 10 were waited for; matrix products, arithmetic and copies ran while one was open for 1% of the time, Pallas kernels for 26%

profile of v8, /device:TPU:1, one launch (start us, length us, event | category | flops | bytes accessed | tf_op | source)
XLA Modules:
  0.0 214.2 jit_solution(17594069893754089283)
XLA Ops:
  2.2 3.3 %collective-permute-start.2 = (bf16[160,512]{1,0:T(8,128)(2,1)}, bf16[160,512]{1,0:T(8,128)(2,1)S(1)}, u32[]{:S(2)}, u32[]{:S(2)}) collective-permute-start(bf16[160,512]{1,0:T(8,128)(2,1)} %shard_map.113.refs_0_), channel_id=1, source_target_pairs={{0,6},{1,7},{2,0},{3,1},{4,2},{5,3},{6,4},{7,5},{8,14},{9,15},{10,... | collective-permute-start | bytes 491528 | tf_op jit(solution)/shard_map/ppermute | solution.py:49
  6.9 2.8 %shard_map.114 = (bf16[8,96,640]{2,1,0:T(8,128)(2,1)}, bf16[128,384]{1,0:T(8,128)(2,1)}, bf16[128,384]{1,0:T(8,128)(2,1)}, bf16[128,384]{1,0:T(8,128)(2,1)}) custom-call(s32[2,128]{1,0:T(2,128)} %bitcast.43, s32[2,128]{1,0:T(2,128)} %bitcast.41, bf16[128,512]{1,0:T(8,128)(2,1)} %bitcast.38, bf16[128,512]{1,0:T(8,128)(2,1)} %bitcast.34), custom_call_target="tpu_custom_call" | custom-call | tf_op jit(solution)/shard_map/pallas_call | solution.py:165
  9.7 2.1 collective-permute-done.1.refs_2_
  11.7 7.2 %all-to-all-start = ((bf16[8,96,640]{2,1,0:T(8,128)(2,1)}), bf16[8,96,640]{2,1,0:T(8,128)(2,1)S(1)}, u32[]{:S(2)}, u32[]{:S(2)}) async-start(bf16[8,96,640]{2,1,0:T(8,128)(2,1)} %get-tuple-element.37), calls=%async_computation | async-start | bytes 1966080 | tf_op jit(solution)/shard_map/all_to_all | solution.py:40
  20.4 4.3 %collective-permute-done.4.refs_5_ = bf16[160,512]{1,0:T(8,128)(2,1)S(1)} collective-permute-done((bf16[160,512]{1,0:T(8,128)(2,1)S(1)}, bf16[160,512]{1,0:T(8,128)(2,1)S(1)}, u32[]{:S(2)}, u32[]{:S(2)}) %collective-permute-start.4) | collective-permute-done | bytes 163872 | tf_op jit(solution)/shard_map/ppermute | solution.py:49
  24.7 2.7 %collective-permute-start.6 = (bf16[160,512]{1,0:T(8,128)(2,1)S(1)}, bf16[160,512]{1,0:T(8,128)(2,1)S(1)}, u32[]{:S(2)}, u32[]{:S(2)}) collective-permute-start(bf16[160,512]{1,0:T(8,128)(2,1)S(1)} %collective-permute-done.4.refs_5_), channel_id=1, source_target_pairs={{0,6},{1,7},{2,0},{3,1},{4,2},{5,3},{6,4},{7,5},{8,14},{9,15},{10,... | collective-permute-start | bytes 491528 | tf_op jit(solution)/shard_map/ppermute | solution.py:49
  27.4 3.2 %collective-permute-done.5.refs_6_ = bf16[160,512]{1,0:T(8,128)(2,1)S(1)} collective-permute-done((bf16[160,512]{1,0:T(8,128)(2,1)S(1)}, bf16[160,512]{1,0:T(8,128)(2,1)S(1)}, u32[]{:S(2)}, u32[]{:S(2)}) %collective-permute-start.5) | collective-permute-done | bytes 163872 | tf_op jit(solution)/shard_map/ppermute | solution.py:49
  31.4 4.6 %shard_map.115 = (bf16[8,8,48,512]{3,2,1,0:T(8,128)(2,1)}, bf16[8,32,512]{2,1,0:T(8,128)(2,1)}, f32[128,128]{1,0:T(8,128)}, f32[128,128]{1,0:T(8,128)}) custom-call(s32[2,128]{1,0:T(2,128)} %bitcast.42, bf16[128,384]{1,0:T(8,128)(2,1)} %get-tuple-element.38.one_n, bf16[128,384]{1,0:T(8,128)(2,1)} %get-tuple-element.39.two_n, ...), custom_call_target="tpu_custom_call" | custom-call | tf_op jit(solution)/shard_map/pallas_call | solution.py:205
  36.0 5.6 %all-to-all-start.1 = ((bf16[8,8,48,512]{3,2,1,0:T(8,128)(2,1)}), bf16[8,8,48,512]{3,2,1,0:T(8,128)(2,1)}, u32[]{:S(2)}, u32[]{:S(2)}) async-start(bf16[8,8,48,512]{3,2,1,0:T(8,128)(2,1)} %get-tuple-element.47), calls=%async_computation.1 | async-start | bytes 6291456 | tf_op jit(solution)/shard_map/all_to_all | solution.py:40
  41.7 3.4 %collective-permute-start.9 = (bf16[8,96,512]{2,1,0:T(8,128)(2,1)S(1)}, bf16[8,96,512]{2,1,0:T(8,128)(2,1)S(1)}, u32[]{:S(2)}, u32[]{:S(2)}) collective-permute-start(bf16[8,96,512]{2,1,0:T(8,128)(2,1)S(1)} %slice.9.refs_7_), channel_id=1, source_target_pairs={{0,6},{1,7},{2,0},{3,1},{4,2},{5,3},{6,4},{7,5},{8,14},{9,15},{10,... | collective-permute-start | bytes 2359304 | tf_op jit(solution)/shard_map/ppermute | solution.py:49
  46.4 15.5 %collective-permute-done.9.refs_11_ = bf16[8,96,512]{2,1,0:T(8,128)(2,1)S(1)} collective-permute-done((bf16[8,96,512]{2,1,0:T(8,128)(2,1)S(1)}, bf16[8,96,512]{2,1,0:T(8,128)(2,1)S(1)}, u32[]{:S(2)}, u32[]{:S(2)}) %collective-permute-start.9) | collective-permute-done | bytes 786464 | tf_op jit(solution)/shard_map/ppermute | solution.py:49
  61.9 3.2 %collective-permute-done.8.refs_9_ = bf16[8,96,512]{2,1,0:T(8,128)(2,1)S(1)} collective-permute-done((bf16[8,96,512]{2,1,0:T(8,128)(2,1)S(1)}, bf16[8,96,512]{2,1,0:T(8,128)(2,1)S(1)}, u32[]{:S(2)}, u32[]{:S(2)}) %collective-permute-start.8) | collective-permute-done | bytes 786464 | tf_op jit(solution)/shard_map/ppermute | solution.py:49
  67.3 15.7 %collective-permute-done.11.refs_12_ = bf16[8,96,512]{2,1,0:T(8,128)(2,1)S(1)} collective-permute-done((bf16[8,96,512]{2,1,0:T(8,128)(2,1)S(1)}, bf16[8,96,512]{2,1,0:T(8,128)(2,1)S(1)}, u32[]{:S(2)}, u32[]{:S(2)}) %collective-permute-start.11) | collective-permute-done | bytes 786464 | tf_op jit(solution)/shard_map/ppermute | solution.py:49
  83.0 1.8 collective-permute-done.10.refs_10_
  84.8 2.7 %collective-permute-start.13 = (bf16[8,96,512]{2,1,0:T(8,128)(2,1)S(1)}, bf16[8,96,512]{2,1,0:T(8,128)(2,1)S(1)}, u32[]{:S(2)}, u32[]{:S(2)}) collective-permute-start(bf16[8,96,512]{2,1,0:T(8,128)(2,1)S(1)} %collective-permute-done.11.refs_12_), channel_id=1, source_target_pairs={{0,6},{1,7},{2,0},{3,1},{4,2},{5,3},{6,4},{7,5},{8,14},{9,15},{10,... | collective-permute-start | bytes 2359304 | tf_op jit(solution)/shard_map/ppermute | solution.py:49
  87.5 16.9 %shard_map.116 = bf16[8,8,48,512]{3,2,1,0:T(8,128)(2,1)} custom-call(s32[8]{0:T(128)} %stack.35.order.refs_0_, bf16[8,8,48,512]{3,2,1,0:T(8,128)(2,1)} %all-to-all-done.1.moved, bf16[4096,896]{1,0:T(8,128)(2,1)} %bitcast.44, bf16[4096,896]{1,0:T(8,128)(2,1)} %bitcast.46, bf16[896,4096]{1,0:T(8,128)(2,1)} %bitcast.48), custom_call_target="tpu_custom_call" | custom-call | flops 8455716864 | bytes 28311552 | tf_op jit(solution)/shard_map/pallas_call | solution.py:380
  106.2 9.0 %all-to-all-start.2 = ((bf16[64,48,512]{2,1,0:T(8,128)(2,1)}), bf16[64,48,512]{2,1,0:T(8,128)(2,1)S(1)}, u32[]{:S(2)}, u32[]{:S(2)}) async-start(bf16[64,48,512]{2,1,0:T(8,128)(2,1)} %bitcast.37), calls=%async_computation.2 | async-start | bytes 6291456 | tf_op jit(solution)/shard_map/all_to_all | solution.py:40
  116.8 29.9 %shard_map.117 = bf16[8,8,48,512]{3,2,1,0:T(8,128)(2,1)} custom-call(s32[8]{0:T(128)} %stack.35.order.refs_0_, s32[1]{0:T(128)} %bitcast.17.refs_1_, bf16[8,96,128]{2,1,0:T(8,128)(2,1)} %slice.8.refs_2_, bf16[8,32,512]{2,1,0:T(8,128)(2,1)} %get-tuple-element.43.refs_3_, bf16[4096,896]{1,0:T(8,128)(2,1)} %bitcast.45, bf16[4096,896]{1,0:T(8,128)(2,1)} %bitcast.47, ...), custom_call_target="tpu_custom_call" | custom-call | flops 14092861440 | bytes 31457280 | tf_op jit(solution)/shard_map/pallas_call | solution.py:496
  146.7 8.6 %all-to-all-done.2 = bf16[64,48,512]{2,1,0:T(8,128)(2,1)S(1)} async-done(((bf16[64,48,512]{2,1,0:T(8,128)(2,1)}), bf16[64,48,512]{2,1,0:T(8,128)(2,1)S(1)}, u32[]{:S(2)}, u32[]{:S(2)}) %all-to-all-start.2) | async-done | bytes 3145760 | tf_op jit(solution)/shard_map/all_to_all | solution.py:40
  155.3 7.2 %all-to-all-start.3 = ((bf16[64,48,512]{2,1,0:T(8,128)(2,1)}), bf16[64,48,512]{2,1,0:T(8,128)(2,1)}, u32[]{:S(2)}, u32[]{:S(2)}) async-start(bf16[64,48,512]{2,1,0:T(8,128)(2,1)} %bitcast.36), calls=%async_computation.3 | async-start | bytes 6291456 | tf_op jit(solution)/shard_map/all_to_all | solution.py:40
  167.3 35.3 %all-to-all-done.3 = bf16[64,48,512]{2,1,0:T(8,128)(2,1)} async-done(((bf16[64,48,512]{2,1,0:T(8,128)(2,1)}), bf16[64,48,512]{2,1,0:T(8,128)(2,1)}, u32[]{:S(2)}, u32[]{:S(2)}) %all-to-all-start.3) | async-done | bytes 3145760 | tf_op jit(solution)/shard_map/all_to_all | solution.py:40
  203.5 2.6 %shard_map.118 = bf16[128,512]{1,0:T(8,128)(2,1)S(1)} custom-call(bf16[128,384]{1,0:T(8,128)(2,1)S(1)} %copy-done.4, bf16[8,8,48,512]{3,2,1,0:T(8,128)(2,1)} %bitcast.24.home, bf16[128,512]{1,0:T(8,128)(2,1)S(1)} %bitcast.35), custom_call_target="tpu_custom_call" | custom-call | tf_op jit(solution)/shard_map/pallas_call | solution.py:537
  206.8 2.6 %collective-permute-start.14 = (bf16[128,512]{1,0:T(8,128)(2,1)S(1)}, bf16[128,512]{1,0:T(8,128)(2,1)S(1)}, u32[]{:S(2)}, u32[]{:S(2)}) collective-permute-start(bf16[128,512]{1,0:T(8,128)(2,1)S(1)} %get-tuple-element.62), channel_id=1, source_target_pairs={{0,64},{64,0},{1,65},{65,1},{2,66},{66,2},{3,67},{67,3},{4,68},{68... | collective-permute-start | bytes 393224 | tf_op jit(solution)/shard_map/ppermute | solution.py:36
  209.4 4.1 %collective-permute-done.14 = bf16[128,512]{1,0:T(8,128)(2,1)S(1)} collective-permute-done((bf16[128,512]{1,0:T(8,128)(2,1)S(1)}, bf16[128,512]{1,0:T(8,128)(2,1)S(1)}, u32[]{:S(2)}, u32[]{:S(2)}) %collective-permute-start.14) | collective-permute-done | bytes 131104 | tf_op jit(solution)/shard_map/ppermute | solution.py:36
  (72 shorter events, 19.2 us)
Async XLA Ops:
  2.2 7.4 %collective-permute-start.2 = (bf16[160,512]{1,0:T(8,128)(2,1)}, bf16[160,512]{1,0:T(8,128)(2,1)S(1)}, u32[]{:S(2)}, u32[]{:S(2)}) collective-permute-start(bf16[160,512]{1,0:T(8,128)(2,1)} %shard_map.113.refs_0_), channel_id=1, source_target_pairs={{0,6},{1,7},{2,0},{3,1},{4,2},{5,3},{6,4},{7,5},{8,14},{9,15},{10,... | collective-permute-start | bytes 491528 | tf_op jit(solution)/shard_map/ppermute | solution.py:49
  5.6 6.2 %collective-permute-start.1 = (bf16[160,512]{1,0:T(8,128)(2,1)}, bf16[160,512]{1,0:T(8,128)(2,1)S(1)}, u32[]{:S(2)}, u32[]{:S(2)}) collective-permute-start(bf16[160,512]{1,0:T(8,128)(2,1)} %shard_map.113.refs_0_), channel_id=1, source_target_pairs={{0,2},{1,3},{2,4},{3,5},{4,6},{5,7},{6,0},{7,1},{8,10},{9,11},{10,... | collective-permute-start | bytes 491528 | tf_op jit(solution)/shard_map/ppermute | solution.py:49
  5.6 6.2 %collective-permute-start = (bf16[160,512]{1,0:T(8,128)(2,1)}, bf16[160,512]{1,0:T(8,128)(2,1)S(1)}, u32[]{:S(2)}, u32[]{:S(2)}) collective-permute-start(bf16[160,512]{1,0:T(8,128)(2,1)} %shard_map.113.refs_0_), channel_id=1, source_target_pairs={{0,1},{1,0},{2,3},{3,2},{4,5},{5,4},{6,7},{7,6},{8,9},{9,8},{10,11... | collective-permute-start | bytes 491528 | tf_op jit(solution)/shard_map/ppermute | solution.py:49
  9.7 21.0 %copy-start.9 = (bf16[160,512]{1,0:T(8,128)(2,1)}, bf16[160,512]{1,0:T(8,128)(2,1)S(1)}, u32[]{:S(2)}) copy-start(bf16[160,512]{1,0:T(8,128)(2,1)S(1)} %collective-permute-done.2.refs_4_) | copy-start | bytes 491524
  11.7 24.3 %all-to-all-start = ((bf16[8,96,640]{2,1,0:T(8,128)(2,1)}), bf16[8,96,640]{2,1,0:T(8,128)(2,1)S(1)}, u32[]{:S(2)}, u32[]{:S(2)}) async-start(bf16[8,96,640]{2,1,0:T(8,128)(2,1)} %get-tuple-element.37), calls=%async_computation | async-start | bytes 1966080 | tf_op jit(solution)/shard_map/all_to_all | solution.py:40
  18.9 5.8 %collective-permute-start.4 = (bf16[160,512]{1,0:T(8,128)(2,1)S(1)}, bf16[160,512]{1,0:T(8,128)(2,1)S(1)}, u32[]{:S(2)}, u32[]{:S(2)}) collective-permute-start(bf16[160,512]{1,0:T(8,128)(2,1)S(1)} %collective-permute-done.refs_1_), channel_id=1, source_target_pairs={{0,6},{1,7},{2,0},{3,1},{4,2},{5,3},{6,4},{7,5},{8,14},{9,15},{10,... | collective-permute-start | bytes 491528 | tf_op jit(solution)/shard_map/ppermute | solution.py:49
  20.4 10.2 %collective-permute-start.3 = (bf16[160,512]{1,0:T(8,128)(2,1)S(1)}, bf16[160,512]{1,0:T(8,128)(2,1)S(1)}, u32[]{:S(2)}, u32[]{:S(2)}) collective-permute-start(bf16[160,512]{1,0:T(8,128)(2,1)S(1)} %collective-permute-done.refs_1_), channel_id=1, source_target_pairs={{0,2},{1,3},{2,4},{3,5},{4,6},{5,7},{6,0},{7,1},{8,10},{9,11},{10,... | collective-permute-start | bytes 491528 | tf_op jit(solution)/shard_map/ppermute | solution.py:49
  20.4 10.2 %collective-permute-start.5 = (bf16[160,512]{1,0:T(8,128)(2,1)S(1)}, bf16[160,512]{1,0:T(8,128)(2,1)S(1)}, u32[]{:S(2)}, u32[]{:S(2)}) collective-permute-start(bf16[160,512]{1,0:T(8,128)(2,1)S(1)} %collective-permute-done.1.refs_2_), channel_id=1, source_target_pairs={{0,2},{1,3},{2,4},{3,5},{4,6},{5,7},{6,0},{7,1},{8,10},{9,11},{10,... | collective-permute-start | bytes 491528 | tf_op jit(solution)/shard_map/ppermute | solution.py:49
  24.7 5.9 %collective-permute-start.6 = (bf16[160,512]{1,0:T(8,128)(2,1)S(1)}, bf16[160,512]{1,0:T(8,128)(2,1)S(1)}, u32[]{:S(2)}, u32[]{:S(2)}) collective-permute-start(bf16[160,512]{1,0:T(8,128)(2,1)S(1)} %collective-permute-done.4.refs_5_), channel_id=1, source_target_pairs={{0,6},{1,7},{2,0},{3,1},{4,2},{5,3},{6,4},{7,5},{8,14},{9,15},{10,... | collective-permute-start | bytes 491528 | tf_op jit(solution)/shard_map/ppermute | solution.py:49
  36.0 48.8 %all-to-all-start.1 = ((bf16[8,8,48,512]{3,2,1,0:T(8,128)(2,1)}), bf16[8,8,48,512]{3,2,1,0:T(8,128)(2,1)}, u32[]{:S(2)}, u32[]{:S(2)}) async-start(bf16[8,8,48,512]{3,2,1,0:T(8,128)(2,1)} %get-tuple-element.47), calls=%async_computation.1 | async-start | bytes 6291456 | tf_op jit(solution)/shard_map/all_to_all | solution.py:40
  41.7 20.2 %collective-permute-start.9 = (bf16[8,96,512]{2,1,0:T(8,128)(2,1)S(1)}, bf16[8,96,512]{2,1,0:T(8,128)(2,1)S(1)}, u32[]{:S(2)}, u32[]{:S(2)}) collective-permute-start(bf16[8,96,512]{2,1,0:T(8,128)(2,1)S(1)} %slice.9.refs_7_), channel_id=1, source_target_pairs={{0,6},{1,7},{2,0},{3,1},{4,2},{5,3},{6,4},{7,5},{8,14},{9,15},{10,... | collective-permute-start | bytes 2359304 | tf_op jit(solution)/shard_map/ppermute | solution.py:49
  45.1 20.0 %collective-permute-start.8 = (bf16[8,96,512]{2,1,0:T(8,128)(2,1)S(1)}, bf16[8,96,512]{2,1,0:T(8,128)(2,1)S(1)}, u32[]{:S(2)}, u32[]{:S(2)}) collective-permute-start(bf16[8,96,512]{2,1,0:T(8,128)(2,1)S(1)} %slice.9.refs_7_), channel_id=1, source_target_pairs={{0,2},{1,3},{2,4},{3,5},{4,6},{5,7},{6,0},{7,1},{8,10},{9,11},{10,... | collective-permute-start | bytes 2359304 | tf_op jit(solution)/shard_map/ppermute | solution.py:49
  45.1 20.0 %collective-permute-start.7 = (bf16[8,96,512]{2,1,0:T(8,128)(2,1)S(1)}, bf16[8,96,512]{2,1,0:T(8,128)(2,1)S(1)}, u32[]{:S(2)}, u32[]{:S(2)}) collective-permute-start(bf16[8,96,512]{2,1,0:T(8,128)(2,1)S(1)} %slice.9.refs_7_), channel_id=1, source_target_pairs={{0,1},{1,0},{2,3},{3,2},{4,5},{5,4},{6,7},{7,6},{8,9},{9,8},{10,11... | collective-permute-start | bytes 2359304 | tf_op jit(solution)/shard_map/ppermute | solution.py:49
  65.1 39.3 %copy-start.17 = (bf16[8,96,512]{2,1,0:T(8,128)(2,1)}, bf16[8,96,512]{2,1,0:T(8,128)(2,1)S(1)}, u32[]{:S(2)}) copy-start(bf16[8,96,512]{2,1,0:T(8,128)(2,1)S(1)} %collective-permute-done.8.refs_9_) | copy-start | bytes 2359300
  65.1 39.3 %copy-start.18 = (bf16[8,96,512]{2,1,0:T(8,128)(2,1)}, bf16[8,96,512]{2,1,0:T(8,128)(2,1)S(1)}, u32[]{:S(2)}) copy-start(bf16[8,96,512]{2,1,0:T(8,128)(2,1)S(1)} %collective-permute-done.7.refs_8_) | copy-start | bytes 2359300
  65.1 17.9 %collective-permute-start.11 = (bf16[8,96,512]{2,1,0:T(8,128)(2,1)S(1)}, bf16[8,96,512]{2,1,0:T(8,128)(2,1)S(1)}, u32[]{:S(2)}, u32[]{:S(2)}) collective-permute-start(bf16[8,96,512]{2,1,0:T(8,128)(2,1)S(1)} %collective-permute-done.7.refs_8_), channel_id=1, source_target_pairs={{0,6},{1,7},{2,0},{3,1},{4,2},{5,3},{6,4},{7,5},{8,14},{9,15},{10,... | collective-permute-start | bytes 2359304 | tf_op jit(solution)/shard_map/ppermute | solution.py:49
  66.3 18.5 %collective-permute-start.10 = (bf16[8,96,512]{2,1,0:T(8,128)(2,1)S(1)}, bf16[8,96,512]{2,1,0:T(8,128)(2,1)S(1)}, u32[]{:S(2)}, u32[]{:S(2)}) collective-permute-start(bf16[8,96,512]{2,1,0:T(8,128)(2,1)S(1)} %collective-permute-done.7.refs_8_), channel_id=1, source_target_pairs={{0,2},{1,3},{2,4},{3,5},{4,6},{5,7},{6,0},{7,1},{8,10},{9,11},{10,... | collective-permute-start | bytes 2359304 | tf_op jit(solution)/shard_map/ppermute | solution.py:49
  83.0 21.4 %copy-start.19 = (bf16[8,96,512]{2,1,0:T(8,128)(2,1)}, bf16[8,96,512]{2,1,0:T(8,128)(2,1)S(1)}, u32[]{:S(2)}) copy-start(bf16[8,96,512]{2,1,0:T(8,128)(2,1)S(1)} %collective-permute-done.11.refs_12_) | copy-start | bytes 2359300
  84.8 19.6 %collective-permute-start.12 = (bf16[8,96,512]{2,1,0:T(8,128)(2,1)S(1)}, bf16[8,96,512]{2,1,0:T(8,128)(2,1)S(1)}, u32[]{:S(2)}, u32[]{:S(2)}) collective-permute-start(bf16[8,96,512]{2,1,0:T(8,128)(2,1)S(1)} %collective-permute-done.8.refs_9_), channel_id=1, source_target_pairs={{0,2},{1,3},{2,4},{3,5},{4,6},{5,7},{6,0},{7,1},{8,10},{9,11},{10,... | collective-permute-start | bytes 2359304 | tf_op jit(solution)/shard_map/ppermute | solution.py:49
  84.8 19.6 %collective-permute-start.13 = (bf16[8,96,512]{2,1,0:T(8,128)(2,1)S(1)}, bf16[8,96,512]{2,1,0:T(8,128)(2,1)S(1)}, u32[]{:S(2)}, u32[]{:S(2)}) collective-permute-start(bf16[8,96,512]{2,1,0:T(8,128)(2,1)S(1)} %collective-permute-done.11.refs_12_), channel_id=1, source_target_pairs={{0,6},{1,7},{2,0},{3,1},{4,2},{5,3},{6,4},{7,5},{8,14},{9,15},{10,... | collective-permute-start | bytes 2359304 | tf_op jit(solution)/shard_map/ppermute | solution.py:49
  106.2 49.1 %all-to-all-start.2 = ((bf16[64,48,512]{2,1,0:T(8,128)(2,1)}), bf16[64,48,512]{2,1,0:T(8,128)(2,1)S(1)}, u32[]{:S(2)}, u32[]{:S(2)}) async-start(bf16[64,48,512]{2,1,0:T(8,128)(2,1)} %bitcast.37), calls=%async_computation.2 | async-start | bytes 6291456 | tf_op jit(solution)/shard_map/all_to_all | solution.py:40
  155.3 47.3 %all-to-all-start.3 = ((bf16[64,48,512]{2,1,0:T(8,128)(2,1)}), bf16[64,48,512]{2,1,0:T(8,128)(2,1)}, u32[]{:S(2)}, u32[]{:S(2)}) async-start(bf16[64,48,512]{2,1,0:T(8,128)(2,1)} %bitcast.36), calls=%async_computation.3 | async-start | bytes 6291456 | tf_op jit(solution)/shard_map/all_to_all | solution.py:40
  162.5 40.1 %copy-start.1 = (bf16[1,128,512]{2,1,0:T(8,128)(2,1)S(1)}, bf16[1,128,512]{2,1,0:T(8,128)(2,1)}, u32[]{:S(2)}) copy-start(bf16[1,128,512]{2,1,0:T(8,128)(2,1)} %param.11) | copy-start | bytes 393220
  206.8 6.7 %collective-permute-start.14 = (bf16[128,512]{1,0:T(8,128)(2,1)S(1)}, bf16[128,512]{1,0:T(8,128)(2,1)S(1)}, u32[]{:S(2)}, u32[]{:S(2)}) collective-permute-start(bf16[128,512]{1,0:T(8,128)(2,1)S(1)} %get-tuple-element.62), channel_id=1, source_target_pairs={{0,64},{64,0},{1,65},{65,1},{2,66},{66,2},{3,67},{67,3},{4,68},{68... | collective-permute-start | bytes 393224 | tf_op jit(solution)/shard_map/ppermute | solution.py:36
  (18 other events, 91.2 us)
